TPU v7x, 32 devices: a whole 2x2x4 slice. The times are simulated.
32 devices in a mesh: dp: 2 (over x), expert: 16 (over z, y, core).
Axes of the slice: x: 2, y: 2, z: 4, core: 2. Of those that a mesh axis runs over, the one named last changes fastest.
Arguments:
- tokens: bfloat16 [4096, 1024], P(('dp', 'expert')), may hold values from -6 to 6
- routes: int32 [4096, 4], P(('dp', 'expert')), may hold values from 0 to 15, all different within a row; in each aligned block of 128 rows (0 to 127, 128 to 255, ...) at most 40 rows name the same one
- gates: float32 [4096, 4], P(('dp', 'expert')), may hold values from 0.05 to 0.5
- gate_weight: bfloat16 [16, 1024, 384], P('expert', 'dp'), may hold values from -0.1875 to 0.1875
- up_weight: bfloat16 [16, 1024, 384], P('expert', 'dp'), may hold values from -0.1875 to 0.1875
- down_weight: bfloat16 [16, 1024, 384], P('expert', 'dp'), may hold values from -0.3125 to 0.3125
- cotangent: bfloat16 [4096, 1024], P(('dp', 'expert')), may hold values from -1.1953125 to 1.1953125
Outputs:
- mixed: bfloat16 [4096, 1024], P(('dp', 'expert'))
- token_grads: bfloat16 [4096, 1024], P(('dp', 'expert'))
- gate_grads: float32 [4096, 4], P(('dp', 'expert'))
- gate_weight_grad: float32 [16, 1024, 384], P('expert', 'dp')
- up_weight_grad: float32 [16, 1024, 384], P('expert', 'dp')
- down_weight_grad: float32 [16, 1024, 384], P('expert', 'dp')
Inputs may be any that keep to these rules, and one draw needn't show every extreme that they name: `routes`: each row names 4 different experts. In each aligned block of 128 rows (the tokens of one device) no expert is named by more than 40 rows, and in some blocks one expert is named by exactly 40 rows.
All inputs are finite; a program needn't handle non-finite values.
Results may differ from a plain program's by a relative error of at most 0.0065.
Values may be sent and summed in bfloat16 or wider, within the bound.
No kernel may reach another device: no remote copies, remote signals or barrier semaphores. Data moves between devices by JAX's collectives and lax.ppermute only.
A program may use at most 64 MiB of HBM per device.

v0:
```python
import jax
import jax.numpy as jnp
from jax import lax
from jax.sharding import PartitionSpec as P


def to_items(values, item_count, owners):
    return values.reshape(owners, item_count, values.shape[-1])


def contract_rows(left, right):
    return lax.dot_general(
        left, right, (((0,), (0,)), ((), ())), preferred_element_type=jnp.float32
    )


def contract_last(left, right):
    return lax.dot_general(
        left, right, (((1,), (1,)), ((), ())), preferred_element_type=jnp.float32
    )


def on_device(tokens, routes, gates, gate_weight, up_weight, down_weight, cotangent):
    owners = lax.axis_size("expert")
    tok_rows, feat_width = tokens.shape
    top_count = routes.shape[1]
    pair_count = tok_rows * top_count
    capacity = max(2, pair_count * 5 // (4 * owners))
    slot_count = owners * capacity
    flat_routes = routes.reshape(pair_count)
    onehot = (flat_routes[:, None] == jnp.arange(owners, dtype=jnp.int32)[None, :]).astype(
        jnp.int32
    )
    position = jnp.sum((jnp.cumsum(onehot, axis=0) - 1) * onehot, axis=1)
    slot_of = flat_routes * capacity + position
    chosen = slot_of[None, :] == jnp.arange(slot_count, dtype=jnp.int32)[:, None]
    pair_map = chosen.astype(jnp.bfloat16)
    token_map = jnp.any(chosen.reshape(slot_count, tok_rows, top_count), axis=2).astype(
        jnp.bfloat16
    )
    outgoing = jnp.dot(token_map, tokens, preferred_element_type=jnp.float32).astype(jnp.bfloat16)
    gathered = (
        lax.all_gather(gate_weight, "dp", axis=1, tiled=True),
        lax.all_gather(up_weight, "dp", axis=1, tiled=True),
        lax.all_gather(down_weight, "dp", axis=1, tiled=True),
    )
    w_gate = gathered[0][0]
    w_up = gathered[1][0]
    w_down = gathered[2][0]
    arrived = lax.all_to_all(
        outgoing.reshape(owners, capacity, feat_width),
        "expert",
        split_axis=0,
        concat_axis=0,
        tiled=True,
    )
    item_count = arrived.shape[1]
    flat_rows = arrived.reshape(owners * item_count, feat_width)
    pre_gate = jnp.dot(flat_rows, w_gate, preferred_element_type=jnp.float32)
    pre_up = jnp.dot(flat_rows, w_up, preferred_element_type=jnp.float32)
    hidden = (jax.nn.silu(pre_gate) * pre_up).astype(jnp.bfloat16)
    expert_out = contract_last(hidden, w_down).astype(jnp.bfloat16)
    returned = lax.all_to_all(
        to_items(expert_out, item_count, owners), "expert", split_axis=0, concat_axis=0, tiled=True
    )
    x_slots = arrived.reshape(slot_count, feat_width)
    out_pairs = contract_rows(pair_map, returned.reshape(slot_count, feat_width))
    out_pairs = out_pairs.reshape(tok_rows, top_count, feat_width)
    mixed = jnp.sum(gates[:, :, None] * out_pairs, axis=1).astype(jnp.bfloat16)
    cot_float = cotangent.astype(jnp.float32)
    gate_grads = jnp.sum(cot_float[:, None, :] * out_pairs, axis=2)
    scaled = (
        (gates[:, :, None] * cot_float[:, None, :])
        .astype(jnp.bfloat16)
        .reshape(pair_count, feat_width)
    )
    sendable = jnp.dot(pair_map, scaled, preferred_element_type=jnp.float32).astype(jnp.bfloat16)
    arrived_grad = lax.all_to_all(
        sendable.reshape(owners, capacity, feat_width),
        "expert",
        split_axis=0,
        concat_axis=0,
        tiled=True,
    )
    arrived_grad = arrived_grad.reshape(slot_count, feat_width)
    pre_gate = jnp.dot(x_slots, w_gate, preferred_element_type=jnp.float32)
    pre_up = jnp.dot(x_slots, w_up, preferred_element_type=jnp.float32)
    sigmoid_gate = jax.nn.sigmoid(pre_gate)
    hidden = (jax.nn.silu(pre_gate) * pre_up).astype(jnp.bfloat16)
    grad_hidden = jnp.dot(arrived_grad, w_down, preferred_element_type=jnp.float32)
    d_gate = (grad_hidden * pre_up * sigmoid_gate * (1.0 + pre_gate * (1.0 - sigmoid_gate))).astype(
        jnp.bfloat16
    )
    d_up = (grad_hidden * pre_gate * sigmoid_gate).astype(jnp.bfloat16)
    grad_rows = (contract_last(d_gate, w_gate) + contract_last(d_up, w_up)).astype(jnp.bfloat16)
    back_rows = lax.all_to_all(
        grad_rows.reshape(owners, capacity, feat_width),
        "expert",
        split_axis=0,
        concat_axis=0,
        tiled=True,
    )
    token_grads = contract_rows(token_map, back_rows.reshape(slot_count, feat_width)).astype(
        jnp.bfloat16
    )
    partial_gate = contract_rows(x_slots, d_gate).astype(jnp.bfloat16)
    partial_up = contract_rows(x_slots, d_up).astype(jnp.bfloat16)
    partial_down = contract_rows(arrived_grad, hidden).astype(jnp.bfloat16)
    received = (
        lax.all_to_all(partial_gate[None], "dp", split_axis=1, concat_axis=0, tiled=True),
        lax.all_to_all(partial_up[None], "dp", split_axis=1, concat_axis=0, tiled=True),
        lax.all_to_all(partial_down[None], "dp", split_axis=1, concat_axis=0, tiled=True),
    )
    grad_gate_w = jnp.sum(received[0].astype(jnp.float32), axis=0)
    grad_up_w = jnp.sum(received[1].astype(jnp.float32), axis=0)
    grad_down_w = jnp.sum(received[2].astype(jnp.float32), axis=0)
    return (mixed, token_grads, gate_grads, grad_gate_w[None], grad_up_w[None], grad_down_w[None])


def solution(mesh):
    placed = (
        P(("dp", "expert"), None),
        P(("dp", "expert"), None),
        P(("dp", "expert"), None),
        P("expert", "dp", None),
        P("expert", "dp", None),
        P("expert", "dp", None),
        P(("dp", "expert"), None),
    )
    return jax.shard_map(
        on_device,
        mesh=mesh,
        in_specs=placed,
        out_specs=(
            P(("dp", "expert"), None),
            P(("dp", "expert"), None),
            P(("dp", "expert"), None),
            P("expert", "dp", None),
            P("expert", "dp", None),
            P("expert", "dp", None),
        ),
        check_vma=False,
    )
```

profile of v0, /device:TPU:0, one launch (start us, length us, event | category | flops | bytes accessed | tf_op | source)
XLA Modules:
  0.0 219.8 jit_solution(5725351280638407360)
XLA Ops:
  5.9 7.6 %all-to-all-start = ((bf16[16,40,1024]{2,1,0:T(8,128)(2,1)}), bf16[16,40,1024]{2,1,0:T(8,128)(2,1)}, u32[]{:S(2)}, u32[]{:S(2)}) async-start(bf16[16,40,1024]{2,1,0:T(8,128)(2,1)} %bitcast.2), calls=%async_computation | async-start | bytes 2621440 | tf_op jit(solution)/shard_map/all_to_all | solution.py:50
  16.0 3.6 %convolution_convert_fusion = bf16[640,1024]{1,0:T(8,128)(2,1)} fusion(f32[512,1024]{1,0:T(8,128)} %mul.90, f32[512]{0:T(512)S(1)} %mul.87, s32[512]{0:T(512)S(1)} %multiply_add_fusion), kind=kOutput, calls=%fused_computation.4 | convolution fusion | flops 673120256 | bytes 3411968 | tf_op jit(solution)/shard_map/dot_general | solution.py:77
  19.6 21.3 %all-to-all-done = bf16[16,40,1024]{2,1,0:T(8,128)(2,1)} async-done(((bf16[16,40,1024]{2,1,0:T(8,128)(2,1)}), bf16[16,40,1024]{2,1,0:T(8,128)(2,1)}, u32[]{:S(2)}, u32[]{:S(2)}) %all-to-all-start) | async-done | bytes 1310752 | tf_op jit(solution)/shard_map/all_to_all | solution.py:50
  40.9 8.2 %all-to-all-start.2 = ((bf16[16,40,1024]{2,1,0:T(8,128)(2,1)}), bf16[16,40,1024]{2,1,0:T(8,128)(2,1)}, u32[]{:S(2)}, u32[]{:S(2)}) async-start(bf16[16,40,1024]{2,1,0:T(8,128)(2,1)} %bitcast.10), calls=%async_computation.2 | async-start | bytes 2621440 | tf_op jit(solution)/shard_map/all_to_all | solution.py:78
  49.2 12.2 %all_gather.9 = bf16[1,1024,384]{2,1,0:T(8,128)(2,1)S(1)} all-gather(bf16[1,512,384]{2,1,0:T(8,128)(2,1)S(1)} %copy-done.16), channel_id=1, replica_groups=mesh['dp'=2,'expert'=16] {'dp'}, dimensions={1}, use_global_device_ids=true | all-gather | bytes 1179648 | tf_op jit(solution)/shard_map/all_gather | solution.py:43
  61.3 11.3 %all_gather.10 = bf16[1,1024,384]{2,1,0:T(8,128)(2,1)S(1)} all-gather(bf16[1,512,384]{2,1,0:T(8,128)(2,1)S(1)} %copy-done.17), channel_id=1, replica_groups=mesh['dp'=2,'expert'=16] {'dp'}, dimensions={1}, use_global_device_ids=true | all-gather | bytes 1179648 | tf_op jit(solution)/shard_map/all_gather | solution.py:44
  72.7 10.6 %all_gather.11 = bf16[1,1024,384]{2,1,0:T(8,128)(2,1)S(1)} all-gather(bf16[1,512,384]{2,1,0:T(8,128)(2,1)S(1)} %copy-done.18), channel_id=1, replica_groups=mesh['dp'=2,'expert'=16] {'dp'}, dimensions={1}, use_global_device_ids=true | all-gather | bytes 1179648 | tf_op jit(solution)/shard_map/all_gather | solution.py:45
  83.3 3.4 %fusion.16 = f32[640,384]{1,0:T(8,128)} fusion(bf16[640,1024]{1,0:T(8,128)(2,1)} %bitcast.3, bf16[1,1024,384]{2,1,0:T(8,128)(2,1)S(1)} %all_gather.9), kind=kOutput, calls=%fused_computation.33 | convolution fusion | flops 503316480 | bytes 3080192 | tf_op jit(solution)/shard_map/dot_general | solution.py:59
  86.8 3.1 %fusion.12 = f32[640,384]{1,0:T(8,128)} fusion(bf16[640,1024]{1,0:T(8,128)(2,1)} %bitcast.3, bf16[1,1024,384]{2,1,0:T(8,128)(2,1)S(1)} %all_gather.10), kind=kOutput, calls=%fused_computation.29 | convolution fusion | flops 503316480 | bytes 3080192 | tf_op jit(solution)/shard_map/dot_general | solution.py:60
  89.9 4.2 %multiply_convert_fusion.2 = (bf16[640,384]{1,0:T(8,128)(2,1)}, bf16[640,384]{1,0:T(8,128)(2,1)}, bf16[640,384]{1,0:T(8,128)(2,1)}) fusion(f32[640,384]{1,0:T(8,128)} %fusion.16, f32[640,384]{1,0:T(8,128)} %fusion.12, bf16[640,1024]{1,0:T(8,128)(2,1)} %bitcast.11, bf16[1,1024,384]{2,1,0:T(8,128)(2,1)S(1)} %all_gather.11), kind=kOutput, calls=%fused_computation.21 | convolution fusion | flops 507248640 | bytes 5537792 | tf_op jit(solution)/shard_map/dot_general | solution.py:90
  94.1 2.4 %fusion.4 = bf16[1,1024,384]{2,1,0:T(8,128)(2,1)S(1)} fusion(bf16[640,1024]{1,0:T(8,128)(2,1)} %bitcast.3, bf16[640,384]{1,0:T(8,128)(2,1)} %get-tuple-element.9), kind=kOutput, calls=%fused_computation.16 | convolution fusion | flops 503709696 | bytes 2588672 | tf_op jit(solution)/shard_map/dot_general | solution.py:12
  98.2 5.4 %reduce.2 = bf16[1024,384]{1,0:T(8,128)(2,1)S(1)} reduce(bf16[1024,1,384]{2,1,0:T(2,128)(2,1)S(1)} %bitcast.89, bf16[]{:T(256)} %broadcast.61), dimensions={1}, to_apply=%bitcast.87.reduce_sub_computation | reduce | bytes 1572866
  104.7 4.6 %all-to-all-start.4 = ((bf16[2,2,98304]{2,1,0:T(2,128)(2,1)}), bf16[2,2,98304]{2,1,0:T(2,128)(2,1)}, u32[]{:S(2)}, u32[]{:S(2)}) async-start(bf16[2,2,98304]{2,1,0:T(2,128)(2,1)} %reshape.131), calls=%async_computation.4 | async-start | bytes 1572864 | tf_op jit(solution)/shard_map/all_to_all | solution.py:110
  112.7 5.4 %reduce.3 = bf16[1024,384]{1,0:T(8,128)(2,1)S(1)} reduce(bf16[1024,1,384]{2,1,0:T(2,128)(2,1)S(1)} %bitcast.93, bf16[]{:T(256)} %broadcast.61), dimensions={1}, to_apply=%bitcast.86.reduce_sub_computation | reduce | bytes 1572866
  119.3 4.6 %all-to-all-start.5 = ((bf16[2,2,98304]{2,1,0:T(2,128)(2,1)}), bf16[2,2,98304]{2,1,0:T(2,128)(2,1)}, u32[]{:S(2)}, u32[]{:S(2)}) async-start(bf16[2,2,98304]{2,1,0:T(2,128)(2,1)} %reshape.133), calls=%async_computation.5 | async-start | bytes 1572864 | tf_op jit(solution)/shard_map/all_to_all | solution.py:111
  127.4 5.4 %reduce.4 = bf16[1024,384]{1,0:T(8,128)(2,1)S(1)} reduce(bf16[1024,1,384]{2,1,0:T(2,128)(2,1)S(1)} %bitcast.91, bf16[]{:T(256)} %broadcast.61), dimensions={1}, to_apply=%bitcast.85.reduce_sub_computation | reduce | bytes 1572866
  133.9 3.5 %all-to-all-start.6 = ((bf16[2,2,98304]{2,1,0:T(2,128)(2,1)}), bf16[2,2,98304]{2,1,0:T(2,128)(2,1)S(1)}, u32[]{:S(2)}, u32[]{:S(2)}) async-start(bf16[2,2,98304]{2,1,0:T(2,128)(2,1)} %reshape.135), calls=%async_computation.6 | async-start | bytes 1572864 | tf_op jit(solution)/shard_map/all_to_all | solution.py:112
  141.3 5.1 %all-to-all-done.6 = bf16[2,2,98304]{2,1,0:T(2,128)(2,1)S(1)} async-done(((bf16[2,2,98304]{2,1,0:T(2,128)(2,1)}), bf16[2,2,98304]{2,1,0:T(2,128)(2,1)S(1)}, u32[]{:S(2)}, u32[]{:S(2)}) %all-to-all-start.6) | async-done | bytes 786464 | tf_op jit(solution)/shard_map/all_to_all | solution.py:112
  147.3 5.2 %all-to-all-start.3 = ((bf16[16,40,1024]{2,1,0:T(8,128)(2,1)}), bf16[16,40,1024]{2,1,0:T(8,128)(2,1)S(1)}, u32[]{:S(2)}, u32[]{:S(2)}) async-start(bf16[16,40,1024]{2,1,0:T(8,128)(2,1)} %bitcast.12), calls=%async_computation.3 | async-start | bytes 2621440 | tf_op jit(solution)/shard_map/all_to_all | solution.py:96
  154.5 25.4 %all-to-all-done.3 = bf16[16,40,1024]{2,1,0:T(8,128)(2,1)S(1)} async-done(((bf16[16,40,1024]{2,1,0:T(8,128)(2,1)}), bf16[16,40,1024]{2,1,0:T(8,128)(2,1)S(1)}, u32[]{:S(2)}, u32[]{:S(2)}) %all-to-all-start.3) | async-done | bytes 1310752 | tf_op jit(solution)/shard_map/all_to_all | solution.py:96
  181.0 8.1 %all-to-all-start.1 = ((bf16[16,40,1024]{2,1,0:T(8,128)(2,1)}), bf16[16,40,1024]{2,1,0:T(8,128)(2,1)}, u32[]{:S(2)}, u32[]{:S(2)}) async-start(bf16[16,40,1024]{2,1,0:T(8,128)(2,1)} %bitcast.7), calls=%async_computation.1 | async-start | bytes 2621440 | tf_op jit(solution)/shard_map/all_to_all | solution.py:63
  191.8 2.6 %reshape.134 = bf16[1024,1,384]{2,1,0:T(2,128)(2,1)} reshape(bf16[2,2,98304]{2,1,0:T(2,128)(2,1)} %all-to-all-done.5) | data formatting | bytes 1572864
  201.7 14.8 %all-to-all-done.1 = bf16[16,40,1024]{2,1,0:T(8,128)(2,1)} async-done(((bf16[16,40,1024]{2,1,0:T(8,128)(2,1)}), bf16[16,40,1024]{2,1,0:T(8,128)(2,1)}, u32[]{:S(2)}, u32[]{:S(2)}) %all-to-all-start.1) | async-done | bytes 1310752 | tf_op jit(solution)/shard_map/all_to_all | solution.py:63
  216.5 3.2 %multiply_reduce_fusion = (f32[128,4]{0,1:T(4,128)}, bf16[128,1024]{1,0:T(8,128)(2,1)}) fusion(f32[128,1024]{1,0:T(8,128)S(1)} %copy-done.11, f32[128,4]{0,1:T(4,128)S(1)} %copy-done.19, bf16[640,1024,1]{1,0,2:T(8,128)(2,1)} %bitcast.9, s32[128,4]{0,1:T(4,128)S(1)} %multiply_add_fusion.1), kind=kOutput, calls=%fused_computation.1 | convolution fusion | flops 673381888 | bytes 2103296 | tf_op jit(solution)/shard_map/dot_general | solution.py:12
  (84 shorter events, 37.4 us)
Async XLA Ops:
  0.6 3.6 %copy-start = (bf16[128,1024]{1,0:T(8,128)(2,1)S(1)}, bf16[128,1024]{1,0:T(8,128)(2,1)}, u32[]{:S(2)}) copy-start(bf16[128,1024]{1,0:T(8,128)(2,1)} %param.7) | copy-start | bytes 786436
  5.9 7.6 %copy-start.9 = (bf16[128,1024]{1,0:T(8,128)(2,1)S(1)}, bf16[128,1024]{1,0:T(8,128)(2,1)}, u32[]{:S(2)}) copy-start(bf16[128,1024]{1,0:T(8,128)(2,1)} %param.13) | copy-start | bytes 786436
  5.9 35.0 %all-to-all-start = ((bf16[16,40,1024]{2,1,0:T(8,128)(2,1)}), bf16[16,40,1024]{2,1,0:T(8,128)(2,1)}, u32[]{:S(2)}, u32[]{:S(2)}) async-start(bf16[16,40,1024]{2,1,0:T(8,128)(2,1)} %bitcast.2), calls=%async_computation | async-start | bytes 2621440 | tf_op jit(solution)/shard_map/all_to_all | solution.py:50
  14.0 1.8 copy-start.19
  40.9 8.2 %copy-start.16 = (bf16[1,512,384]{2,1,0:T(8,128)(2,1)S(1)}, bf16[1,512,384]{2,1,0:T(8,128)(2,1)}, u32[]{:S(2)}) copy-start(bf16[1,512,384]{2,1,0:T(8,128)(2,1)} %param.10) | copy-start | bytes 1179652
  40.9 20.4 %copy-start.17 = (bf16[1,512,384]{2,1,0:T(8,128)(2,1)S(1)}, bf16[1,512,384]{2,1,0:T(8,128)(2,1)}, u32[]{:S(2)}) copy-start(bf16[1,512,384]{2,1,0:T(8,128)(2,1)} %param.11) | copy-start | bytes 1179652
  40.9 48.9 %all-to-all-start.2 = ((bf16[16,40,1024]{2,1,0:T(8,128)(2,1)}), bf16[16,40,1024]{2,1,0:T(8,128)(2,1)}, u32[]{:S(2)}, u32[]{:S(2)}) async-start(bf16[16,40,1024]{2,1,0:T(8,128)(2,1)} %bitcast.10), calls=%async_computation.2 | async-start | bytes 2621440 | tf_op jit(solution)/shard_map/all_to_all | solution.py:78
  49.1 23.6 %copy-start.18 = (bf16[1,512,384]{2,1,0:T(8,128)(2,1)S(1)}, bf16[1,512,384]{2,1,0:T(8,128)(2,1)}, u32[]{:S(2)}) copy-start(bf16[1,512,384]{2,1,0:T(8,128)(2,1)} %param.12) | copy-start | bytes 1179652
  61.3 25.4 %copy-start.7 = (bf16[1,1024,384]{2,1,0:T(8,128)(2,1)}, bf16[1,1024,384]{2,1,0:T(8,128)(2,1)S(1)}, u32[]{:S(2)}) copy-start(bf16[1,1024,384]{2,1,0:T(8,128)(2,1)S(1)} %all_gather.9) | copy-start | bytes 2359300
  83.3 6.5 %copy-start.3 = (bf16[1,1024,384]{2,1,0:T(8,128)(2,1)}, bf16[1,1024,384]{2,1,0:T(8,128)(2,1)S(1)}, u32[]{:S(2)}) copy-start(bf16[1,1024,384]{2,1,0:T(8,128)(2,1)S(1)} %all_gather.11) | copy-start | bytes 2359300
  103.6 5.6 %copy-start.14 = (bf16[640,384]{1,0:T(8,128)(2,1)S(1)}, bf16[640,384]{1,0:T(8,128)(2,1)}, u32[]{:S(2)}) copy-start(bf16[640,384]{1,0:T(8,128)(2,1)} %get-tuple-element.8) | copy-start | bytes 1474564
  104.7 14.6 %all-to-all-start.4 = ((bf16[2,2,98304]{2,1,0:T(2,128)(2,1)}), bf16[2,2,98304]{2,1,0:T(2,128)(2,1)}, u32[]{:S(2)}, u32[]{:S(2)}) async-start(bf16[2,2,98304]{2,1,0:T(2,128)(2,1)} %reshape.131), calls=%async_computation.4 | async-start | bytes 1572864 | tf_op jit(solution)/shard_map/all_to_all | solution.py:110
  118.2 5.7 %copy-start.12 = (bf16[640,384]{1,0:T(8,128)(2,1)S(1)}, bf16[640,384]{1,0:T(8,128)(2,1)}, u32[]{:S(2)}) copy-start(bf16[640,384]{1,0:T(8,128)(2,1)} %get-tuple-element.10) | copy-start | bytes 1474564
  119.3 14.6 %all-to-all-start.5 = ((bf16[2,2,98304]{2,1,0:T(2,128)(2,1)}), bf16[2,2,98304]{2,1,0:T(2,128)(2,1)}, u32[]{:S(2)}, u32[]{:S(2)}) async-start(bf16[2,2,98304]{2,1,0:T(2,128)(2,1)} %reshape.133), calls=%async_computation.5 | async-start | bytes 1572864 | tf_op jit(solution)/shard_map/all_to_all | solution.py:111
  132.8 4.6 %copy-start.8 = (bf16[1,1024,384]{2,1,0:T(8,128)(2,1)S(1)}, bf16[1,1024,384]{2,1,0:T(8,128)(2,1)}, u32[]{:S(2)}) copy-start(bf16[1,1024,384]{2,1,0:T(8,128)(2,1)} %copy-done.7) | copy-start | bytes 2359300
  133.9 12.6 %all-to-all-start.6 = ((bf16[2,2,98304]{2,1,0:T(2,128)(2,1)}), bf16[2,2,98304]{2,1,0:T(2,128)(2,1)S(1)}, u32[]{:S(2)}, u32[]{:S(2)}) async-start(bf16[2,2,98304]{2,1,0:T(2,128)(2,1)} %reshape.135), calls=%async_computation.6 | async-start | bytes 1572864 | tf_op jit(solution)/shard_map/all_to_all | solution.py:112
  137.4 2.0 copy-start.15
  146.5 6.1 %copy-start.4 = (bf16[1,1024,384]{2,1,0:T(8,128)(2,1)S(1)}, bf16[1,1024,384]{2,1,0:T(8,128)(2,1)}, u32[]{:S(2)}) copy-start(bf16[1,1024,384]{2,1,0:T(8,128)(2,1)} %copy-done.3) | copy-start | bytes 2359300
  146.5 6.1 %copy-start.13 = (bf16[640,384]{1,0:T(8,128)(2,1)S(1)}, bf16[640,384]{1,0:T(8,128)(2,1)}, u32[]{:S(2)}) copy-start(bf16[640,384]{1,0:T(8,128)(2,1)} %get-tuple-element.10) | copy-start | bytes 1474564
  147.3 32.6 %all-to-all-start.3 = ((bf16[16,40,1024]{2,1,0:T(8,128)(2,1)}), bf16[16,40,1024]{2,1,0:T(8,128)(2,1)S(1)}, u32[]{:S(2)}, u32[]{:S(2)}) async-start(bf16[16,40,1024]{2,1,0:T(8,128)(2,1)} %bitcast.12), calls=%async_computation.3 | async-start | bytes 2621440 | tf_op jit(solution)/shard_map/all_to_all | solution.py:96
  179.9 9.1 %copy-start.10 = (bf16[128,1024]{1,0:T(8,128)(2,1)S(1)}, bf16[128,1024]{1,0:T(8,128)(2,1)}, u32[]{:S(2)}) copy-start(bf16[128,1024]{1,0:T(8,128)(2,1)} %param.13) | copy-start | bytes 786436
  181.0 35.5 %all-to-all-start.1 = ((bf16[16,40,1024]{2,1,0:T(8,128)(2,1)}), bf16[16,40,1024]{2,1,0:T(8,128)(2,1)}, u32[]{:S(2)}, u32[]{:S(2)}) async-start(bf16[16,40,1024]{2,1,0:T(8,128)(2,1)} %bitcast.7), calls=%async_computation.1 | async-start | bytes 2621440 | tf_op jit(solution)/shard_map/all_to_all | solution.py:63
  199.0 1.6 copy-start.2
  200.0 16.5 %copy-start.11 = (f32[128,1024]{1,0:T(8,128)S(1)}, f32[128,1024]{1,0:T(8,128)}, u32[]{:S(2)}) copy-start(f32[128,1024]{1,0:T(8,128)} %convert_element_type.83) | copy-start | bytes 1572868
  (3 other events, 3.2 us)
where the time goes:
time: 223 us; the launch traced here: 220 us
  waiting for transfers between devices  66.7 us (30%)
  starting transfers between devices  41.7 us (19%)
  blocking collectives  34.2 us (15%)
  matrix products  33.1 us (15%)
  other arithmetic  22.5 us (10%)
  local copies, waits for them, and re-layouts  20.7 us (9%)
    all_to_all x1, waiting for transfers between devices, on_device(): lax.all_to_all(grad_rows.reshape(owners, capacity, feat_width), 'expert',...  25.4 us
    all_to_all x1, waiting for transfers between devices, on_device(): lax.all_to_all(outgoing.reshape(owners, capacity, feat_width), 'expert',...  21.3 us
    unnamed x3, other arithmetic  16.3 us
    all_to_all x1, waiting for transfers between devices, on_device(): lax.all_to_all(to_items(expert_out, item_count, owners), 'expert', split_...  14.8 us
    unnamed x52, local copies, waits for them, and re-layouts  14 us
    all_gather x1, blocking collectives, on_device(): lax.all_gather(gate_weight, 'dp', axis=1, tiled=True)  12.2 us
    all_gather x1, blocking collectives, on_device(): lax.all_gather(up_weight, 'dp', axis=1, tiled=True)  11.3 us
    dot_general x5, matrix products, contract_rows(): lax.dot_general(left, right, (((0,), (0,)), ((), ())), preferred_element_...  11.3 us
  transfers between devices with their start and end apart: 7, of which 4 were waited for; matrix products, arithmetic and copies ran while one was open for 23% of the time, Pallas kernels for 0%

commit v1 on v0

v1 whole, which is shorter than its diff:
```python
import functools

import jax
import jax.numpy as jnp
from jax import lax
from jax.experimental import pallas as pl
from jax.experimental.pallas import tpu as pltpu
from jax.sharding import PartitionSpec as P

BF = jnp.bfloat16
F32 = jnp.float32


def dot(left, right):
    return jnp.dot(left, right, preferred_element_type=F32)


def dot_rows(left, right):
    return lax.dot_general(left, right, (((0,), (0,)), ((), ())), preferred_element_type=F32)


def dot_last(left, right):
    return lax.dot_general(left, right, (((1,), (1,)), ((), ())), preferred_element_type=F32)


def chunk_of(rows):
    return 128 if rows % 128 == 0 else rows


def cost(flops, nbytes):
    return pl.CostEstimate(flops=flops, bytes_accessed=nbytes, transcendentals=0)


def slots_kernel(owners, capacity, routes_ref, slot_ref):
    top, rows = routes_ref.shape
    routes = routes_ref[...]
    expert = lax.broadcasted_iota(jnp.int32, (owners, rows), 0)
    named = [(routes[k : k + 1, :] == expert).astype(F32) for k in range(top)]
    onehot = sum(named)
    before = lax.broadcasted_iota(jnp.int32, (rows, rows), 0) < lax.broadcasted_iota(
        jnp.int32, (rows, rows), 1
    )
    position = dot(onehot.astype(BF), before.astype(F32).astype(BF))
    for k in range(top):
        own = jnp.sum(named[k] * position, axis=0, keepdims=True).astype(jnp.int32)
        slot_ref[k : k + 1, :] = routes[k : k + 1, :] * capacity + own


def select_of(slots, start, count):
    at = lax.broadcasted_iota(jnp.int32, (count, slots.shape[1]), 0) + start
    hit = slots[0:1, :] == at
    for k in range(1, slots.shape[0]):
        hit = hit | (slots[k : k + 1, :] == at)
    return hit


def gather_kernel(chunk, slot_ref, rows_ref, out_ref):
    slots = slot_ref[...]
    for start in range(0, out_ref.shape[0], chunk):
        picked = select_of(slots, start, chunk).astype(F32).astype(BF)
        out_ref[start : start + chunk, :] = dot(picked, rows_ref[...]).astype(BF)


def scaled_kernel(chunk, slot_ref, gates_ref, rows_ref, out_ref):
    slots = slot_ref[...]
    top = slots.shape[0]
    for start in range(0, out_ref.shape[0], chunk):
        at = lax.broadcasted_iota(jnp.int32, (chunk, slots.shape[1]), 0) + start
        weight = jnp.zeros((chunk, slots.shape[1]), F32)
        for k in range(top):
            weight = weight + jnp.where(slots[k : k + 1, :] == at, gates_ref[k : k + 1, :], 0.0)
        picked = select_of(slots, start, chunk).astype(F32).astype(BF)
        gate = jnp.sum(weight, axis=1, keepdims=True)
        out_ref[start : start + chunk, :] = (gate * dot(picked, rows_ref[...])).astype(BF)


def forward_kernel(pieces, at_ref, x_ref, *refs):
    weights = refs[: 3 * pieces]
    out_ref, gate_ref, up_ref, hidden_ref = refs[3 * pieces :]
    width = weights[0].shape[0]
    pre_gate = pre_up = 0.0
    for p in range(pieces):
        cols = pl.ds(pl.multiple_of(at_ref[p], 128), width)
        part = x_ref[:, cols]
        pre_gate = pre_gate + dot(part, weights[p][...])
        pre_up = pre_up + dot(part, weights[pieces + p][...])
    gate_ref[...] = pre_gate
    up_ref[...] = pre_up
    hidden = (pre_gate / (1.0 + jnp.exp(-pre_gate)) * pre_up).astype(BF)
    hidden_ref[...] = hidden
    for p in range(pieces):
        cols = pl.ds(pl.multiple_of(at_ref[p], 128), width)
        out_ref[:, cols] = dot_last(hidden, weights[2 * pieces + p][...]).astype(BF)


def backward_kernel(pieces, at_ref, g_ref, gate_ref, up_ref, *refs):
    weights = refs[: 3 * pieces]
    out_ref, d_gate_ref, d_up_ref = refs[3 * pieces :]
    width = weights[0].shape[0]
    grad = 0.0
    for p in range(pieces):
        cols = pl.ds(pl.multiple_of(at_ref[p], 128), width)
        grad = grad + dot(g_ref[:, cols], weights[2 * pieces + p][...])
    pre_gate = gate_ref[...]
    sig = 1.0 / (1.0 + jnp.exp(-pre_gate))
    d_gate = (grad * up_ref[...] * sig * (1.0 + pre_gate * (1.0 - sig))).astype(BF)
    d_up = (grad * pre_gate * sig).astype(BF)
    d_gate_ref[...] = d_gate
    d_up_ref[...] = d_up
    for p in range(pieces):
        cols = pl.ds(pl.multiple_of(at_ref[p], 128), width)
        out_ref[:, cols] = (
            dot_last(d_gate, weights[p][...]) + dot_last(d_up, weights[pieces + p][...])
        ).astype(BF)


def weights_kernel(width, at_ref, x_ref, g_ref, d_gate_ref, d_up_ref, hidden_ref, out_ref):
    cols = pl.ds(pl.multiple_of(at_ref[pl.program_id(0)], 128), width)
    x = x_ref[:, cols]
    out_ref[0, 0] = dot_rows(x, d_gate_ref[...]).astype(BF)
    out_ref[0, 1] = dot_rows(x, d_up_ref[...]).astype(BF)
    out_ref[0, 2] = dot_rows(g_ref[:, cols], hidden_ref[...]).astype(BF)


def mix_kernel(slot_ref, gates_ref, cot_ref, rows_ref, mixed_ref, grads_ref):
    slots = slot_ref[...]
    rows = rows_ref[...]
    cot = cot_ref[...].astype(F32)
    at = lax.broadcasted_iota(jnp.int32, (rows.shape[0], slots.shape[1]), 0)
    total = 0.0
    for k in range(slots.shape[0]):
        picked = (slots[k : k + 1, :] == at).astype(F32).astype(BF)
        row = dot_rows(picked, rows)
        total = total + gates_ref[:, k : k + 1] * row
        grads_ref[:, k : k + 1] = jnp.sum(cot * row, axis=1, keepdims=True)
    mixed_ref[...] = total.astype(BF)


def combine_kernel(slot_ref, rows_ref, out_ref):
    rows = rows_ref[...]
    picked = select_of(slot_ref[...], 0, rows.shape[0]).astype(F32).astype(BF)
    out_ref[...] = dot_rows(picked, rows).astype(BF)


def whole(shape):
    return pl.BlockSpec(shape, lambda i, *_: (0,) * len(shape))


def expert_call(kernel, at, streamed, weights, outs, chunk, flops):
    rows = streamed[0].shape[0]
    tiles = lambda a: pl.BlockSpec((chunk, a.shape[1]), lambda i, *_: (i, 0))
    nbytes = sum(a.size * a.dtype.itemsize for a in (*streamed, *weights, *outs))
    return pl.pallas_call(
        kernel,
        out_shape=outs,
        grid_spec=pltpu.PrefetchScalarGridSpec(
            num_scalar_prefetch=1,
            grid=(rows // chunk,),
            in_specs=[tiles(a) for a in streamed] + [whole(w.shape) for w in weights],
            out_specs=[tiles(a) for a in outs],
        ),
        cost_estimate=cost(flops, nbytes),
    )(at, *streamed, *weights)


def on_device(tokens, routes, gates, gate_weight, up_weight, down_weight, cotangent):
    owners = lax.axis_size("expert")
    replicas = lax.axis_size("dp")
    tok_rows, feat = tokens.shape
    top = routes.shape[1]
    hid = gate_weight.shape[2]
    pair_count = tok_rows * top
    capacity = max(2, pair_count * 5 // (4 * owners))
    slot_count = owners * capacity
    chunk = chunk_of(slot_count)
    sds = jax.ShapeDtypeStruct

    own = [gate_weight[0], up_weight[0], down_weight[0]]
    share = own[0].shape[0]
    if replicas == 2:
        me = lax.axis_index("dp")
        swap = [(0, 1), (1, 0)]
        peer = [lax.ppermute(w, "dp", swap) for w in own]
        weights = [own[0], peer[0], own[1], peer[1], own[2], peer[2]]
        pieces = 2
        at = jnp.stack([me * share, (1 - me) * share]).astype(jnp.int32)
    else:
        weights = [lax.all_gather(w, "dp", axis=0, tiled=True) for w in own]
        pieces = 1
        at = jnp.zeros((1,), jnp.int32)

    def exchange(rows):
        moved = lax.all_to_all(
            rows.reshape(owners, capacity, feat), "expert", split_axis=0, concat_axis=0, tiled=True
        )
        return moved.reshape(slot_count, feat)

    slots = pl.pallas_call(
        functools.partial(slots_kernel, owners, capacity),
        out_shape=sds((top, tok_rows), jnp.int32),
    )(routes.T)
    row_bytes = slot_count * feat * 2
    picking = cost(2 * slot_count * tok_rows * feat, row_bytes + tok_rows * feat * 2)
    outgoing = pl.pallas_call(
        functools.partial(gather_kernel, chunk),
        out_shape=sds((slot_count, feat), BF),
        cost_estimate=picking,
    )(slots, tokens)
    arrived = exchange(outgoing)
    sendable = pl.pallas_call(
        functools.partial(scaled_kernel, chunk),
        out_shape=sds((slot_count, feat), BF),
        cost_estimate=picking,
    )(slots, gates.T, cotangent)
    arrived_grad = exchange(sendable)

    wide = sds((slot_count, hid), F32)
    narrow = sds((slot_count, hid), BF)
    work = 2 * slot_count * feat * hid
    expert_out, pre_gate, pre_up, hidden = expert_call(
        functools.partial(forward_kernel, pieces),
        at,
        [arrived],
        weights,
        [sds((slot_count, feat), BF), wide, wide, narrow],
        chunk,
        3 * work,
    )
    returned = exchange(expert_out)
    grad_rows, d_gate, d_up = expert_call(
        functools.partial(backward_kernel, pieces),
        at,
        [arrived_grad, pre_gate, pre_up],
        weights,
        [sds((slot_count, feat), BF), narrow, narrow],
        chunk,
        3 * work,
    )
    back_rows = exchange(grad_rows)

    width = feat // pieces
    partial = pl.pallas_call(
        functools.partial(weights_kernel, width),
        out_shape=sds((pieces, 3, width, hid), BF),
        grid_spec=pltpu.PrefetchScalarGridSpec(
            num_scalar_prefetch=1,
            grid=(pieces,),
            in_specs=[whole((slot_count, feat))] * 2 + [whole((slot_count, hid))] * 3,
            out_specs=pl.BlockSpec((1, 3, width, hid), lambda i, *_: (i, 0, 0, 0)),
        ),
        cost_estimate=cost(3 * work, 2 * row_bytes + 12 * feat * hid),
    )(at, arrived, arrived_grad, d_gate, d_up, hidden)
    if replicas == 2:
        got = lax.ppermute(partial[1], "dp", swap)
        grads = [partial[0, i].astype(F32) + got[i].astype(F32) for i in range(3)]
    else:
        got = lax.all_to_all(partial[0], "dp", split_axis=1, concat_axis=0, tiled=True)
        got = got.reshape(replicas, 3, share, hid).astype(F32)
        grads = [jnp.sum(got[:, i], axis=0) for i in range(3)]

    mixed, gate_grads = pl.pallas_call(
        mix_kernel,
        out_shape=(sds((tok_rows, feat), BF), sds((tok_rows, top), F32)),
        cost_estimate=cost(2 * top * slot_count * tok_rows * feat, row_bytes),
    )(slots, gates, cotangent, returned)
    token_grads = pl.pallas_call(
        combine_kernel,
        out_shape=sds((tok_rows, feat), BF),
        cost_estimate=picking,
    )(slots, back_rows)
    return (mixed, token_grads, gate_grads, grads[0][None], grads[1][None], grads[2][None])


def solution(mesh):
    rows = P(("dp", "expert"), None)
    weight = P("expert", "dp", None)
    return jax.shard_map(
        on_device,
        mesh=mesh,
        in_specs=(rows, rows, rows, weight, weight, weight, rows),
        out_specs=(rows, rows, rows, weight, weight, weight),
        check_vma=False,
    )
```

time: 223 us -> 184 us (0.83); the launches traced: 220 us -> 183 us
  Pallas kernels: 0 us -> 34.9 us
  matrix products: 33.1 us -> 0 us
  other arithmetic: 22.5 us -> 3.3 us
  starting transfers between devices: 41.7 us -> 24.9 us
  local copies, waits for them, and re-layouts: 20.7 us -> 6.64 us
  waiting for transfers between devices: 66.7 us -> 75.5 us
  blocking collectives: 34.2 us -> 37.3 us
    ppermute x0 -> x4, waiting for transfers between devices: none -> 50.6 us  [the longest x1 26.4 us: on_device(): got = lax.ppermute(partial[1], 'dp', swap)]
    all_to_all x7 -> x3, waiting for transfers between devices: 66.7 us -> 24.8 us  [exchange(): lax.all_to_all(rows.reshape(owners, capacity, feat), 'expert', split_axis...]
    all_to_all x0 -> x1, blocking collectives: none -> 37.3 us  [exchange(): lax.all_to_all(rows.reshape(owners, capacity, feat), 'expert', split_axis...]
    pallas_call x0 -> x8, Pallas kernels: none -> 34.9 us  [the longest x2 15.7 us: expert_call(): pl.pallas_call(kernel, out_shape=outs, grid_spec=pltpu.PrefetchScalarGrid...]
    all_gather x3 -> x0, blocking collectives: 34.2 us -> none  [the longest x1 12.2 us: on_device(): lax.all_gather(gate_weight, 'dp', axis=1, tiled=True)]
    dot_general x13 -> x0, matrix products: 33.1 us -> none  [the longest x5 11.3 us: contract_rows(): lax.dot_general(left, right, (((0,), (0,)), ((), ())), preferred_element_...]
    all_to_all x7 -> x3, starting transfers between devices: 41.7 us -> 19.8 us  [exchange(): lax.all_to_all(rows.reshape(owners, capacity, feat), 'expert', split_axis...]
    unnamed x3 -> x0, other arithmetic: 16.3 us -> none
  transfers between devices with their start and end apart: 7 -> 7, of which waited for: 4 -> 5; matrix products, arithmetic and copies ran while one was open for 23% -> 3% of each run, Pallas kernels for 0% -> 10%
where the time goes in v1:
time: 184 us; the launch traced here: 183 us
  waiting for transfers between devices  75.5 us (41%)
  blocking collectives  37.3 us (20%)
  Pallas kernels  34.9 us (19%)
  starting transfers between devices  24.9 us (14%)
  local copies, waits for them, and re-layouts  6.64 us (4%)
  other arithmetic  3.3 us (2%)
    all_to_all x1, blocking collectives, exchange(): lax.all_to_all(rows.reshape(owners, capacity, feat), 'expert', split_axis...  37.3 us
    ppermute x1, waiting for transfers between devices, on_device(): got = lax.ppermute(partial[1], 'dp', swap)  26.4 us
    all_to_all x3, waiting for transfers between devices, exchange(): lax.all_to_all(rows.reshape(owners, capacity, feat), 'expert', split_axis...  24.8 us
    ppermute x3, waiting for transfers between devices, on_device(): peer = [lax.ppermute(w, 'dp', swap) for w in own]  24.2 us
    all_to_all x3, starting transfers between devices, exchange(): lax.all_to_all(rows.reshape(owners, capacity, feat), 'expert', split_axis...  19.8 us
    pallas_call x2, Pallas kernels, expert_call(): pl.pallas_call(kernel, out_shape=outs, grid_spec=pltpu.PrefetchScalarGrid...  15.7 us
    pallas_call x1, Pallas kernels, on_device(): pl.pallas_call(functools.partial(weights_kernel, width), out_shape=sds((p...  6.73 us
    unnamed x20, local copies, waits for them, and re-layouts  5.1 us
  transfers between devices with their start and end apart: 7, of which 5 were waited for; matrix products, arithmetic and copies ran while one was open for 3% of the time, Pallas kernels for 10%

profile of v1, /device:TPU:0, one launch (start us, length us, event | category | flops | bytes accessed | tf_op | source)
XLA Modules:
  0.0 183.2 jit_solution(4285418063208779871)
XLA Ops:
  0.6 1.4 shard_map.118.slot_ref
  2.0 2.5 %shard_map.119 = bf16[640,1024]{1,0:T(8,128)(2,1)} custom-call(s32[4,128]{1,0:T(4,128)} %shard_map.118.slot_ref, bf16[128,1024]{1,0:T(8,128)(2,1)} %rows_ref.2), custom_call_target="tpu_custom_call" | custom-call | flops 167772160 | bytes 1572864 | tf_op jit(solution)/shard_map/pallas_call | solution.py:204
  4.6 7.4 %all-to-all-start = ((bf16[16,40,1024]{2,1,0:T(8,128)(2,1)}), bf16[16,40,1024]{2,1,0:T(8,128)(2,1)S(1)}, u32[]{:S(2)}, u32[]{:S(2)}) async-start(bf16[16,40,1024]{2,1,0:T(8,128)(2,1)} %bitcast.38), calls=%async_computation | async-start | bytes 2621440 | tf_op jit(solution)/shard_map/all_to_all | solution.py:193
  12.0 2.6 %shard_map.122 = bf16[640,1024]{1,0:T(8,128)(2,1)} custom-call(s32[4,128]{1,0:T(4,128)} %shard_map.118.slot_ref, f32[4,128]{1,0:T(4,128)} %bitcast.49, bf16[128,1024]{1,0:T(8,128)(2,1)} %rows_ref.3), custom_call_target="tpu_custom_call" | custom-call | flops 167772160 | bytes 1572864 | tf_op jit(solution)/shard_map/pallas_call | solution.py:210
  14.6 24.8 %all-to-all-done = bf16[16,40,1024]{2,1,0:T(8,128)(2,1)S(1)} async-done(((bf16[16,40,1024]{2,1,0:T(8,128)(2,1)}), bf16[16,40,1024]{2,1,0:T(8,128)(2,1)S(1)}, u32[]{:S(2)}, u32[]{:S(2)}) %all-to-all-start) | async-done | bytes 1310752 | tf_op jit(solution)/shard_map/all_to_all | solution.py:193
  40.5 8.0 %all-to-all-start.2 = ((bf16[16,40,1024]{2,1,0:T(8,128)(2,1)}), bf16[16,40,1024]{2,1,0:T(8,128)(2,1)S(1)}, u32[]{:S(2)}, u32[]{:S(2)}) async-start(bf16[16,40,1024]{2,1,0:T(8,128)(2,1)} %bitcast.36), calls=%async_computation.2 | async-start | bytes 2621440 | tf_op jit(solution)/shard_map/all_to_all | solution.py:193
  48.5 1.5 collective-permute-start
  50.6 1.5 collective-permute-start.2
  52.6 7.8 %collective-permute-done.refs_1_ = bf16[512,384]{1,0:T(8,128)(2,1)S(1)} collective-permute-done((bf16[512,384]{1,0:T(8,128)(2,1)S(1)}, bf16[512,384]{1,0:T(8,128)(2,1)S(1)}, u32[]{:S(2)}, u32[]{:S(2)}) %collective-permute-start) | collective-permute-done | bytes 393248 | tf_op jit(solution)/shard_map/ppermute | solution.py:183
  60.5 8.4 %collective-permute-done.1.refs_3_ = bf16[512,384]{1,0:T(8,128)(2,1)S(1)} collective-permute-done((bf16[512,384]{1,0:T(8,128)(2,1)S(1)}, bf16[512,384]{1,0:T(8,128)(2,1)S(1)}, u32[]{:S(2)}, u32[]{:S(2)}) %collective-permute-start.1) | collective-permute-done | bytes 393248 | tf_op jit(solution)/shard_map/ppermute | solution.py:183
  68.9 8.0 %collective-permute-done.2.refs_5_ = bf16[512,384]{1,0:T(8,128)(2,1)S(1)} collective-permute-done((bf16[512,384]{1,0:T(8,128)(2,1)}, bf16[512,384]{1,0:T(8,128)(2,1)S(1)}, u32[]{:S(2)}, u32[]{:S(2)}) %collective-permute-start.2) | collective-permute-done | bytes 393248 | tf_op jit(solution)/shard_map/ppermute | solution.py:183
  77.6 7.4 %shard_map.120 = (bf16[640,1024]{1,0:T(8,128)(2,1)}, f32[640,384]{1,0:T(8,128)}, f32[640,384]{1,0:T(8,128)}, bf16[640,384]{1,0:T(8,128)(2,1)}) custom-call(s32[2]{0:T(128)} %pad_add_fusion.at_ref, bf16[640,1024]{1,0:T(8,128)(2,1)} %bitcast.34, bf16[512,384]{1,0:T(8,128)(2,1)} %bitcast.40, bf16[512,384]{1,0:T(8,128)(2,1)} %copy-done.5, ...), custom_call_target="tpu_custom_call" | custom-call | flops 1509949440 | bytes 7438336 | tf_op jit(solution)/shard_map/pallas_call | solution.py:153
  85.0 1.1 copy-done
  86.1 8.4 %shard_map.123 = (bf16[640,1024]{1,0:T(8,128)(2,1)}, bf16[640,384]{1,0:T(8,128)(2,1)}, bf16[640,384]{1,0:T(8,128)(2,1)}) custom-call(s32[2]{0:T(128)} %pad_add_fusion.at_ref, bf16[640,1024]{1,0:T(8,128)(2,1)} %bitcast.32, f32[640,384]{1,0:T(8,128)} %get-tuple-element.17.gate_ref, f32[640,384]{1,0:T(8,128)} %get-tuple-element.18.up_ref, ...), custom_call_target="tpu_custom_call" | custom-call | flops 1509949440 | bytes 7929856 | tf_op jit(solution)/shard_map/pallas_call | solution.py:153
  94.4 37.3 %all_to_all.20 = bf16[16,40,1024]{2,1,0:T(8,128)(2,1)} all-to-all(bf16[16,40,1024]{2,1,0:T(8,128)(2,1)} %bitcast.39), channel_id=1, replica_groups=mesh['dp'=2,'expert'=16] {'expert'}, dimensions={0} | all-to-all | bytes 2621440 | tf_op jit(solution)/shard_map/all_to_all | solution.py:193
  131.8 4.4 %all-to-all-start.1 = ((bf16[16,40,1024]{2,1,0:T(8,128)(2,1)}), bf16[16,40,1024]{2,1,0:T(8,128)(2,1)}, u32[]{:S(2)}, u32[]{:S(2)}) async-start(bf16[16,40,1024]{2,1,0:T(8,128)(2,1)} %bitcast.8), calls=%async_computation.1 | async-start | bytes 2621440 | tf_op jit(solution)/shard_map/all_to_all | solution.py:193
  136.2 6.7 %shard_map.125 = bf16[2,3,512,384]{3,2,1,0:T(8,128)(2,1)} custom-call(s32[2]{0:T(128)} %pad_add_fusion.at_ref, bf16[640,1024]{1,0:T(8,128)(2,1)} %bitcast.35, bf16[640,1024]{1,0:T(8,128)(2,1)} %bitcast.33, bf16[640,384]{1,0:T(8,128)(2,1)} %get-tuple-element.21.d_gate_ref, bf16[640,384]{1,0:T(8,128)(2,1)} %get-tuple-element.22.d_up_ref, ...), custom_call_target="tpu_custom_call" | custom-call | flops 1509949440 | bytes 7340032 | tf_op jit(solution)/shard_map/pallas_call | solution.py:242
  142.9 1.5 slice_bitcast_fusion
  144.4 1.5 collective-permute-start.3
  146.7 26.4 %collective-permute-done.3 = bf16[3,512,384]{2,1,0:T(8,128)(2,1)} collective-permute-done((bf16[3,512,384]{2,1,0:T(8,128)(2,1)S(1)}, bf16[3,512,384]{2,1,0:T(8,128)(2,1)}, u32[]{:S(2)}, u32[]{:S(2)}) %collective-permute-start.3) | collective-permute-done | bytes 1179680 | tf_op jit(solution)/shard_map/ppermute | solution.py:254
  173.2 2.7 %convert_add_fusion = (f32[1,512,384]{2,1,0:T(8,128)}, f32[1,512,384]{2,1,0:T(8,128)}, f32[1,512,384]{2,1,0:T(8,128)}) fusion(bf16[3,512,384]{2,1,0:T(8,128)(2,1)} %collective-permute-done.3, bf16[2,3,512,384]{3,2,1,0:T(8,128)(2,1)S(1)} %copy-done.1), kind=kLoop, calls=%fused_computation.1 | loop fusion | flops 1769472 | bytes 4718592 | tf_op jit(solution)/shard_map/add | solution.py:255
  175.9 2.5 %shard_map.124 = bf16[128,1024]{1,0:T(8,128)(2,1)} custom-call(s32[4,128]{1,0:T(4,128)} %shard_map.118.slot_ref, bf16[640,1024]{1,0:T(8,128)(2,1)} %bitcast.37), custom_call_target="tpu_custom_call" | custom-call | flops 167772160 | bytes 1572864 | tf_op jit(solution)/shard_map/pallas_call | solution.py:266
  178.4 3.4 %shard_map.121 = (bf16[128,1024]{1,0:T(8,128)(2,1)}, f32[128,4]{1,0:T(8,128)}) custom-call(s32[4,128]{1,0:T(4,128)} %shard_map.118.slot_ref, f32[128,4]{1,0:T(8,128)} %copy.13.gates_ref, bf16[128,1024]{1,0:T(8,128)(2,1)} %rows_ref.3, bf16[640,1024]{1,0:T(8,128)(2,1)} %bitcast.9.rows_ref), custom_call_target="tpu_custom_call" | custom-call | flops 671088640 | bytes 1310720 | tf_op jit(solution)/shard_map/pallas_call | solution.py:261
  181.8 1.5 copy.14
  (22 shorter events, 3.7 us)
Async XLA Ops:
  4.6 34.8 %all-to-all-start = ((bf16[16,40,1024]{2,1,0:T(8,128)(2,1)}), bf16[16,40,1024]{2,1,0:T(8,128)(2,1)S(1)}, u32[]{:S(2)}, u32[]{:S(2)}) async-start(bf16[16,40,1024]{2,1,0:T(8,128)(2,1)} %bitcast.38), calls=%async_computation | async-start | bytes 2621440 | tf_op jit(solution)/shard_map/all_to_all | solution.py:193
  39.4 1.1 copy-start.2
  39.4 9.1 %copy-start.3 = (bf16[1,512,384]{2,1,0:T(8,128)(2,1)S(1)}, bf16[1,512,384]{2,1,0:T(8,128)(2,1)}, u32[]{:S(2)}) copy-start(bf16[1,512,384]{2,1,0:T(8,128)(2,1)} %param.10) | copy-start | bytes 1179652
  39.4 10.6 %copy-start.4 = (bf16[1,512,384]{2,1,0:T(8,128)(2,1)S(1)}, bf16[1,512,384]{2,1,0:T(8,128)(2,1)}, u32[]{:S(2)}) copy-start(bf16[1,512,384]{2,1,0:T(8,128)(2,1)} %param.11) | copy-start | bytes 1179652
  40.5 44.5 %all-to-all-start.2 = ((bf16[16,40,1024]{2,1,0:T(8,128)(2,1)}), bf16[16,40,1024]{2,1,0:T(8,128)(2,1)S(1)}, u32[]{:S(2)}, u32[]{:S(2)}) async-start(bf16[16,40,1024]{2,1,0:T(8,128)(2,1)} %bitcast.36), calls=%async_computation.2 | async-start | bytes 2621440 | tf_op jit(solution)/shard_map/all_to_all | solution.py:193
  48.5 12.0 %collective-permute-start = (bf16[512,384]{1,0:T(8,128)(2,1)S(1)}, bf16[512,384]{1,0:T(8,128)(2,1)S(1)}, u32[]{:S(2)}, u32[]{:S(2)}) collective-permute-start(bf16[512,384]{1,0:T(8,128)(2,1)S(1)} %bitcast.42), channel_id=1, source_target_pairs={{0,16},{16,0},{1,17},{17,1},{2,18},{18,2},{3,19},{19,3},{4,20},{20... | collective-permute-start | bytes 1179656 | tf_op jit(solution)/shard_map/ppermute | solution.py:183
  50.0 18.9 %collective-permute-start.1 = (bf16[512,384]{1,0:T(8,128)(2,1)S(1)}, bf16[512,384]{1,0:T(8,128)(2,1)S(1)}, u32[]{:S(2)}, u32[]{:S(2)}) collective-permute-start(bf16[512,384]{1,0:T(8,128)(2,1)S(1)} %bitcast.45), channel_id=1, source_target_pairs={{0,16},{16,0},{1,17},{17,1},{2,18},{18,2},{3,19},{19,3},{4,20},{20... | collective-permute-start | bytes 1179656 | tf_op jit(solution)/shard_map/ppermute | solution.py:183
  50.6 26.3 %collective-permute-start.2 = (bf16[512,384]{1,0:T(8,128)(2,1)}, bf16[512,384]{1,0:T(8,128)(2,1)S(1)}, u32[]{:S(2)}, u32[]{:S(2)}) collective-permute-start(bf16[512,384]{1,0:T(8,128)(2,1)} %bitcast.46), channel_id=1, source_target_pairs={{0,16},{16,0},{1,17},{17,1},{2,18},{18,2},{3,19},{19,3},{4,20},{20... | collective-permute-start | bytes 1179656 | tf_op jit(solution)/shard_map/ppermute | solution.py:183
  60.5 16.4 %copy-start.5 = (bf16[512,384]{1,0:T(8,128)(2,1)}, bf16[512,384]{1,0:T(8,128)(2,1)S(1)}, u32[]{:S(2)}) copy-start(bf16[512,384]{1,0:T(8,128)(2,1)S(1)} %collective-permute-done.refs_1_) | copy-start | bytes 1179652
  68.9 8.0 %copy-start.6 = (bf16[512,384]{1,0:T(8,128)(2,1)}, bf16[512,384]{1,0:T(8,128)(2,1)S(1)}, u32[]{:S(2)}) copy-start(bf16[512,384]{1,0:T(8,128)(2,1)S(1)} %collective-permute-done.1.refs_3_) | copy-start | bytes 1179652
  76.9 0.8 copy-start.7
  85.0 1.1 copy-start
  131.8 46.6 %all-to-all-start.1 = ((bf16[16,40,1024]{2,1,0:T(8,128)(2,1)}), bf16[16,40,1024]{2,1,0:T(8,128)(2,1)}, u32[]{:S(2)}, u32[]{:S(2)}) async-start(bf16[16,40,1024]{2,1,0:T(8,128)(2,1)} %bitcast.8), calls=%async_computation.1 | async-start | bytes 2621440 | tf_op jit(solution)/shard_map/all_to_all | solution.py:193
  136.2 9.8 %copy-start.8 = (f32[128,4]{0,1:T(4,128)S(1)}, f32[128,4]{0,1:T(4,128)}, u32[]{:S(2)}) copy-start(f32[128,4]{0,1:T(4,128)} %param.9) | copy-start | bytes 6148
  142.9 30.3 %copy-start.1 = (bf16[2,3,512,384]{3,2,1,0:T(8,128)(2,1)S(1)}, bf16[2,3,512,384]{3,2,1,0:T(8,128)(2,1)}, u32[]{:S(2)}) copy-start(bf16[2,3,512,384]{3,2,1,0:T(8,128)(2,1)} %shard_map.125) | copy-start | bytes 7077892
  144.4 28.7 %collective-permute-start.3 = (bf16[3,512,384]{2,1,0:T(8,128)(2,1)S(1)}, bf16[3,512,384]{2,1,0:T(8,128)(2,1)}, u32[]{:S(2)}, u32[]{:S(2)}) collective-permute-start(bf16[3,512,384]{2,1,0:T(8,128)(2,1)S(1)} %slice_bitcast_fusion), channel_id=1, source_target_pairs={{0,16},{16,0},{1,17},{17,1},{2,18},{18,2},{3,19},{19,3},{4,20},{20... | collective-permute-start | bytes 3538952 | tf_op jit(solution)/shard_map/ppermute | solution.py:254

commit v2 on v1

v2 whole, which is shorter than its diff:
```python
import functools

import jax
import jax.numpy as jnp
from jax import lax
from jax.experimental import pallas as pl
from jax.experimental.pallas import tpu as pltpu
from jax.sharding import PartitionSpec as P

BF = jnp.bfloat16
F32 = jnp.float32


def dot(left, right):
    return jnp.dot(left, right, preferred_element_type=F32)


def dot_rows(left, right):
    return lax.dot_general(left, right, (((0,), (0,)), ((), ())), preferred_element_type=F32)


def dot_last(left, right):
    return lax.dot_general(left, right, (((1,), (1,)), ((), ())), preferred_element_type=F32)


def cost(flops, nbytes):
    return pl.CostEstimate(flops=flops, bytes_accessed=nbytes, transcendentals=0)


def slots_kernel(owners, capacity, routes_ref, gates_ref, out_ref):
    top, rows = routes_ref.shape
    routes = routes_ref[...]
    expert = lax.broadcasted_iota(jnp.int32, (owners, rows), 0)
    named = [(routes[k : k + 1, :] == expert).astype(F32) for k in range(top)]
    onehot = sum(named)
    before = lax.broadcasted_iota(jnp.int32, (rows, rows), 0) < lax.broadcasted_iota(
        jnp.int32, (rows, rows), 1
    )
    position = dot(onehot.astype(BF), before.astype(F32).astype(BF))
    base = (routes * capacity).astype(F32)
    for k in range(top):
        own = jnp.sum(named[k] * position, axis=0, keepdims=True)
        out_ref[k : k + 1, :] = base[k : k + 1, :] + own
    out_ref[top : 2 * top, :] = gates_ref[...]


def slots_of(top, base_ref, plan_ref):
    return plan_ref[0:top, :].astype(jnp.int32) - base_ref[0]


def pick_kernel(chunk, base_ref, plan_ref, tokens_ref, cot_ref, out_ref):
    top = plan_ref.shape[0] // 2
    slots = slots_of(top, base_ref, plan_ref)
    feat = tokens_ref.shape[1]
    for start in range(0, out_ref.shape[0], chunk):
        at = lax.broadcasted_iota(jnp.int32, (chunk, slots.shape[1]), 0) + start
        hits = [slots[k : k + 1, :] == at for k in range(top)]
        weight = sum(
            jnp.where(hit, plan_ref[top + k : top + k + 1, :], 0.0) for k, hit in enumerate(hits)
        )
        gate = jnp.sum(weight, axis=1, keepdims=True)
        picked = sum(hit.astype(F32) for hit in hits).astype(BF)
        rows = slice(start, start + chunk)
        out_ref[rows, :feat] = dot(picked, tokens_ref[...]).astype(BF)
        out_ref[rows, feat:] = (gate * dot(picked, cot_ref[...])).astype(BF)


def expert_kernel(pieces, at_ref, in_ref, *refs):
    weights = refs[: 3 * pieces]
    out_ref, d_gate_ref, d_up_ref, hidden_ref = refs[3 * pieces :]
    feat = in_ref.shape[1] // 2
    width = feat // pieces

    def cols(p, offset):
        return pl.ds(pl.multiple_of(at_ref[p] + offset, 128), width)

    pre_gate = pre_up = grad = 0.0
    for p in range(pieces):
        part = in_ref[:, cols(p, 0)]
        pre_gate = pre_gate + dot(part, weights[p][...])
        pre_up = pre_up + dot(part, weights[pieces + p][...])
    sig = 1.0 / (1.0 + jnp.exp(-pre_gate))
    hidden = (pre_gate * sig * pre_up).astype(BF)
    hidden_ref[...] = hidden
    for p in range(pieces):
        down = weights[2 * pieces + p][...]
        out_ref[:, cols(p, 0)] = dot_last(hidden, down).astype(BF)
        grad = grad + dot(in_ref[:, cols(p, feat)], down)
    d_gate = (grad * pre_up * sig * (1.0 + pre_gate * (1.0 - sig))).astype(BF)
    d_up = (grad * pre_gate * sig).astype(BF)
    d_gate_ref[...] = d_gate
    d_up_ref[...] = d_up
    for p in range(pieces):
        out_ref[:, cols(p, feat)] = (
            dot_last(d_gate, weights[p][...]) + dot_last(d_up, weights[pieces + p][...])
        ).astype(BF)


def weights_kernel(parts, at_ref, *refs):
    ins, out_ref = refs[:-1], refs[-1]
    width = out_ref.shape[1]
    feat = ins[0].shape[1] // 2
    sums = [0.0, 0.0, 0.0]
    for i in range(parts):
        rows, d_gate, d_up, hidden = ins[4 * i : 4 * i + 4]
        x = rows[:, pl.ds(pl.multiple_of(at_ref[0], 128), width)]
        g = rows[:, pl.ds(pl.multiple_of(at_ref[0] + feat, 128), width)]
        sums[0] = sums[0] + dot_rows(x, d_gate[...])
        sums[1] = sums[1] + dot_rows(x, d_up[...])
        sums[2] = sums[2] + dot_rows(g, hidden[...])
    for i in range(3):
        out_ref[i] = sums[i].astype(BF)


def combine_kernel(base_ref, plan_ref, gates_ref, cot_ref, rows_ref, out_ref, grads_ref):
    top = plan_ref.shape[0] // 2
    slots = slots_of(top, base_ref, plan_ref)
    feat = cot_ref.shape[1]
    rows = rows_ref[:, :feat]
    cot = cot_ref[...].astype(F32)
    at = lax.broadcasted_iota(jnp.int32, (rows.shape[0], slots.shape[1]), 0)
    total, every = 0.0, 0.0
    for k in range(top):
        picked = (slots[k : k + 1, :] == at).astype(F32)
        every = every + picked
        row = dot_rows(picked.astype(BF), rows)
        total = total + gates_ref[:, k : k + 1] * row
        grads_ref[:, k : k + 1] = jnp.sum(cot * row, axis=1, keepdims=True)
    out_ref[:, :feat] = total.astype(out_ref.dtype)
    out_ref[:, feat:] = dot_rows(every.astype(BF), rows_ref[:, feat:]).astype(out_ref.dtype)


SMEM = pl.BlockSpec(memory_space=pltpu.SMEM)
VMEM = pl.BlockSpec(memory_space=pltpu.VMEM)


def call(kernel, scalar, arrays, outs, flops):
    one = not isinstance(outs, (list, tuple))
    listed = [outs] if one else list(outs)
    nbytes = sum(a.size * a.dtype.itemsize for a in (*arrays, *listed))
    return pl.pallas_call(
        kernel,
        out_shape=outs,
        in_specs=([] if scalar is None else [SMEM]) + [VMEM] * len(arrays),
        out_specs=VMEM if one else [VMEM] * len(listed),
        cost_estimate=cost(flops, nbytes),
    )(*([] if scalar is None else [scalar]), *arrays)


def on_device(tokens, routes, gates, gate_weight, up_weight, down_weight, cotangent):
    owners = lax.axis_size("expert")
    replicas = lax.axis_size("dp")
    tok_rows, feat = tokens.shape
    top = routes.shape[1]
    hid = gate_weight.shape[2]
    pair_count = tok_rows * top
    capacity = max(2, pair_count * 5 // (4 * owners))
    half = owners // 2
    slot_count = half * capacity
    sds = jax.ShapeDtypeStruct

    across = [(i, (i + half) % owners) for i in range(owners)]
    groups = [list(range(half)), list(range(half, owners))]
    base = ((lax.axis_index("expert") // half) * slot_count).astype(jnp.int32).reshape(1)

    def send(rows):
        return lax.ppermute(rows, "expert", across)

    def exchange(rows):
        moved = lax.all_to_all(
            rows.reshape(half, capacity, 2 * feat),
            "expert",
            split_axis=0,
            concat_axis=0,
            tiled=True,
            axis_index_groups=groups,
        )
        return moved.reshape(slot_count, 2 * feat)

    far_tokens = send(tokens)
    far_cot = send(cotangent)
    plan = call(
        functools.partial(slots_kernel, owners, capacity),
        None,
        [routes.T, gates.T],
        sds((2 * top, tok_rows), F32),
        2 * owners * tok_rows * tok_rows,
    )
    far_plan = send(plan)
    far_gates = send(gates)

    own = [gate_weight[0], up_weight[0], down_weight[0]]
    share = own[0].shape[0]
    if replicas == 2:
        me = lax.axis_index("dp")
        swap = [(0, 1), (1, 0)]
        peer = [lax.ppermute(w, "dp", swap) for w in own]
        weights = [own[0], peer[0], own[1], peer[1], own[2], peer[2]]
        pieces = 2
        at = jnp.stack([me * share, (1 - me) * share]).astype(jnp.int32)
    else:
        weights = [lax.all_gather(w, "dp", axis=0, tiled=True) for w in own]
        pieces = 1
        at = jnp.zeros((1,), jnp.int32)
    width = feat // pieces

    wide = sds((slot_count, 2 * feat), BF)
    narrow = sds((slot_count, hid), BF)
    chunk = 64 if slot_count % 64 == 0 else slot_count
    work = 2 * slot_count * feat * hid

    def pick(plan_at, tokens_at, cot_at):
        return call(
            functools.partial(pick_kernel, chunk),
            base,
            [plan_at, tokens_at, cot_at],
            wide,
            4 * slot_count * tok_rows * feat,
        )

    def expert(rows):
        return call(
            functools.partial(expert_kernel, pieces),
            at,
            [rows, *weights],
            [wide, narrow, narrow, narrow],
            6 * work,
        )

    def combine(plan_at, gates_at, cot_at, rows, dtype):
        return call(
            combine_kernel,
            base,
            [plan_at, gates_at, cot_at, rows],
            [sds((tok_rows, 2 * feat), dtype), sds((tok_rows, top), F32)],
            2 * (top + 1) * slot_count * tok_rows * feat,
        )

    near_in = exchange(pick(plan, tokens, cotangent))
    far_rows = pick(far_plan, far_tokens, far_cot)
    near_in, far_rows = lax.optimization_barrier((near_in, far_rows))
    far_in = exchange(far_rows)
    near_out, *near_parts = expert(near_in)
    far_out, *far_parts = expert(far_in)
    far_back = exchange(far_out)
    near_out, far_back = lax.optimization_barrier((near_out, far_back))
    near_back = exchange(near_out)

    far_sum, far_gg = combine(far_plan, far_gates, far_cot, far_back, BF)
    got_sum = send(far_sum)
    got_gg = send(far_gg)

    def partial(p):
        return call(
            functools.partial(weights_kernel, 2),
            at[p : p + 1],
            [near_in, *near_parts, far_in, *far_parts],
            sds((3, width, hid), BF),
            6 * work // pieces,
        )

    if replicas == 2:
        got = lax.ppermute(partial(1), "dp", swap)
        kept = partial(0)
        grads = [kept[i].astype(F32) + got[i].astype(F32) for i in range(3)]
    else:
        got = lax.all_to_all(partial(0), "dp", split_axis=1, concat_axis=0, tiled=True)
        got = got.reshape(replicas, 3, share, hid).astype(F32)
        grads = [jnp.sum(got[:, i], axis=0) for i in range(3)]

    near_sum, near_gg = combine(plan, gates, cotangent, near_back, F32)
    total = (near_sum + got_sum.astype(F32)).astype(BF)
    mixed, token_grads = total[:, :feat], total[:, feat:]
    gate_grads = near_gg + got_gg
    return (mixed, token_grads, gate_grads, grads[0][None], grads[1][None], grads[2][None])


def solution(mesh):
    rows = P(("dp", "expert"), None)
    weight = P("expert", "dp", None)
    return jax.shard_map(
        on_device,
        mesh=mesh,
        in_specs=(rows, rows, rows, weight, weight, weight, rows),
        out_specs=(rows, rows, rows, weight, weight, weight),
        check_vma=False,
    )
```

time: 184 us -> 162 us (0.88)
  blocking collectives: 37.3 us -> 0 us
  starting transfers between devices: 24.9 us -> 33.8 us
  waiting for transfers between devices: 75.5 us -> 80 us
    all_to_all x1 -> x0, blocking collectives: 37.3 us -> none  [exchange(): lax.all_to_all(rows.reshape(owners, capacity, feat), 'expert', split_axis...]
    ppermute x1 -> x7, waiting for transfers between devices: 26.4 us -> 44 us  [the longest x6 39.2 us: send(): return lax.ppermute(rows, 'expert', across)]
    all_to_all x3 -> x4, waiting for transfers between devices: 24.8 us -> 11.8 us  [exchange(): lax.all_to_all(rows.reshape(half, capacity, 2 * feat), 'expert', split_ax...]
    ppermute x1 -> x7, starting transfers between devices: 1.55 us -> 10.6 us  [the longest x6 9.11 us: send(): return lax.ppermute(rows, 'expert', across)]
    unnamed x20 -> x42, local copies, waits for them, and re-layouts: 5.1 us -> 7.28 us
    pallas_call x8 -> x9, Pallas kernels: 34.9 us -> 34.1 us  [call(): pl.pallas_call(kernel, out_shape=outs, in_specs=([] if scalar is None els...]
    all_to_all x3 -> x4, starting transfers between devices: 19.8 us -> 19.6 us  [exchange(): lax.all_to_all(rows.reshape(half, capacity, 2 * feat), 'expert', split_ax...]
  transfers between devices with their start and end apart: 7 -> 14, of which waited for: 5 -> 8; matrix products, arithmetic and copies ran while one was open for 3% -> 3% of each run, Pallas kernels for 10% -> 15%
where the time goes in v2:
time: 162 us; the launch traced here: 161 us
  waiting for transfers between devices  80 us (49%)
  Pallas kernels  34.1 us (21%)
  starting transfers between devices  33.8 us (21%)
  local copies, waits for them, and re-layouts  8.11 us (5%)
  other arithmetic  4.69 us (3%)
    ppermute x6, waiting for transfers between devices, send(): return lax.ppermute(rows, 'expert', across)  39.2 us
    pallas_call x9, Pallas kernels, call(): pl.pallas_call(kernel, out_shape=outs, in_specs=([] if scalar is None els...  34.1 us
    ppermute x3, waiting for transfers between devices, on_device(): peer = [lax.ppermute(w, 'dp', swap) for w in own]  24.2 us
    all_to_all x4, starting transfers between devices, exchange(): lax.all_to_all(rows.reshape(half, capacity, 2 * feat), 'expert', split_ax...  19.6 us
    all_to_all x4, waiting for transfers between devices, exchange(): lax.all_to_all(rows.reshape(half, capacity, 2 * feat), 'expert', split_ax...  11.8 us
    ppermute x6, starting transfers between devices, send(): return lax.ppermute(rows, 'expert', across)  9.11 us
    unnamed x42, local copies, waits for them, and re-layouts  7.28 us
    ppermute x1, waiting for transfers between devices, on_device(): got = lax.ppermute(partial(1), 'dp', swap)  4.78 us
  transfers between devices with their start and end apart: 14, of which 8 were waited for; matrix products, arithmetic and copies ran while one was open for 3% of the time, Pallas kernels for 15%

profile of v2, /device:TPU:0, one launch (start us, length us, event | category | flops | bytes accessed | tf_op | source)
XLA Modules:
  0.0 161.5 jit_solution(16133904636758749957)
XLA Ops:
  2.1 2.6 %shard_map.119 = bf16[320,2048]{1,0:T(8,128)(2,1)} custom-call(s32[1]{0:T(128)} %bitcast.base_ref, f32[8,128]{1,0:T(8,128)} %shard_map.118.plan_ref, bf16[128,1024]{1,0:T(8,128)(2,1)} %tokens_ref.1, bf16[128,1024]{1,0:T(8,128)(2,1)} %cot_ref.3), custom_call_target="tpu_custom_call" | custom-call | flops 167772160 | bytes 1839104 | tf_op jit(solution)/shard_map/pallas_call | solution.py:141
  4.7 5.4 %all-to-all-start = ((bf16[8,40,2048]{2,1,0:T(8,128)(2,1)}), bf16[8,40,2048]{2,1,0:T(8,128)(2,1)S(1)}, u32[]{:S(2)}, u32[]{:S(2)}) async-start(bf16[8,40,2048]{2,1,0:T(8,128)(2,1)} %bitcast.25), calls=%async_computation | async-start | bytes 2621440 | tf_op jit(solution)/shard_map/all_to_all | solution.py:170
  10.1 2.7 %collective-permute-start.1 = (bf16[128,1024]{1,0:T(8,128)(2,1)S(1)}, bf16[128,1024]{1,0:T(8,128)(2,1)S(1)}, u32[]{:S(2)}, u32[]{:S(2)}) collective-permute-start(bf16[128,1024]{1,0:T(8,128)(2,1)S(1)} %copy-done.7), channel_id=1, source_target_pairs={{0,8},{1,9},{2,10},{3,11},{4,12},{5,13},{6,14},{7,15},{8,0},{9,1},... | collective-permute-start | bytes 786440 | tf_op jit(solution)/shard_map/ppermute | solution.py:167
  13.1 2.6 %collective-permute-start = (f32[8,128]{1,0:T(8,128)S(1)}, f32[8,128]{1,0:T(8,128)S(1)}, u32[]{:S(2)}, u32[]{:S(2)}) collective-permute-start(f32[8,128]{1,0:T(8,128)S(1)} %copy-done.11), channel_id=1, source_target_pairs={{0,8},{1,9},{2,10},{3,11},{4,12},{5,13},{6,14},{7,15},{8,0},{9,1},... | collective-permute-start | bytes 12296 | tf_op jit(solution)/shard_map/ppermute | solution.py:167
  15.7 20.9 %collective-permute-done.plan_ref = f32[8,128]{1,0:T(8,128)S(1)} collective-permute-done((f32[8,128]{1,0:T(8,128)S(1)}, f32[8,128]{1,0:T(8,128)S(1)}, u32[]{:S(2)}, u32[]{:S(2)}) %collective-permute-start) | collective-permute-done | bytes 4128 | tf_op jit(solution)/shard_map/ppermute | solution.py:167
  38.0 2.6 %shard_map.120 = bf16[320,2048]{1,0:T(8,128)(2,1)} custom-call(s32[1]{0:T(128)} %bitcast.base_ref, f32[8,128]{1,0:T(8,128)} %copy-done.12, bf16[128,1024]{1,0:T(8,128)(2,1)} %copy-done.8, bf16[128,1024]{1,0:T(8,128)(2,1)} %copy-done.5), custom_call_target="tpu_custom_call" | custom-call | flops 167772160 | bytes 1839104 | tf_op jit(solution)/shard_map/pallas_call | solution.py:141
  41.8 6.8 %all-to-all-start.1 = ((bf16[8,40,2048]{2,1,0:T(8,128)(2,1)}), bf16[8,40,2048]{2,1,0:T(8,128)(2,1)S(1)}, u32[]{:S(2)}, u32[]{:S(2)}) async-start(bf16[8,40,2048]{2,1,0:T(8,128)(2,1)} %bitcast.23), calls=%async_computation.1 | async-start | bytes 2621440 | tf_op jit(solution)/shard_map/all_to_all | solution.py:170
  52.8 7.8 %collective-permute-done.3.refs_1_ = bf16[512,384]{1,0:T(8,128)(2,1)S(1)} collective-permute-done((bf16[512,384]{1,0:T(8,128)(2,1)S(1)}, bf16[512,384]{1,0:T(8,128)(2,1)S(1)}, u32[]{:S(2)}, u32[]{:S(2)}) %collective-permute-start.3) | collective-permute-done | bytes 393248 | tf_op jit(solution)/shard_map/ppermute | solution.py:197
  60.6 8.4 %collective-permute-done.4.refs_3_ = bf16[512,384]{1,0:T(8,128)(2,1)S(1)} collective-permute-done((bf16[512,384]{1,0:T(8,128)(2,1)S(1)}, bf16[512,384]{1,0:T(8,128)(2,1)S(1)}, u32[]{:S(2)}, u32[]{:S(2)}) %collective-permute-start.4) | collective-permute-done | bytes 393248 | tf_op jit(solution)/shard_map/ppermute | solution.py:197
  69.0 8.0 %collective-permute-done.5.refs_5_ = bf16[512,384]{1,0:T(8,128)(2,1)S(1)} collective-permute-done((bf16[512,384]{1,0:T(8,128)(2,1)}, bf16[512,384]{1,0:T(8,128)(2,1)S(1)}, u32[]{:S(2)}, u32[]{:S(2)}) %collective-permute-start.5) | collective-permute-done | bytes 393248 | tf_op jit(solution)/shard_map/ppermute | solution.py:197
  78.2 5.5 %shard_map.122 = (bf16[320,2048]{1,0:T(8,128)(2,1)}, bf16[320,384]{1,0:T(8,128)(2,1)}, bf16[320,384]{1,0:T(8,128)(2,1)}, bf16[320,384]{1,0:T(8,128)(2,1)}) custom-call(s32[2]{0:T(128)} %pad_add_fusion.at_ref, bf16[320,2048]{1,0:T(8,128)(2,1)} %bitcast.19, bf16[512,384]{1,0:T(8,128)(2,1)} %bitcast.30, bf16[512,384]{1,0:T(8,128)(2,1)} %copy-done.16, ...), custom_call_target="tpu_custom_call" | custom-call | flops 1509949440 | bytes 5718016 | tf_op jit(solution)/shard_map/pallas_call | solution.py:141
  83.7 3.8 %all-to-all-start.2 = ((bf16[8,40,2048]{2,1,0:T(8,128)(2,1)}), bf16[8,40,2048]{2,1,0:T(8,128)(2,1)S(1)}, u32[]{:S(2)}, u32[]{:S(2)}) async-start(bf16[8,40,2048]{2,1,0:T(8,128)(2,1)} %bitcast.27), calls=%async_computation.2 | async-start | bytes 2621440 | tf_op jit(solution)/shard_map/all_to_all | solution.py:170
  87.5 5.5 %shard_map.121 = (bf16[320,2048]{1,0:T(8,128)(2,1)}, bf16[320,384]{1,0:T(8,128)(2,1)}, bf16[320,384]{1,0:T(8,128)(2,1)}, bf16[320,384]{1,0:T(8,128)(2,1)}) custom-call(s32[2]{0:T(128)} %pad_add_fusion.at_ref, bf16[320,2048]{1,0:T(8,128)(2,1)} %bitcast.16, bf16[512,384]{1,0:T(8,128)(2,1)} %bitcast.31, bf16[512,384]{1,0:T(8,128)(2,1)} %copy-done.16, ...), custom_call_target="tpu_custom_call" | custom-call | flops 1509949440 | bytes 5718016 | tf_op jit(solution)/shard_map/pallas_call | solution.py:141
  92.9 11.8 %all-to-all-done.2 = bf16[8,40,2048]{2,1,0:T(8,128)(2,1)S(1)} async-done(((bf16[8,40,2048]{2,1,0:T(8,128)(2,1)}), bf16[8,40,2048]{2,1,0:T(8,128)(2,1)S(1)}, u32[]{:S(2)}, u32[]{:S(2)}) %all-to-all-start.2) | async-done | bytes 1310752 | tf_op jit(solution)/shard_map/all_to_all | solution.py:170
  105.9 3.6 %all-to-all-start.3 = ((bf16[8,40,2048]{2,1,0:T(8,128)(2,1)}), bf16[8,40,2048]{2,1,0:T(8,128)(2,1)S(1)}, u32[]{:S(2)}, u32[]{:S(2)}) async-start(bf16[8,40,2048]{2,1,0:T(8,128)(2,1)} %bitcast.26), calls=%async_computation.3 | async-start | bytes 2621440 | tf_op jit(solution)/shard_map/all_to_all | solution.py:170
  109.4 4.9 %shard_map.126 = bf16[3,512,384]{2,1,0:T(8,128)(2,1)} custom-call(s32[1]{0:T(128)} %bitcast.4.at_ref, bf16[320,2048]{1,0:T(8,128)(2,1)} %bitcast.17, bf16[320,384]{1,0:T(8,128)(2,1)} %get-tuple-element.32.refs_1_, bf16[320,384]{1,0:T(8,128)(2,1)} %get-tuple-element.33.refs_2_, bf16[320,384]{1,0:T(8,128)(2,1)} %get-tuple-element.34.refs_3_, ...), custom_call_target="tpu_custom_call" | custom-call | flops 754974720 | bytes 5275648 | tf_op jit(solution)/shard_map/pallas_call | solution.py:141
  116.1 9.8 %collective-permute-done.6.gates_ref = f32[128,4]{1,0:T(8,128)S(1)} collective-permute-done((f32[128,4]{1,0:T(8,128)S(1)}, f32[128,4]{1,0:T(8,128)S(1)}, u32[]{:S(2)}, u32[]{:S(2)}) %collective-permute-start.6) | collective-permute-done | bytes 2080 | tf_op jit(solution)/shard_map/ppermute | solution.py:167
  126.6 3.2 %shard_map.124 = (bf16[128,2048]{1,0:T(8,128)(2,1)}, f32[128,4]{1,0:T(8,128)}) custom-call(s32[1]{0:T(128)} %bitcast.base_ref, f32[8,128]{1,0:T(8,128)} %copy-done.12, f32[128,4]{1,0:T(8,128)} %copy-done.10, bf16[128,1024]{1,0:T(8,128)(2,1)} %copy-done.5, bf16[320,2048]{1,0:T(8,128)(2,1)} %bitcast.24), custom_call_target="tpu_custom_call" | custom-call | flops 419430400 | bytes 2105344 | tf_op jit(solution)/shard_map/pallas_call | solution.py:141
  129.8 3.4 %collective-permute-start.7 = (bf16[128,2048]{1,0:T(8,128)(2,1)}, bf16[128,2048]{1,0:T(8,128)(2,1)S(1)}, u32[]{:S(2)}, u32[]{:S(2)}) collective-permute-start(bf16[128,2048]{1,0:T(8,128)(2,1)} %get-tuple-element.29), channel_id=1, source_target_pairs={{0,8},{1,9},{2,10},{3,11},{4,12},{5,13},{6,14},{7,15},{8,0},{9,1},... | collective-permute-start | bytes 1572872 | tf_op jit(solution)/shard_map/ppermute | solution.py:167
  133.1 5.0 %shard_map.125 = bf16[3,512,384]{2,1,0:T(8,128)(2,1)} custom-call(s32[1]{0:T(128)} %bitcast.3.at_ref, bf16[320,2048]{1,0:T(8,128)(2,1)} %bitcast.18, bf16[320,384]{1,0:T(8,128)(2,1)} %get-tuple-element.32.refs_1_, bf16[320,384]{1,0:T(8,128)(2,1)} %get-tuple-element.33.refs_2_, bf16[320,384]{1,0:T(8,128)(2,1)} %get-tuple-element.34.refs_3_, ...), custom_call_target="tpu_custom_call" | custom-call | flops 754974720 | bytes 5275648 | tf_op jit(solution)/shard_map/pallas_call | solution.py:141
  138.1 4.8 %collective-permute-done.9 = bf16[3,512,384]{2,1,0:T(8,128)(2,1)S(1)} collective-permute-done((bf16[3,512,384]{2,1,0:T(8,128)(2,1)}, bf16[3,512,384]{2,1,0:T(8,128)(2,1)S(1)}, u32[]{:S(2)}, u32[]{:S(2)}) %collective-permute-start.9) | collective-permute-done | bytes 1179680 | tf_op jit(solution)/shard_map/ppermute | solution.py:263
  142.9 2.7 %convert_add_fusion = (f32[1,512,384]{2,1,0:T(8,128)}, f32[1,512,384]{2,1,0:T(8,128)}, f32[1,512,384]{2,1,0:T(8,128)}) fusion(bf16[3,512,384]{2,1,0:T(8,128)(2,1)S(1)} %collective-permute-done.9, bf16[3,512,384]{2,1,0:T(8,128)(2,1)} %shard_map.125), kind=kLoop, calls=%fused_computation.1 | loop fusion | flops 1769472 | bytes 4718592 | tf_op jit(solution)/shard_map/add | solution.py:265
  146.8 3.4 %shard_map.123 = (f32[128,2048]{1,0:T(8,128)}, f32[128,4]{1,0:T(8,128)}) custom-call(s32[1]{0:T(128)} %bitcast.base_ref, f32[8,128]{1,0:T(8,128)} %shard_map.118.plan_ref, f32[128,4]{1,0:T(8,128)} %copy-done.6, bf16[128,1024]{1,0:T(8,128)(2,1)} %cot_ref.3, bf16[320,2048]{1,0:T(8,128)(2,1)} %bitcast.22), custom_call_target="tpu_custom_call" | custom-call | flops 419430400 | bytes 2629632 | tf_op jit(solution)/shard_map/pallas_call | solution.py:141
  150.2 8.5 %collective-permute-done.7 = bf16[128,2048]{1,0:T(8,128)(2,1)S(1)} collective-permute-done((bf16[128,2048]{1,0:T(8,128)(2,1)}, bf16[128,2048]{1,0:T(8,128)(2,1)S(1)}, u32[]{:S(2)}, u32[]{:S(2)}) %collective-permute-start.7) | collective-permute-done | bytes 524320 | tf_op jit(solution)/shard_map/ppermute | solution.py:167
  (60 shorter events, 17.1 us)
Async XLA Ops:
  4.7 5.4 %copy-start.7 = (bf16[128,1024]{1,0:T(8,128)(2,1)S(1)}, bf16[128,1024]{1,0:T(8,128)(2,1)}, u32[]{:S(2)}) copy-start(bf16[128,1024]{1,0:T(8,128)(2,1)} %tokens_ref.1) | copy-start | bytes 786436
  4.7 8.1 %copy-start.4 = (bf16[128,1024]{1,0:T(8,128)(2,1)S(1)}, bf16[128,1024]{1,0:T(8,128)(2,1)}, u32[]{:S(2)}) copy-start(bf16[128,1024]{1,0:T(8,128)(2,1)} %cot_ref.3) | copy-start | bytes 786436
  4.7 8.4 %copy-start.11 = (f32[8,128]{1,0:T(8,128)S(1)}, f32[8,128]{1,0:T(8,128)}, u32[]{:S(2)}) copy-start(f32[8,128]{1,0:T(8,128)} %shard_map.118.plan_ref) | copy-start | bytes 12292
  4.7 35.9 %all-to-all-start = ((bf16[8,40,2048]{2,1,0:T(8,128)(2,1)}), bf16[8,40,2048]{2,1,0:T(8,128)(2,1)S(1)}, u32[]{:S(2)}, u32[]{:S(2)}) async-start(bf16[8,40,2048]{2,1,0:T(8,128)(2,1)} %bitcast.25), calls=%async_computation | async-start | bytes 2621440 | tf_op jit(solution)/shard_map/all_to_all | solution.py:170
  10.1 26.5 %collective-permute-start.1 = (bf16[128,1024]{1,0:T(8,128)(2,1)S(1)}, bf16[128,1024]{1,0:T(8,128)(2,1)S(1)}, u32[]{:S(2)}, u32[]{:S(2)}) collective-permute-start(bf16[128,1024]{1,0:T(8,128)(2,1)S(1)} %copy-done.7), channel_id=1, source_target_pairs={{0,8},{1,9},{2,10},{3,11},{4,12},{5,13},{6,14},{7,15},{8,0},{9,1},... | collective-permute-start | bytes 786440 | tf_op jit(solution)/shard_map/ppermute | solution.py:167
  12.8 23.9 %collective-permute-start.2 = (bf16[128,1024]{1,0:T(8,128)(2,1)S(1)}, bf16[128,1024]{1,0:T(8,128)(2,1)S(1)}, u32[]{:S(2)}, u32[]{:S(2)}) collective-permute-start(bf16[128,1024]{1,0:T(8,128)(2,1)S(1)} %copy-done.4), channel_id=1, source_target_pairs={{0,8},{1,9},{2,10},{3,11},{4,12},{5,13},{6,14},{7,15},{8,0},{9,1},... | collective-permute-start | bytes 786440 | tf_op jit(solution)/shard_map/ppermute | solution.py:167
  13.1 23.5 %collective-permute-start = (f32[8,128]{1,0:T(8,128)S(1)}, f32[8,128]{1,0:T(8,128)S(1)}, u32[]{:S(2)}, u32[]{:S(2)}) collective-permute-start(f32[8,128]{1,0:T(8,128)S(1)} %copy-done.11), channel_id=1, source_target_pairs={{0,8},{1,9},{2,10},{3,11},{4,12},{5,13},{6,14},{7,15},{8,0},{9,1},... | collective-permute-start | bytes 12296 | tf_op jit(solution)/shard_map/ppermute | solution.py:167
  40.7 8.0 %copy-start.14 = (bf16[1,512,384]{2,1,0:T(8,128)(2,1)S(1)}, bf16[1,512,384]{2,1,0:T(8,128)(2,1)}, u32[]{:S(2)}) copy-start(bf16[1,512,384]{2,1,0:T(8,128)(2,1)} %param.10) | copy-start | bytes 1179652
  40.7 9.5 %copy-start.15 = (bf16[1,512,384]{2,1,0:T(8,128)(2,1)S(1)}, bf16[1,512,384]{2,1,0:T(8,128)(2,1)}, u32[]{:S(2)}) copy-start(bf16[1,512,384]{2,1,0:T(8,128)(2,1)} %param.11) | copy-start | bytes 1179652
  41.8 35.2 %all-to-all-start.1 = ((bf16[8,40,2048]{2,1,0:T(8,128)(2,1)}), bf16[8,40,2048]{2,1,0:T(8,128)(2,1)S(1)}, u32[]{:S(2)}, u32[]{:S(2)}) async-start(bf16[8,40,2048]{2,1,0:T(8,128)(2,1)} %bitcast.23), calls=%async_computation.1 | async-start | bytes 2621440 | tf_op jit(solution)/shard_map/all_to_all | solution.py:170
  48.6 12.0 %collective-permute-start.3 = (bf16[512,384]{1,0:T(8,128)(2,1)S(1)}, bf16[512,384]{1,0:T(8,128)(2,1)S(1)}, u32[]{:S(2)}, u32[]{:S(2)}) collective-permute-start(bf16[512,384]{1,0:T(8,128)(2,1)S(1)} %bitcast.32), channel_id=1, source_target_pairs={{0,16},{16,0},{1,17},{17,1},{2,18},{18,2},{3,19},{19,3},{4,20},{20... | collective-permute-start | bytes 1179656 | tf_op jit(solution)/shard_map/ppermute | solution.py:197
  50.2 18.9 %collective-permute-start.4 = (bf16[512,384]{1,0:T(8,128)(2,1)S(1)}, bf16[512,384]{1,0:T(8,128)(2,1)S(1)}, u32[]{:S(2)}, u32[]{:S(2)}) collective-permute-start(bf16[512,384]{1,0:T(8,128)(2,1)S(1)} %bitcast.35), channel_id=1, source_target_pairs={{0,16},{16,0},{1,17},{17,1},{2,18},{18,2},{3,19},{19,3},{4,20},{20... | collective-permute-start | bytes 1179656 | tf_op jit(solution)/shard_map/ppermute | solution.py:197
  50.7 26.3 %collective-permute-start.5 = (bf16[512,384]{1,0:T(8,128)(2,1)}, bf16[512,384]{1,0:T(8,128)(2,1)S(1)}, u32[]{:S(2)}, u32[]{:S(2)}) collective-permute-start(bf16[512,384]{1,0:T(8,128)(2,1)} %bitcast.36), channel_id=1, source_target_pairs={{0,16},{16,0},{1,17},{17,1},{2,18},{18,2},{3,19},{19,3},{4,20},{20... | collective-permute-start | bytes 1179656 | tf_op jit(solution)/shard_map/ppermute | solution.py:197
  60.6 16.4 %copy-start.16 = (bf16[512,384]{1,0:T(8,128)(2,1)}, bf16[512,384]{1,0:T(8,128)(2,1)S(1)}, u32[]{:S(2)}) copy-start(bf16[512,384]{1,0:T(8,128)(2,1)S(1)} %collective-permute-done.3.refs_1_) | copy-start | bytes 1179652
  69.0 8.0 %copy-start.17 = (bf16[512,384]{1,0:T(8,128)(2,1)}, bf16[512,384]{1,0:T(8,128)(2,1)S(1)}, u32[]{:S(2)}) copy-start(bf16[512,384]{1,0:T(8,128)(2,1)S(1)} %collective-permute-done.4.refs_3_) | copy-start | bytes 1179652
  83.7 21.1 %all-to-all-start.2 = ((bf16[8,40,2048]{2,1,0:T(8,128)(2,1)}), bf16[8,40,2048]{2,1,0:T(8,128)(2,1)S(1)}, u32[]{:S(2)}, u32[]{:S(2)}) async-start(bf16[8,40,2048]{2,1,0:T(8,128)(2,1)} %bitcast.27), calls=%async_computation.2 | async-start | bytes 2621440 | tf_op jit(solution)/shard_map/all_to_all | solution.py:170
  105.9 39.8 %all-to-all-start.3 = ((bf16[8,40,2048]{2,1,0:T(8,128)(2,1)}), bf16[8,40,2048]{2,1,0:T(8,128)(2,1)S(1)}, u32[]{:S(2)}, u32[]{:S(2)}) async-start(bf16[8,40,2048]{2,1,0:T(8,128)(2,1)} %bitcast.26), calls=%async_computation.3 | async-start | bytes 2621440 | tf_op jit(solution)/shard_map/all_to_all | solution.py:170
  109.4 6.4 %copy-start.13 = (f32[128,4]{0,1:T(4,128)S(1)}, f32[128,4]{0,1:T(4,128)}, u32[]{:S(2)}) copy-start(f32[128,4]{0,1:T(4,128)} %param.9) | copy-start | bytes 6148
  114.4 28.5 %collective-permute-start.9 = (bf16[3,512,384]{2,1,0:T(8,128)(2,1)}, bf16[3,512,384]{2,1,0:T(8,128)(2,1)S(1)}, u32[]{:S(2)}, u32[]{:S(2)}) collective-permute-start(bf16[3,512,384]{2,1,0:T(8,128)(2,1)} %shard_map.126), channel_id=1, source_target_pairs={{0,16},{16,0},{1,17},{17,1},{2,18},{18,2},{3,19},{19,3},{4,20},{20... | collective-permute-start | bytes 3538952 | tf_op jit(solution)/shard_map/ppermute | solution.py:263
  116.0 22.1 %copy-start.6 = (f32[128,4]{1,0:T(8,128)}, f32[128,4]{1,0:T(8,128)S(1)}, u32[]{:S(2)}) copy-start(f32[128,4]{1,0:T(8,128)S(1)} %copy.13.gates_ref) | copy-start | bytes 6148
  116.0 9.9 %collective-permute-start.6 = (f32[128,4]{1,0:T(8,128)S(1)}, f32[128,4]{1,0:T(8,128)S(1)}, u32[]{:S(2)}, u32[]{:S(2)}) collective-permute-start(f32[128,4]{1,0:T(8,128)S(1)} %copy.13.gates_ref), channel_id=1, source_target_pairs={{0,8},{1,9},{2,10},{3,11},{4,12},{5,13},{6,14},{7,15},{8,0},{9,1},... | collective-permute-start | bytes 6152 | tf_op jit(solution)/shard_map/ppermute | solution.py:167
  129.8 28.9 %collective-permute-start.7 = (bf16[128,2048]{1,0:T(8,128)(2,1)}, bf16[128,2048]{1,0:T(8,128)(2,1)S(1)}, u32[]{:S(2)}, u32[]{:S(2)}) collective-permute-start(bf16[128,2048]{1,0:T(8,128)(2,1)} %get-tuple-element.29), channel_id=1, source_target_pairs={{0,8},{1,9},{2,10},{3,11},{4,12},{5,13},{6,14},{7,15},{8,0},{9,1},... | collective-permute-start | bytes 1572872 | tf_op jit(solution)/shard_map/ppermute | solution.py:167
  138.1 7.5 %copy-start.19 = (f32[128,4]{1,0:T(8,128)S(1)}, f32[128,4]{1,0:T(8,128)}, u32[]{:S(2)}) copy-start(f32[128,4]{1,0:T(8,128)} %get-tuple-element.31) | copy-start | bytes 6148
  145.6 15.2 %collective-permute-start.8 = (f32[128,4]{1,0:T(8,128)S(1)}, f32[128,4]{1,0:T(8,128)S(1)}, u32[]{:S(2)}, u32[]{:S(2)}) collective-permute-start(f32[128,4]{1,0:T(8,128)S(1)} %copy-done.19), channel_id=1, source_target_pairs={{0,8},{1,9},{2,10},{3,11},{4,12},{5,13},{6,14},{7,15},{8,0},{9,1},... | collective-permute-start | bytes 6152 | tf_op jit(solution)/shard_map/ppermute | solution.py:167
  (10 other events, 10.0 us)

commit v3 on v2

v3 whole, which is shorter than its diff:
```python
import functools

import jax
import jax.numpy as jnp
from jax import lax
from jax.experimental import pallas as pl
from jax.experimental.pallas import tpu as pltpu
from jax.sharding import PartitionSpec as P

BF = jnp.bfloat16
F32 = jnp.float32
STRETCH = 12
NEAR = 0


def dot(left, right):
    return jnp.dot(left, right, preferred_element_type=F32)


def dot_rows(left, right):
    return lax.dot_general(left, right, (((0,), (0,)), ((), ())), preferred_element_type=F32)


def dot_last(left, right):
    return lax.dot_general(left, right, (((1,), (1,)), ((), ())), preferred_element_type=F32)


def cost(flops, nbytes):
    return pl.CostEstimate(flops=flops, bytes_accessed=nbytes, transcendentals=0)


def slots_in(owners, capacity, routes):
    top, rows = routes.shape
    expert = lax.broadcasted_iota(jnp.int32, (owners, rows), 0)
    named = [(routes[k : k + 1, :] == expert).astype(F32) for k in range(top)]
    onehot = sum(named)
    before = lax.broadcasted_iota(jnp.int32, (rows, rows), 0) < lax.broadcasted_iota(
        jnp.int32, (rows, rows), 1
    )
    position = dot(onehot.astype(BF), before.astype(F32).astype(BF)).astype(jnp.int32)
    return [
        routes[k : k + 1, :] * capacity
        + jnp.sum(jnp.where(routes[k : k + 1, :] == expert, position, 0), axis=0, keepdims=True)
        for k in range(top)
    ]


def pick_kernel(owners, capacity, packed, starts_ref, *refs):
    if packed:
        facts_ref, tokens_ref, cot_ref, *outs = refs
        top = facts_ref.shape[0] // 2
        routes = facts_ref[0:top, :].astype(jnp.int32)
        gates = facts_ref[top : 2 * top, :]
    else:
        routes_ref, gates_ref, tokens_ref, cot_ref, *outs = refs
        top = routes_ref.shape[0]
        routes, gates = routes_ref[...], gates_ref[...]
    *outs, plan_ref = outs
    slots = slots_in(owners, capacity, routes)
    for k in range(top):
        plan_ref[k : k + 1, :] = slots[k].astype(F32)
    plan_ref[top : 2 * top, :] = gates
    feat = tokens_ref.shape[1]
    for b, out_ref in enumerate(outs):
        rows = out_ref.shape[0]
        at = lax.broadcasted_iota(jnp.int32, (rows, slots[0].shape[1]), 0) + starts_ref[b]
        hits = [slot == at for slot in slots]
        weight = sum(
            jnp.where(hit, gates[k : k + 1, :], 0.0) for k, hit in enumerate(hits)
        )
        gate = jnp.sum(weight, axis=1, keepdims=True)
        picked = sum(hit.astype(F32) for hit in hits).astype(BF)
        out_ref[:, :feat] = dot(picked, tokens_ref[...]).astype(BF)
        out_ref[:, feat:] = (gate * dot(picked, cot_ref[...])).astype(BF)


def joined(refs, columns):
    if len(refs) == 1:
        return refs[0][:, columns]
    return jnp.concatenate([ref[:, columns] for ref in refs], axis=0)


def store_rows(at_ref, first, out_ref, columns, value):
    if len(out_ref.shape) == 2:
        out_ref[:, columns] = value
        return
    count, rows = out_ref.shape[:2]
    for b in range(count):
        out_ref[at_ref[first + b], :, columns] = value[b * rows : (b + 1) * rows]


def expert_kernel(pieces, blocks, at_ref, *refs):
    ins, weights = refs[:blocks], refs[blocks : blocks + 3 * pieces]
    out_ref, d_gate_ref, d_up_ref, hidden_ref = refs[blocks + 3 * pieces :]
    feat = ins[0].shape[1] // 2
    width = feat // pieces

    def cols(p, offset):
        return pl.ds(pl.multiple_of(at_ref[p] + offset, 128), width)

    pre_gate = pre_up = grad = 0.0
    for p in range(pieces):
        part = joined(ins, cols(p, 0))
        pre_gate = pre_gate + dot(part, weights[p][...])
        pre_up = pre_up + dot(part, weights[pieces + p][...])
    sig = 1.0 / (1.0 + jnp.exp(-pre_gate))
    hidden = (pre_gate * sig * pre_up).astype(BF)
    hidden_ref[...] = hidden
    for p in range(pieces):
        down = weights[2 * pieces + p][...]
        store_rows(at_ref, pieces, out_ref, cols(p, 0), dot_last(hidden, down).astype(BF))
        grad = grad + dot(joined(ins, cols(p, feat)), down)
    d_gate = (grad * pre_up * sig * (1.0 + pre_gate * (1.0 - sig))).astype(BF)
    d_up = (grad * pre_gate * sig).astype(BF)
    d_gate_ref[...] = d_gate
    d_up_ref[...] = d_up
    for p in range(pieces):
        back = dot_last(d_gate, weights[p][...]) + dot_last(d_up, weights[pieces + p][...])
        store_rows(at_ref, pieces, out_ref, cols(p, feat), back.astype(BF))


def weights_kernel(blocks, at_ref, *refs):
    ins, out_ref = refs[:-1], refs[-1]
    width = out_ref.shape[1]
    feat = ins[0].shape[1] // 2
    sums = [0.0, 0.0, 0.0]
    for count in blocks:
        part, ins = ins[: count + 3], ins[count + 3 :]
        rows, (d_gate, d_up, hidden) = part[:count], part[count:]
        x = joined(rows, pl.ds(pl.multiple_of(at_ref[0], 128), width))
        g = joined(rows, pl.ds(pl.multiple_of(at_ref[0] + feat, 128), width))
        sums[0] = sums[0] + dot_rows(x, d_gate[...])
        sums[1] = sums[1] + dot_rows(x, d_up[...])
        sums[2] = sums[2] + dot_rows(g, hidden[...])
    for i in range(3):
        out_ref[i] = sums[i].astype(BF)


def combine_kernel(blocks, starts_ref, plan_ref, cot_ref, *refs):
    ins, (out_ref, grads_ref) = refs[:blocks], refs[blocks:]
    top = plan_ref.shape[0] // 2
    slots = plan_ref[0:top, :].astype(jnp.int32)
    gates = jnp.transpose(plan_ref[...])
    feat = cot_ref.shape[1]
    rows = joined(ins, slice(0, feat))
    cot = cot_ref[...].astype(F32)
    shape = (ins[0].shape[0], slots.shape[1])
    at = [lax.broadcasted_iota(jnp.int32, shape, 0) + starts_ref[b] for b in range(blocks)]
    at = at[0] if blocks == 1 else jnp.concatenate(at, axis=0)
    total, every = 0.0, 0.0
    for k in range(top):
        picked = (slots[k : k + 1, :] == at).astype(F32)
        every = every + picked
        row = dot_rows(picked.astype(BF), rows)
        total = total + gates[:, top + k : top + k + 1] * row
        grads_ref[:, k : k + 1] = jnp.sum(cot * row, axis=1, keepdims=True)
    out_ref[:, :feat] = total.astype(out_ref.dtype)
    back = dot_rows(every.astype(BF), joined(ins, slice(feat, 2 * feat)))
    out_ref[:, feat:] = back.astype(out_ref.dtype)


def finish_kernel(near_ref, far_ref, near_gg_ref, far_gg_ref, mixed_ref, grads_ref, gg_ref):
    feat = mixed_ref.shape[1]
    mixed_ref[...] = (near_ref[:, :feat] + far_ref[:, :feat].astype(F32)).astype(BF)
    grads_ref[...] = (near_ref[:, feat:] + far_ref[:, feat:].astype(F32)).astype(BF)
    gg_ref[...] = near_gg_ref[...] + far_gg_ref[...]


SMEM = pl.BlockSpec(memory_space=pltpu.SMEM)
VMEM = pl.BlockSpec(memory_space=pltpu.VMEM)


def call(kernel, scalar, arrays, outs, flops):
    one = not isinstance(outs, (list, tuple))
    listed = [outs] if one else list(outs)
    nbytes = sum(a.size * a.dtype.itemsize for a in (*arrays, *listed)) if flops else 0
    return pl.pallas_call(
        kernel,
        out_shape=outs,
        in_specs=([] if scalar is None else [SMEM]) + [VMEM] * len(arrays),
        out_specs=VMEM if one else [VMEM] * len(listed),
        cost_estimate=cost(flops, nbytes),
    )(*([] if scalar is None else [scalar]), *arrays)


def on_device(tokens, routes, gates, gate_weight, up_weight, down_weight, cotangent):
    owners = lax.axis_size("expert")
    replicas = lax.axis_size("dp")
    tok_rows, feat = tokens.shape
    top = routes.shape[1]
    hid = gate_weight.shape[2]
    pair_count = tok_rows * top
    capacity = max(2, pair_count * 5 // (4 * owners))
    half = owners // 2
    slot_count = half * capacity
    sds = jax.ShapeDtypeStruct

    group = lax.axis_index("expert") // half
    member = lax.axis_index("expert") % half
    base = group * slot_count
    across = [(i, (i + half) % owners) for i in range(owners)]
    split = half <= 8 and half & (half - 1) == 0
    one_start = base.astype(jnp.int32).reshape(1)
    if split:
        starts = jnp.stack([base + (member ^ k) * capacity for k in range(half)])
        starts = starts.astype(jnp.int32)

    def send(rows):
        return lax.ppermute(rows, "expert", across)

    def exchange(parts):
        if len(parts) > 1:
            moved = [
                lax.ppermute(part, "expert", [(i, i ^ k) for i in range(owners)])
                for k, part in reversed(list(enumerate(parts)))
                if k
            ]
            return [parts[0], *reversed(moved)]
        moved = lax.all_to_all(
            parts[0].reshape(half, capacity, 2 * feat),
            "expert",
            split_axis=0,
            concat_axis=0,
            tiled=True,
            axis_index_groups=[list(range(half)), list(range(half, owners))],
        )
        return [moved.reshape(slot_count, 2 * feat)]

    far_facts = send(jnp.concatenate([routes.T.astype(F32), gates.T], axis=0))
    far_tokens = send(tokens)
    far_cot = send(cotangent)
    own = [gate_weight[0], up_weight[0], down_weight[0]]
    share = own[0].shape[0]
    if replicas == 2:
        me = lax.axis_index("dp")
        swap = [(0, 1), (1, 0)]
        peer = [lax.ppermute(w, "dp", swap) for w in own]
        far_tokens, far_cot, peer[0], peer[1] = lax.optimization_barrier(
            (far_tokens, far_cot, peer[0], peer[1])
        )
        weights = [own[0], peer[0], own[1], peer[1], own[2], peer[2]]
        pieces = 2
        at = jnp.stack([me * share, (1 - me) * share]).astype(jnp.int32)
    else:
        weights = [lax.all_gather(w, "dp", axis=0, tiled=True) for w in own]
        pieces = 1
        at = jnp.zeros((1,), jnp.int32)
    width = feat // pieces

    places = jnp.concatenate([at, (starts - base) // capacity]) if split else at
    whole_rows = [sds((slot_count, 2 * feat), BF)]
    split_rows = [sds((capacity, 2 * feat), BF)] * half if split else whole_rows
    narrow = sds((slot_count, hid), BF)
    work = 2 * slot_count * feat * hid

    def starts_of(rows):
        return starts if len(rows) > 1 else one_start

    def pick(facts, tokens_at, cot_at, rows):
        outs = call(
            functools.partial(pick_kernel, owners, capacity, len(facts) == 1),
            starts_of(rows),
            [*facts, tokens_at, cot_at],
            [*rows, sds((2 * top, tok_rows), F32)],
            4 * slot_count * tok_rows * feat,
        )
        return outs[:-1], outs[-1]

    def expert(rows, stretch):
        outs = call(
            functools.partial(expert_kernel, pieces, len(rows)),
            places,
            [*rows, *weights],
            [sds((half, *rows[0].shape) if len(rows) > 1 else rows[0].shape, BF)] + [narrow] * 3,
            6 * work * stretch,
        )
        return outs[:1], outs[1:]

    def combine(plan_at, cot_at, rows, dtype):
        return call(
            functools.partial(combine_kernel, len(rows)),
            starts_of(rows),
            [plan_at, cot_at, *rows],
            [sds((tok_rows, 2 * feat), dtype), sds((tok_rows, top), F32)],
            2 * (top + 1) * slot_count * tok_rows * feat,
        )

    near_rows, plan = pick((routes.T, gates.T), tokens, cotangent, whole_rows)
    near_in = exchange(near_rows)
    far_rows, far_plan = pick((far_facts,), far_tokens, far_cot, split_rows)
    far_in = exchange(far_rows)
    far_out, far_parts = expert(far_in, STRETCH)
    far_back = exchange(far_out)
    near_out, near_parts = expert(near_in, NEAR)

    def partial(p):
        return call(
            functools.partial(weights_kernel, (len(near_in), len(far_in))),
            at[p : p + 1],
            [*near_in, *near_parts, *far_in, *far_parts],
            sds((3, width, hid), BF),
            6 * work // pieces * NEAR,
        )

    leaving = partial(pieces - 1)
    far_back, leaving = lax.optimization_barrier((far_back, leaving))
    far_sum, far_gg = combine(far_plan, far_cot, far_back, BF)
    near_out, far_sum = lax.optimization_barrier((near_out, far_sum))
    near_back = exchange(near_out)
    got_sum = send(far_sum)
    got_gg = send(far_gg)

    if replicas == 2:
        got = lax.ppermute(leaving, "dp", swap)
        kept = partial(0)
        grads = [kept[i].astype(F32) + got[i].astype(F32) for i in range(3)]
    else:
        got = lax.all_to_all(leaving, "dp", split_axis=1, concat_axis=0, tiled=True)
        got = got.reshape(replicas, 3, share, hid).astype(F32)
        grads = [jnp.sum(got[:, i], axis=0) for i in range(3)]

    near_sum, near_gg = combine(plan, cotangent, near_back, F32)
    mixed, token_grads, gate_grads = call(
        finish_kernel,
        None,
        [near_sum, got_sum, near_gg, got_gg],
        [sds((tok_rows, feat), BF)] * 2 + [sds((tok_rows, top), F32)],
        2 * tok_rows * feat,
    )
    return (mixed, token_grads, gate_grads, grads[0][None], grads[1][None], grads[2][None])


def solution(mesh):
    rows = P(("dp", "expert"), None)
    weight = P("expert", "dp", None)
    return jax.shard_map(
        on_device,
        mesh=mesh,
        in_specs=(rows, rows, rows, weight, weight, weight, rows),
        out_specs=(rows, rows, rows, weight, weight, weight),
        check_vma=False,
    )
```

time: 162 us -> 133 us (0.82)
  waiting for transfers between devices: 80 us -> 51.7 us
    ppermute x1 -> x8, waiting for transfers between devices: 4.78 us -> 29.2 us  [the longest x1 18.8 us: on_device(): got = lax.ppermute(leaving, 'dp', swap)]
    ppermute x3, waiting for transfers between devices: 24.2 us -> 0.01 us  [on_device(): peer = [lax.ppermute(w, 'dp', swap) for w in own]]
    ppermute x6 -> x5, waiting for transfers between devices: 39.2 us -> 15.7 us  [send(): return lax.ppermute(rows, 'expert', across)]
    ppermute x1 -> x8, starting transfers between devices: 1.47 us -> 10.4 us  [the longest x7 8.89 us: exchange(): lax.ppermute(part, 'expert', [(i, i ^ k) for i in range(owners)])]
    all_to_all x4 -> x3, starting transfers between devices: 19.6 us -> 11.7 us  [exchange(): lax.all_to_all(parts[0].reshape(half, capacity, 2 * feat), 'expert', spli...]
    all_to_all x4 -> x3, waiting for transfers between devices: 11.8 us -> 6.75 us  [exchange(): lax.all_to_all(parts[0].reshape(half, capacity, 2 * feat), 'expert', spli...]
    ppermute x6 -> x5, starting transfers between devices: 9.11 us -> 6.01 us  [send(): return lax.ppermute(rows, 'expert', across)]
    unnamed x42 -> x45, local copies, waits for them, and re-layouts: 7.28 us -> 6.78 us
  transfers between devices with their start and end apart: 14 -> 19, of which waited for: 8 -> 9; matrix products, arithmetic and copies ran while one was open for 3% -> 4% of each run, Pallas kernels for 15% -> 23%
where the time goes in v3:
time: 133 us; the launch traced here: 132 us
  waiting for transfers between devices  51.7 us (39%)
  Pallas kernels  35.2 us (26%)
  starting transfers between devices  32.8 us (25%)
  local copies, waits for them, and re-layouts  7.46 us (6%)
  other arithmetic  4.39 us (3%)
    pallas_call x9, Pallas kernels, call(): pl.pallas_call(kernel, out_shape=outs, in_specs=([] if scalar is None els...  35.2 us
    ppermute x1, waiting for transfers between devices, on_device(): got = lax.ppermute(leaving, 'dp', swap)  18.8 us
    ppermute x5, waiting for transfers between devices, send(): return lax.ppermute(rows, 'expert', across)  15.7 us
    all_to_all x3, starting transfers between devices, exchange(): lax.all_to_all(parts[0].reshape(half, capacity, 2 * feat), 'expert', spli...  11.7 us
    ppermute x7, waiting for transfers between devices, exchange(): lax.ppermute(part, 'expert', [(i, i ^ k) for i in range(owners)])  10.4 us
    ppermute x7, starting transfers between devices, exchange(): lax.ppermute(part, 'expert', [(i, i ^ k) for i in range(owners)])  8.89 us
    unnamed x45, local copies, waits for them, and re-layouts  6.78 us
    all_to_all x3, waiting for transfers between devices, exchange(): lax.all_to_all(parts[0].reshape(half, capacity, 2 * feat), 'expert', spli...  6.75 us
  transfers between devices with their start and end apart: 19, of which 9 were waited for; matrix products, arithmetic and copies ran while one was open for 4% of the time, Pallas kernels for 23%

profile of v3, /device:TPU:0, one launch (start us, length us, event | category | flops | bytes accessed | tf_op | source)
XLA Modules:
  0.0 132.4 jit_solution(9129832524267709741)
XLA Ops:
  0.6 3.0 %collective-permute-start.2 = (bf16[512,384]{1,0:T(8,128)(2,1)}, bf16[512,384]{1,0:T(8,128)(2,1)S(1)}, u32[]{:S(2)}, u32[]{:S(2)}) collective-permute-start(bf16[512,384]{1,0:T(8,128)(2,1)} %bitcast.29), channel_id=1, source_target_pairs={{0,16},{16,0},{1,17},{17,1},{2,18},{18,2},{3,19},{19,3},{4,20},{20... | collective-permute-start | bytes 1179656 | tf_op jit(solution)/shard_map/ppermute | solution.py:237
  3.7 3.0 %collective-permute-start = (bf16[128,1024]{1,0:T(8,128)(2,1)}, bf16[128,1024]{1,0:T(8,128)(2,1)S(1)}, u32[]{:S(2)}, u32[]{:S(2)}) collective-permute-start(bf16[128,1024]{1,0:T(8,128)(2,1)} %refs_2_.1), channel_id=1, source_target_pairs={{0,8},{1,9},{2,10},{3,11},{4,12},{5,13},{6,14},{7,15},{8,0},{9,1},... | collective-permute-start | bytes 786440 | tf_op jit(solution)/shard_map/ppermute | solution.py:209
  6.8 2.8 %shard_map.118 = (bf16[320,2048]{1,0:T(8,128)(2,1)}, f32[8,128]{1,0:T(8,128)}) custom-call(s32[1]{0:T(128)} %bitcast.starts_ref, s32[4,128]{1,0:T(4,128)} %bitcast.38, f32[4,128]{1,0:T(4,128)} %bitcast.39, bf16[128,1024]{1,0:T(8,128)(2,1)} %refs_2_.1, bf16[128,1024]{1,0:T(8,128)(2,1)} %cot_ref.1), custom_call_target="tpu_custom_call" | custom-call | flops 167772160 | bytes 1843200 | tf_op jit(solution)/shard_map/pallas_call | solution.py:177
  9.6 4.3 %all-to-all-start = ((bf16[8,40,2048]{2,1,0:T(8,128)(2,1)}), bf16[8,40,2048]{2,1,0:T(8,128)(2,1)S(1)}, u32[]{:S(2)}, u32[]{:S(2)}) async-start(bf16[8,40,2048]{2,1,0:T(8,128)(2,1)} %bitcast.27), calls=%async_computation | async-start | bytes 2621440 | tf_op jit(solution)/shard_map/all_to_all | solution.py:219
  15.5 9.8 %collective-permute-done.refs_1_ = bf16[128,1024]{1,0:T(8,128)(2,1)S(1)} collective-permute-done((bf16[128,1024]{1,0:T(8,128)(2,1)}, bf16[128,1024]{1,0:T(8,128)(2,1)S(1)}, u32[]{:S(2)}, u32[]{:S(2)}) %collective-permute-start) | collective-permute-done | bytes 262176 | tf_op jit(solution)/shard_map/ppermute | solution.py:209
  26.0 3.8 %collective-permute-done.1.refs_2_.cot_ref = bf16[128,1024]{1,0:T(8,128)(2,1)S(1)} collective-permute-done((bf16[128,1024]{1,0:T(8,128)(2,1)}, bf16[128,1024]{1,0:T(8,128)(2,1)S(1)}, u32[]{:S(2)}, u32[]{:S(2)}) %collective-permute-start.1) | collective-permute-done | bytes 262176 | tf_op jit(solution)/shard_map/ppermute | solution.py:209
  32.5 2.7 %shard_map.120 = (bf16[40,2048]{1,0:T(8,128)(2,1)}, bf16[40,2048]{1,0:T(8,128)(2,1)}, bf16[40,2048]{1,0:T(8,128)(2,1)}, bf16[40,2048]{1,0:T(8,128)(2,1)}, bf16[4...) custom-call(s32[8]{0:T(128)} %stack.43.starts_ref, ...), custom_call_target="tpu_custom_call" | custom-call | flops 167772160 | bytes 1843200 | tf_op jit(solution)/shard_map/pallas_call | solution.py:177
  37.0 2.3 %collective-permute-start.9 = (bf16[40,2048]{1,0:T(8,128)(2,1)}, bf16[40,2048]{1,0:T(8,128)(2,1)S(1)}, u32[]{:S(2)}, u32[]{:S(2)}) collective-permute-start(bf16[40,2048]{1,0:T(8,128)(2,1)} %get-tuple-element.52), channel_id=1, source_target_pairs={{0,4},{1,5},{2,6},{3,7},{4,0},{5,1},{6,2},{7,3},{8,12},{9,13},{10,... | collective-permute-start | bytes 491528 | tf_op jit(solution)/shard_map/ppermute | solution.py:214
  39.4 2.6 %collective-permute-start.11 = (bf16[40,2048]{1,0:T(8,128)(2,1)}, bf16[40,2048]{1,0:T(8,128)(2,1)S(1)}, u32[]{:S(2)}, u32[]{:S(2)}) collective-permute-start(bf16[40,2048]{1,0:T(8,128)(2,1)} %get-tuple-element.54), channel_id=1, source_target_pairs={{0,6},{1,7},{2,4},{3,5},{4,2},{5,3},{6,0},{7,1},{8,14},{9,15},{10,... | collective-permute-start | bytes 491528 | tf_op jit(solution)/shard_map/ppermute | solution.py:214
  47.9 5.4 %collective-permute-done.11.refs_6_.refs_10_ = bf16[40,2048]{1,0:T(8,128)(2,1)S(1)} collective-permute-done((bf16[40,2048]{1,0:T(8,128)(2,1)}, bf16[40,2048]{1,0:T(8,128)(2,1)S(1)}, u32[]{:S(2)}, u32[]{:S(2)}) %collective-permute-start.11) | collective-permute-done | bytes 163872 | tf_op jit(solution)/shard_map/ppermute | solution.py:214
  53.3 2.6 %collective-permute-done.12.refs_7_.refs_11_ = bf16[40,2048]{1,0:T(8,128)(2,1)S(1)} collective-permute-done((bf16[40,2048]{1,0:T(8,128)(2,1)}, bf16[40,2048]{1,0:T(8,128)(2,1)S(1)}, u32[]{:S(2)}, u32[]{:S(2)}) %collective-permute-start.12) | collective-permute-done | bytes 163872 | tf_op jit(solution)/shard_map/ppermute | solution.py:214
  56.5 5.6 %shard_map.121 = (bf16[8,40,2048]{2,1,0:T(8,128)(2,1)}, bf16[320,384]{1,0:T(8,128)(2,1)}, bf16[320,384]{1,0:T(8,128)(2,1)}, bf16[320,384]{1,0:T(8,128)(2,1)}) custom-call(s32[10]{0:T(128)} %pad_add_fusion.at_ref, bf16[40,2048]{1,0:T(8,128)(2,1)} %get-tuple-element.48.refs_0_.refs_4_, bf16[40,2048]{1,0:T(8,128)(2,1)} %copy-done.4, ...), custom_call_target="tpu_custom_call" | custom-call | flops 18119393280 | bytes 5718016 | tf_op jit(solution)/shard_map/pallas_call | solution.py:177
  63.1 3.6 %all-to-all-start.1 = ((bf16[8,40,2048]{2,1,0:T(8,128)(2,1)}), bf16[8,40,2048]{2,1,0:T(8,128)(2,1)S(1)}, u32[]{:S(2)}, u32[]{:S(2)}) async-start(bf16[8,40,2048]{2,1,0:T(8,128)(2,1)} %get-tuple-element.56), calls=%async_computation.1 | async-start | bytes 2621440 | tf_op jit(solution)/shard_map/all_to_all | solution.py:219
  66.7 5.5 %shard_map.119 = (bf16[320,2048]{1,0:T(8,128)(2,1)}, bf16[320,384]{1,0:T(8,128)(2,1)}, bf16[320,384]{1,0:T(8,128)(2,1)}, bf16[320,384]{1,0:T(8,128)(2,1)}) custom-call(s32[10]{0:T(128)} %pad_add_fusion.at_ref, bf16[320,2048]{1,0:T(8,128)(2,1)} %bitcast.22, bf16[512,384]{1,0:T(8,128)(2,1)} %bitcast.31, bf16[512,384]{1,0:T(8,128)(2,1)} %copy-done.13, ...), custom_call_target="tpu_custom_call" | custom-call | tf_op jit(solution)/shard_map/pallas_call | solution.py:177
  72.2 5.0 %shard_map.122 = bf16[3,512,384]{2,1,0:T(8,128)(2,1)} custom-call(s32[1]{0:T(128)} %bitcast.4.at_ref, bf16[320,2048]{1,0:T(8,128)(2,1)} %bitcast.23, bf16[320,384]{1,0:T(8,128)(2,1)} %get-tuple-element.57.refs_1_, bf16[320,384]{1,0:T(8,128)(2,1)} %get-tuple-element.58.refs_2_, bf16[320,384]{1,0:T(8,128)(2,1)} %get-tuple-element.59.refs_3_, ...), custom_call_target="tpu_custom_call" | custom-call | tf_op jit(solution)/shard_map/pallas_call | solution.py:177
  77.2 6.7 %all-to-all-done.1 = bf16[8,40,2048]{2,1,0:T(8,128)(2,1)S(1)} async-done(((bf16[8,40,2048]{2,1,0:T(8,128)(2,1)}), bf16[8,40,2048]{2,1,0:T(8,128)(2,1)S(1)}, u32[]{:S(2)}, u32[]{:S(2)}) %all-to-all-start.1) | async-done | bytes 1310752 | tf_op jit(solution)/shard_map/all_to_all | solution.py:219
  85.0 3.2 %shard_map.123 = (bf16[128,2048]{1,0:T(8,128)(2,1)}, f32[128,4]{1,0:T(8,128)}) custom-call(s32[1]{0:T(128)} %bitcast.starts_ref, f32[8,128]{1,0:T(8,128)} %get-tuple-element.47.plan_ref, bf16[128,1024]{1,0:T(8,128)(2,1)} %copy-done.15, bf16[320,2048]{1,0:T(8,128)(2,1)} %bitcast.26), custom_call_target="tpu_custom_call" | custom-call | flops 419430400 | bytes 2103296 | tf_op jit(solution)/shard_map/pallas_call | solution.py:177
  88.2 3.9 %all-to-all-start.2 = ((bf16[8,40,2048]{2,1,0:T(8,128)(2,1)}), bf16[8,40,2048]{2,1,0:T(8,128)(2,1)S(1)}, u32[]{:S(2)}, u32[]{:S(2)}) async-start(bf16[8,40,2048]{2,1,0:T(8,128)(2,1)} %bitcast.28), calls=%async_computation.2 | async-start | bytes 2621440 | tf_op jit(solution)/shard_map/all_to_all | solution.py:219
  93.6 2.3 %collective-permute-start.13 = (bf16[128,2048]{1,0:T(8,128)(2,1)}, bf16[128,2048]{1,0:T(8,128)(2,1)S(1)}, u32[]{:S(2)}, u32[]{:S(2)}) collective-permute-start(bf16[128,2048]{1,0:T(8,128)(2,1)} %get-tuple-element.67), channel_id=1, source_target_pairs={{0,8},{1,9},{2,10},{3,11},{4,12},{5,13},{6,14},{7,15},{8,0},{9,1},... | collective-permute-start | bytes 1572872 | tf_op jit(solution)/shard_map/ppermute | solution.py:209
  95.9 5.0 %shard_map.126 = bf16[3,512,384]{2,1,0:T(8,128)(2,1)} custom-call(s32[1]{0:T(128)} %bitcast.3.at_ref, bf16[320,2048]{1,0:T(8,128)(2,1)} %bitcast.24, bf16[320,384]{1,0:T(8,128)(2,1)} %get-tuple-element.57.refs_1_, bf16[320,384]{1,0:T(8,128)(2,1)} %get-tuple-element.58.refs_2_, bf16[320,384]{1,0:T(8,128)(2,1)} %get-tuple-element.59.refs_3_, ...), custom_call_target="tpu_custom_call" | custom-call | tf_op jit(solution)/shard_map/pallas_call | solution.py:177
  101.5 18.8 %collective-permute-done.15 = bf16[3,512,384]{2,1,0:T(8,128)(2,1)} collective-permute-done((bf16[3,512,384]{2,1,0:T(8,128)(2,1)S(1)}, bf16[3,512,384]{2,1,0:T(8,128)(2,1)}, u32[]{:S(2)}, u32[]{:S(2)}) %collective-permute-start.15) | collective-permute-done | bytes 1179680 | tf_op jit(solution)/shard_map/ppermute | solution.py:314
  120.3 3.1 %convert_add_fusion = (f32[1,512,384]{2,1,0:T(8,128)}, f32[1,512,384]{2,1,0:T(8,128)}, f32[1,512,384]{2,1,0:T(8,128)}) fusion(bf16[3,512,384]{2,1,0:T(8,128)(2,1)} %collective-permute-done.15, bf16[3,512,384]{2,1,0:T(8,128)(2,1)} %shard_map.126), kind=kLoop, calls=%fused_computation | loop fusion | flops 1769472 | bytes 4718592 | tf_op jit(solution)/shard_map/add | solution.py:316
  124.5 3.4 %shard_map.124 = (f32[128,2048]{1,0:T(8,128)}, f32[128,4]{1,0:T(8,128)}) custom-call(s32[1]{0:T(128)} %bitcast.starts_ref, f32[8,128]{1,0:T(8,128)} %get-tuple-element.40.plan_ref, bf16[128,1024]{1,0:T(8,128)(2,1)} %cot_ref.1, bf16[320,2048]{1,0:T(8,128)(2,1)} %bitcast.25), custom_call_target="tpu_custom_call" | custom-call | flops 419430400 | bytes 2627584 | tf_op jit(solution)/shard_map/pallas_call | solution.py:177
  128.7 2.2 %shard_map.125 = (bf16[128,1024]{1,0:T(8,128)(2,1)}, bf16[128,1024]{1,0:T(8,128)(2,1)}, f32[128,4]{1,0:T(8,128)}) custom-call(f32[128,2048]{1,0:T(8,128)} %get-tuple-element.66.near_ref, bf16[128,2048]{1,0:T(8,128)(2,1)} %copy-done.11, f32[128,4]{1,0:T(8,128)} %get-tuple-element.68.near_gg_ref, f32[128,4]{1,0:T(8,128)} %copy-done.16), custom_call_target="tpu_custom_call" | custom-call | flops 262144 | bytes 2103296 | tf_op jit(solution)/shard_map/pallas_call | solution.py:177
  (74 shorter events, 21.2 us)
Async XLA Ops:
  0.6 29.1 %collective-permute-start.2 = (bf16[512,384]{1,0:T(8,128)(2,1)}, bf16[512,384]{1,0:T(8,128)(2,1)S(1)}, u32[]{:S(2)}, u32[]{:S(2)}) collective-permute-start(bf16[512,384]{1,0:T(8,128)(2,1)} %bitcast.29), channel_id=1, source_target_pairs={{0,16},{16,0},{1,17},{17,1},{2,18},{18,2},{3,19},{19,3},{4,20},{20... | collective-permute-start | bytes 1179656 | tf_op jit(solution)/shard_map/ppermute | solution.py:237
  3.6 26.1 %collective-permute-start.3 = (bf16[512,384]{1,0:T(8,128)(2,1)}, bf16[512,384]{1,0:T(8,128)(2,1)S(1)}, u32[]{:S(2)}, u32[]{:S(2)}) collective-permute-start(bf16[512,384]{1,0:T(8,128)(2,1)} %bitcast.32), channel_id=1, source_target_pairs={{0,16},{16,0},{1,17},{17,1},{2,18},{18,2},{3,19},{19,3},{4,20},{20... | collective-permute-start | bytes 1179656 | tf_op jit(solution)/shard_map/ppermute | solution.py:237
  3.7 21.6 %collective-permute-start = (bf16[128,1024]{1,0:T(8,128)(2,1)}, bf16[128,1024]{1,0:T(8,128)(2,1)S(1)}, u32[]{:S(2)}, u32[]{:S(2)}) collective-permute-start(bf16[128,1024]{1,0:T(8,128)(2,1)} %refs_2_.1), channel_id=1, source_target_pairs={{0,8},{1,9},{2,10},{3,11},{4,12},{5,13},{6,14},{7,15},{8,0},{9,1},... | collective-permute-start | bytes 786440 | tf_op jit(solution)/shard_map/ppermute | solution.py:209
  6.8 23.0 %collective-permute-start.1 = (bf16[128,1024]{1,0:T(8,128)(2,1)}, bf16[128,1024]{1,0:T(8,128)(2,1)S(1)}, u32[]{:S(2)}, u32[]{:S(2)}) collective-permute-start(bf16[128,1024]{1,0:T(8,128)(2,1)} %cot_ref.1), channel_id=1, source_target_pairs={{0,8},{1,9},{2,10},{3,11},{4,12},{5,13},{6,14},{7,15},{8,0},{9,1},... | collective-permute-start | bytes 786440 | tf_op jit(solution)/shard_map/ppermute | solution.py:209
  9.6 52.5 %all-to-all-start = ((bf16[8,40,2048]{2,1,0:T(8,128)(2,1)}), bf16[8,40,2048]{2,1,0:T(8,128)(2,1)S(1)}, u32[]{:S(2)}, u32[]{:S(2)}) async-start(bf16[8,40,2048]{2,1,0:T(8,128)(2,1)} %bitcast.27), calls=%async_computation | async-start | bytes 2621440 | tf_op jit(solution)/shard_map/all_to_all | solution.py:219
  13.9 25.5 %collective-permute-start.4 = (bf16[512,384]{1,0:T(8,128)(2,1)S(1)}, bf16[512,384]{1,0:T(8,128)(2,1)}, u32[]{:S(2)}, u32[]{:S(2)}) collective-permute-start(bf16[512,384]{1,0:T(8,128)(2,1)S(1)} %bitcast.37), channel_id=1, source_target_pairs={{0,16},{16,0},{1,17},{17,1},{2,18},{18,2},{3,19},{19,3},{4,20},{20... | collective-permute-start | bytes 1179656 | tf_op jit(solution)/shard_map/ppermute | solution.py:237
  25.3 6.6 %collective-permute-start.5 = (f32[8,128]{1,0:T(8,128)S(1)}, f32[8,128]{1,0:T(8,128)S(1)}, u32[]{:S(2)}, u32[]{:S(2)}) collective-permute-start(f32[8,128]{1,0:T(8,128)S(1)} %pad_maximum_fusion), channel_id=1, source_target_pairs={{0,8},{1,9},{2,10},{3,11},{4,12},{5,13},{6,14},{7,15},{8,0},{9,1},... | collective-permute-start | bytes 12296 | tf_op jit(solution)/shard_map/ppermute | solution.py:209
  29.7 26.1 %copy-start.13 = (bf16[512,384]{1,0:T(8,128)(2,1)}, bf16[512,384]{1,0:T(8,128)(2,1)S(1)}, u32[]{:S(2)}) copy-start(bf16[512,384]{1,0:T(8,128)(2,1)S(1)} %collective-permute-done.2.refs_2_.refs_9_) | copy-start | bytes 1179652
  35.1 4.2 %collective-permute-start.6 = (bf16[40,2048]{1,0:T(8,128)(2,1)}, bf16[40,2048]{1,0:T(8,128)(2,1)S(1)}, u32[]{:S(2)}, u32[]{:S(2)}) collective-permute-start(bf16[40,2048]{1,0:T(8,128)(2,1)} %get-tuple-element.49), channel_id=1, source_target_pairs={{0,1},{1,0},{2,3},{3,2},{4,5},{5,4},{6,7},{7,6},{8,9},{9,8},{10,11... | collective-permute-start | bytes 491528 | tf_op jit(solution)/shard_map/ppermute | solution.py:214
  35.1 7.3 %collective-permute-start.7 = (bf16[40,2048]{1,0:T(8,128)(2,1)}, bf16[40,2048]{1,0:T(8,128)(2,1)S(1)}, u32[]{:S(2)}, u32[]{:S(2)}) collective-permute-start(bf16[40,2048]{1,0:T(8,128)(2,1)} %get-tuple-element.50), channel_id=1, source_target_pairs={{0,2},{1,3},{2,0},{3,1},{4,6},{5,7},{6,4},{7,5},{8,10},{9,11},{10,... | collective-permute-start | bytes 491528 | tf_op jit(solution)/shard_map/ppermute | solution.py:214
  36.7 9.1 %collective-permute-start.8 = (bf16[40,2048]{1,0:T(8,128)(2,1)}, bf16[40,2048]{1,0:T(8,128)(2,1)S(1)}, u32[]{:S(2)}, u32[]{:S(2)}) collective-permute-start(bf16[40,2048]{1,0:T(8,128)(2,1)} %get-tuple-element.51), channel_id=1, source_target_pairs={{0,3},{1,2},{2,1},{3,0},{4,7},{5,6},{6,5},{7,4},{8,11},{9,10},{10,... | collective-permute-start | bytes 491528 | tf_op jit(solution)/shard_map/ppermute | solution.py:214
  37.0 8.8 %collective-permute-start.9 = (bf16[40,2048]{1,0:T(8,128)(2,1)}, bf16[40,2048]{1,0:T(8,128)(2,1)S(1)}, u32[]{:S(2)}, u32[]{:S(2)}) collective-permute-start(bf16[40,2048]{1,0:T(8,128)(2,1)} %get-tuple-element.52), channel_id=1, source_target_pairs={{0,4},{1,5},{2,6},{3,7},{4,0},{5,1},{6,2},{7,3},{8,12},{9,13},{10,... | collective-permute-start | bytes 491528 | tf_op jit(solution)/shard_map/ppermute | solution.py:214
  39.4 8.5 %collective-permute-start.10 = (bf16[40,2048]{1,0:T(8,128)(2,1)}, bf16[40,2048]{1,0:T(8,128)(2,1)S(1)}, u32[]{:S(2)}, u32[]{:S(2)}) collective-permute-start(bf16[40,2048]{1,0:T(8,128)(2,1)} %get-tuple-element.53), channel_id=1, source_target_pairs={{0,5},{1,4},{2,7},{3,6},{4,1},{5,0},{6,3},{7,2},{8,13},{9,12},{10,... | collective-permute-start | bytes 491528 | tf_op jit(solution)/shard_map/ppermute | solution.py:214
  39.4 16.5 %copy-start.4 = (bf16[40,2048]{1,0:T(8,128)(2,1)}, bf16[40,2048]{1,0:T(8,128)(2,1)S(1)}, u32[]{:S(2)}) copy-start(bf16[40,2048]{1,0:T(8,128)(2,1)S(1)} %collective-permute-done.6.refs_1_.refs_5_) | copy-start | bytes 491524
  39.4 13.9 %collective-permute-start.11 = (bf16[40,2048]{1,0:T(8,128)(2,1)}, bf16[40,2048]{1,0:T(8,128)(2,1)S(1)}, u32[]{:S(2)}, u32[]{:S(2)}) collective-permute-start(bf16[40,2048]{1,0:T(8,128)(2,1)} %get-tuple-element.54), channel_id=1, source_target_pairs={{0,6},{1,7},{2,4},{3,5},{4,2},{5,3},{6,0},{7,1},{8,14},{9,15},{10,... | collective-permute-start | bytes 491528 | tf_op jit(solution)/shard_map/ppermute | solution.py:214
  42.4 13.4 %copy-start.5 = (bf16[40,2048]{1,0:T(8,128)(2,1)}, bf16[40,2048]{1,0:T(8,128)(2,1)S(1)}, u32[]{:S(2)}) copy-start(bf16[40,2048]{1,0:T(8,128)(2,1)S(1)} %collective-permute-done.7.refs_2_.refs_6_) | copy-start | bytes 491524
  42.4 13.4 %collective-permute-start.12 = (bf16[40,2048]{1,0:T(8,128)(2,1)}, bf16[40,2048]{1,0:T(8,128)(2,1)S(1)}, u32[]{:S(2)}, u32[]{:S(2)}) collective-permute-start(bf16[40,2048]{1,0:T(8,128)(2,1)} %get-tuple-element.55), channel_id=1, source_target_pairs={{0,7},{1,6},{2,5},{3,4},{4,3},{5,2},{6,1},{7,0},{8,15},{9,14},{10,... | collective-permute-start | bytes 491528 | tf_op jit(solution)/shard_map/ppermute | solution.py:214
  45.8 10.0 %copy-start.6 = (bf16[40,2048]{1,0:T(8,128)(2,1)}, bf16[40,2048]{1,0:T(8,128)(2,1)S(1)}, u32[]{:S(2)}) copy-start(bf16[40,2048]{1,0:T(8,128)(2,1)S(1)} %collective-permute-done.8.refs_3_.refs_7_) | copy-start | bytes 491524
  45.8 10.0 %copy-start.7 = (bf16[40,2048]{1,0:T(8,128)(2,1)}, bf16[40,2048]{1,0:T(8,128)(2,1)S(1)}, u32[]{:S(2)}) copy-start(bf16[40,2048]{1,0:T(8,128)(2,1)S(1)} %collective-permute-done.9.refs_4_.refs_8_) | copy-start | bytes 491524
  63.1 20.8 %all-to-all-start.1 = ((bf16[8,40,2048]{2,1,0:T(8,128)(2,1)}), bf16[8,40,2048]{2,1,0:T(8,128)(2,1)S(1)}, u32[]{:S(2)}, u32[]{:S(2)}) async-start(bf16[8,40,2048]{2,1,0:T(8,128)(2,1)} %get-tuple-element.56), calls=%async_computation.1 | async-start | bytes 2621440 | tf_op jit(solution)/shard_map/all_to_all | solution.py:219
  88.2 35.2 %all-to-all-start.2 = ((bf16[8,40,2048]{2,1,0:T(8,128)(2,1)}), bf16[8,40,2048]{2,1,0:T(8,128)(2,1)S(1)}, u32[]{:S(2)}, u32[]{:S(2)}) async-start(bf16[8,40,2048]{2,1,0:T(8,128)(2,1)} %bitcast.28), calls=%async_computation.2 | async-start | bytes 2621440 | tf_op jit(solution)/shard_map/all_to_all | solution.py:219
  92.1 28.3 %collective-permute-start.15 = (bf16[3,512,384]{2,1,0:T(8,128)(2,1)S(1)}, bf16[3,512,384]{2,1,0:T(8,128)(2,1)}, u32[]{:S(2)}, u32[]{:S(2)}) collective-permute-start(bf16[3,512,384]{2,1,0:T(8,128)(2,1)S(1)} %copy-done.3), channel_id=1, source_target_pairs={{0,16},{16,0},{1,17},{17,1},{2,18},{18,2},{3,19},{19,3},{4,20},{20... | collective-permute-start | bytes 3538952 | tf_op jit(solution)/shard_map/ppermute | solution.py:314
  93.6 34.3 %collective-permute-start.13 = (bf16[128,2048]{1,0:T(8,128)(2,1)}, bf16[128,2048]{1,0:T(8,128)(2,1)S(1)}, u32[]{:S(2)}, u32[]{:S(2)}) collective-permute-start(bf16[128,2048]{1,0:T(8,128)(2,1)} %get-tuple-element.67), channel_id=1, source_target_pairs={{0,8},{1,9},{2,10},{3,11},{4,12},{5,13},{6,14},{7,15},{8,0},{9,1},... | collective-permute-start | bytes 1572872 | tf_op jit(solution)/shard_map/ppermute | solution.py:209
  100.9 27.0 %collective-permute-start.14 = (f32[128,4]{1,0:T(8,128)S(1)}, f32[128,4]{1,0:T(8,128)S(1)}, u32[]{:S(2)}, u32[]{:S(2)}) collective-permute-start(f32[128,4]{1,0:T(8,128)S(1)} %copy-done.20), channel_id=1, source_target_pairs={{0,8},{1,9},{2,10},{3,11},{4,12},{5,13},{6,14},{7,15},{8,0},{9,1},... | collective-permute-start | bytes 6152 | tf_op jit(solution)/shard_map/ppermute | solution.py:209
  (17 other events, 59.4 us)

commit v4 on v3

--- a/solution.py
+++ b/solution.py
@@ -119,21 +119,28 @@
         store_rows(at_ref, pieces, out_ref, cols(p, feat), back.astype(BF))
 
 
-def weights_kernel(blocks, at_ref, *refs):
-    ins, out_ref = refs[:-1], refs[-1]
-    width = out_ref.shape[1]
+def weights_kernel(blocks, pieces, at_ref, *refs):
+    ins, outs = refs[:-pieces], refs[-pieces:]
+    width = outs[0].shape[1]
     feat = ins[0].shape[1] // 2
-    sums = [0.0, 0.0, 0.0]
-    for count in blocks:
-        part, ins = ins[: count + 3], ins[count + 3 :]
-        rows, (d_gate, d_up, hidden) = part[:count], part[count:]
-        x = joined(rows, pl.ds(pl.multiple_of(at_ref[0], 128), width))
-        g = joined(rows, pl.ds(pl.multiple_of(at_ref[0] + feat, 128), width))
-        sums[0] = sums[0] + dot_rows(x, d_gate[...])
-        sums[1] = sums[1] + dot_rows(x, d_up[...])
-        sums[2] = sums[2] + dot_rows(g, hidden[...])
-    for i in range(3):
-        out_ref[i] = sums[i].astype(BF)
+    for p in range(pieces):
+        sums = [0.0, 0.0, 0.0]
+        rest = ins
+        for count in blocks:
+            part, rest = rest[: count + 3], rest[count + 3 :]
+            rows, (d_gate, d_up, hidden) = part[:count], part[count:]
+            x = joined(rows, pl.ds(pl.multiple_of(at_ref[p], 128), width))
+            g = joined(rows, pl.ds(pl.multiple_of(at_ref[p] + feat, 128), width))
+            sums[0] = sums[0] + dot_rows(x, d_gate[...])
+            sums[1] = sums[1] + dot_rows(x, d_up[...])
+            sums[2] = sums[2] + dot_rows(g, hidden[...])
+        for i in range(3):
+            outs[p][i] = sums[i].astype(BF)
+
+
+def add_kernel(kept_ref, got_ref, *outs):
+    for i, out_ref in enumerate(outs):
+        out_ref[0] = kept_ref[i].astype(F32) + got_ref[i].astype(F32)
 
 
 def combine_kernel(blocks, starts_ref, plan_ref, cot_ref, *refs):
@@ -148,12 +155,15 @@
     at = [lax.broadcasted_iota(jnp.int32, shape, 0) + starts_ref[b] for b in range(blocks)]
     at = at[0] if blocks == 1 else jnp.concatenate(at, axis=0)
     total, every = 0.0, 0.0
+    lane = lax.broadcasted_iota(jnp.int32, (slots.shape[1], 128), 1)
+    grads = jnp.zeros((slots.shape[1], 128), F32)
     for k in range(top):
         picked = (slots[k : k + 1, :] == at).astype(F32)
         every = every + picked
         row = dot_rows(picked.astype(BF), rows)
         total = total + gates[:, top + k : top + k + 1] * row
-        grads_ref[:, k : k + 1] = jnp.sum(cot * row, axis=1, keepdims=True)
+        grads = jnp.where(lane == k, jnp.sum(cot * row, axis=1, keepdims=True), grads)
+    grads_ref[...] = jnp.transpose(grads)[0 : grads_ref.shape[0], :]
     out_ref[:, :feat] = total.astype(out_ref.dtype)
     back = dot_rows(every.astype(BF), joined(ins, slice(feat, 2 * feat)))
     out_ref[:, feat:] = back.astype(out_ref.dtype)
@@ -163,22 +173,29 @@
     feat = mixed_ref.shape[1]
     mixed_ref[...] = (near_ref[:, :feat] + far_ref[:, :feat].astype(F32)).astype(BF)
     grads_ref[...] = (near_ref[:, feat:] + far_ref[:, feat:].astype(F32)).astype(BF)
-    gg_ref[...] = near_gg_ref[...] + far_gg_ref[...]
+    gg_ref[...] = (near_gg_ref[...] + far_gg_ref[...])[0 : gg_ref.shape[0], :]
 
 
 SMEM = pl.BlockSpec(memory_space=pltpu.SMEM)
 VMEM = pl.BlockSpec(memory_space=pltpu.VMEM)
 
 
+def near(value):
+    return pltpu.with_memory_space_constraint(value, pltpu.VMEM)
+
+
+def far(value):
+    return pltpu.with_memory_space_constraint(value, pltpu.HBM)
+
+
 def call(kernel, scalar, arrays, outs, flops):
-    one = not isinstance(outs, (list, tuple))
-    listed = [outs] if one else list(outs)
-    nbytes = sum(a.size * a.dtype.itemsize for a in (*arrays, *listed)) if flops else 0
+    nbytes = sum(a.size * a.dtype.itemsize for a in arrays) if flops else 0
     return pl.pallas_call(
         kernel,
         out_shape=outs,
         in_specs=([] if scalar is None else [SMEM]) + [VMEM] * len(arrays),
-        out_specs=VMEM if one else [VMEM] * len(listed),
+        out_specs=[VMEM] * len(outs),
+        compiler_params=pltpu.CompilerParams(vmem_limit_bytes=16 << 20),
         cost_estimate=cost(flops, nbytes),
     )(*([] if scalar is None else [scalar]), *arrays)
 
@@ -248,9 +265,15 @@
     width = feat // pieces
 
     places = jnp.concatenate([at, (starts - base) // capacity]) if split else at
-    whole_rows = [sds((slot_count, 2 * feat), BF)]
-    split_rows = [sds((capacity, 2 * feat), BF)] * half if split else whole_rows
-    narrow = sds((slot_count, hid), BF)
+    whole_rows = [pltpu.VMEM((slot_count, 2 * feat), BF)]
+    split_rows = whole_rows
+    if split:
+        split_rows = [pltpu.HBM((capacity, 2 * feat), BF)]
+        split_rows = split_rows + [pltpu.VMEM((capacity, 2 * feat), BF)] * (half - 1)
+    narrow = pltpu.HBM((slot_count, hid), BF)
+    first_weights = [far(w) if i % pieces == 0 else near(w) for i, w in enumerate(weights)]
+    weights = [far(w) for w in weights]
+    plan_like = sds((2 * top, tok_rows), F32)
     work = 2 * slot_count * feat * hid
 
     def starts_of(rows):
@@ -261,50 +284,51 @@
             functools.partial(pick_kernel, owners, capacity, len(facts) == 1),
             starts_of(rows),
             [*facts, tokens_at, cot_at],
-            [*rows, sds((2 * top, tok_rows), F32)],
+            [*rows, plan_like],
             4 * slot_count * tok_rows * feat,
         )
         return outs[:-1], outs[-1]
 
-    def expert(rows, stretch):
+    def expert(rows, weights_at, stretch):
+        shape = (half, *rows[0].shape) if len(rows) > 1 else rows[0].shape
         outs = call(
             functools.partial(expert_kernel, pieces, len(rows)),
             places,
-            [*rows, *weights],
-            [sds((half, *rows[0].shape) if len(rows) > 1 else rows[0].shape, BF)] + [narrow] * 3,
+            [*[near(r) for r in rows], *weights_at],
+            [pltpu.VMEM(shape, BF)] + [narrow] * 3,
             6 * work * stretch,
         )
         return outs[:1], outs[1:]
 
-    def combine(plan_at, cot_at, rows, dtype):
+    def combine(plan_at, cot_at, rows, dtype, space):
         return call(
             functools.partial(combine_kernel, len(rows)),
             starts_of(rows),
-            [plan_at, cot_at, *rows],
-            [sds((tok_rows, 2 * feat), dtype), sds((tok_rows, top), F32)],
+            [plan_at, cot_at, *[near(r) for r in rows]],
+            [space((tok_rows, 2 * feat), dtype), pltpu.VMEM((8, tok_rows), F32)],
             2 * (top + 1) * slot_count * tok_rows * feat,
         )
 
-    near_rows, plan = pick((routes.T, gates.T), tokens, cotangent, whole_rows)
+    near_rows, plan = pick(
+        (far(routes.T), far(gates.T)), far(tokens), far(cotangent), whole_rows
+    )
     near_in = exchange(near_rows)
-    far_rows, far_plan = pick((far_facts,), far_tokens, far_cot, split_rows)
+    far_rows, far_plan = pick((near(far_facts),), near(far_tokens), near(far_cot), split_rows)
     far_in = exchange(far_rows)
-    far_out, far_parts = expert(far_in, STRETCH)
+    far_out, far_parts = expert(far_in, first_weights, STRETCH)
     far_back = exchange(far_out)
-    near_out, near_parts = expert(near_in, NEAR)
-
-    def partial(p):
-        return call(
-            functools.partial(weights_kernel, (len(near_in), len(far_in))),
-            at[p : p + 1],
-            [*near_in, *near_parts, *far_in, *far_parts],
-            sds((3, width, hid), BF),
-            6 * work // pieces * NEAR,
-        )
-
-    leaving = partial(pieces - 1)
+    near_out, near_parts = expert(near_in, weights, NEAR)
+
+    partials = call(
+        functools.partial(weights_kernel, (len(near_in), len(far_in)), pieces),
+        at,
+        [far(x) for x in (*near_in, *near_parts, *far_in, *far_parts)],
+        [pltpu.HBM((3, width, hid), BF)] * pieces,
+        6 * work * NEAR,
+    )
+    leaving = partials[-1]
     far_back, leaving = lax.optimization_barrier((far_back, leaving))
-    far_sum, far_gg = combine(far_plan, far_cot, far_back, BF)
+    far_sum, far_gg = combine(far_plan, far(far_cot), far_back, BF, pltpu.HBM)
     near_out, far_sum = lax.optimization_barrier((near_out, far_sum))
     near_back = exchange(near_out)
     got_sum = send(far_sum)
@@ -312,22 +336,27 @@
 
     if replicas == 2:
         got = lax.ppermute(leaving, "dp", swap)
-        kept = partial(0)
-        grads = [kept[i].astype(F32) + got[i].astype(F32) for i in range(3)]
+        grads = call(
+            add_kernel,
+            None,
+            [far(partials[0]), near(got)],
+            [sds((1, share, hid), F32)] * 3,
+            6 * work * STRETCH,
+        )
     else:
         got = lax.all_to_all(leaving, "dp", split_axis=1, concat_axis=0, tiled=True)
         got = got.reshape(replicas, 3, share, hid).astype(F32)
-        grads = [jnp.sum(got[:, i], axis=0) for i in range(3)]
-
-    near_sum, near_gg = combine(plan, cotangent, near_back, F32)
+        grads = [jnp.sum(got[:, i], axis=0)[None] for i in range(3)]
+
+    near_sum, near_gg = combine(plan, far(cotangent), near_back, F32, pltpu.VMEM)
     mixed, token_grads, gate_grads = call(
         finish_kernel,
         None,
-        [near_sum, got_sum, near_gg, got_gg],
-        [sds((tok_rows, feat), BF)] * 2 + [sds((tok_rows, top), F32)],
+        [near(near_sum), near(got_sum), near(near_gg), near(got_gg)],
+        [sds((tok_rows, feat), BF)] * 2 + [sds((top, tok_rows), F32)],
         2 * tok_rows * feat,
     )
-    return (mixed, token_grads, gate_grads, grads[0][None], grads[1][None], grads[2][None])
+    return (mixed, token_grads, gate_grads.T, *grads)
 
 
 def solution(mesh):

time: 133 us -> 124 us (0.932)
  Pallas kernels: 35.2 us -> 28.4 us
  waiting for transfers between devices: 51.7 us -> 56.8 us
  other arithmetic: 4.39 us -> 0.18 us
  local copies, waits for them, and re-layouts: 7.46 us -> 4.8 us
    pallas_call x9, Pallas kernels: 35.2 us -> 28.4 us  [call(): pl.pallas_call(kernel, out_shape=outs, in_specs=([] if scalar is None els...]
    all_to_all x3, waiting for transfers between devices: 6.75 us -> 11 us  [exchange(): lax.all_to_all(parts[0].reshape(half, capacity, 2 * feat), 'expert', spli...]
    add x1 -> x0, other arithmetic: 3.06 us -> none  [on_device(): grads = [kept[i].astype(F32) + got[i].astype(F32) for i in range(3)]]
    ppermute x7, waiting for transfers between devices: 10.4 us -> 12.5 us  [exchange(): lax.ppermute(part, 'expert', [(i, i ^ k) for i in range(owners)])]
    unnamed x45 -> x32, local copies, waits for them, and re-layouts: 6.78 us -> 4.72 us
    ppermute x1, waiting for transfers between devices: 18.8 us -> 16.9 us  [on_device(): got = lax.ppermute(leaving, 'dp', swap)]
  transfers between devices with their start and end apart: 19 -> 19, of which waited for: 9 -> 12; matrix products, arithmetic and copies ran while one was open for 4% -> 0% of each run, Pallas kernels for 23% -> 22%
where the time goes in v4:
time: 124 us; the launch traced here: 123 us
  waiting for transfers between devices  56.8 us (46%)
  starting transfers between devices  32.2 us (26%)
  Pallas kernels  28.4 us (23%)
  local copies, waits for them, and re-layouts  4.8 us (4%)
    pallas_call x9, Pallas kernels, call(): pl.pallas_call(kernel, out_shape=outs, in_specs=([] if scalar is None els...  28.4 us
    ppermute x1, waiting for transfers between devices, on_device(): got = lax.ppermute(leaving, 'dp', swap)  16.9 us
    ppermute x5, waiting for transfers between devices, send(): return lax.ppermute(rows, 'expert', across)  16.4 us
    ppermute x7, waiting for transfers between devices, exchange(): lax.ppermute(part, 'expert', [(i, i ^ k) for i in range(owners)])  12.5 us
    all_to_all x3, starting transfers between devices, exchange(): lax.all_to_all(parts[0].reshape(half, capacity, 2 * feat), 'expert', spli...  11.5 us
    all_to_all x3, waiting for transfers between devices, exchange(): lax.all_to_all(parts[0].reshape(half, capacity, 2 * feat), 'expert', spli...  11 us
    ppermute x7, starting transfers between devices, exchange(): lax.ppermute(part, 'expert', [(i, i ^ k) for i in range(owners)])  8.55 us
    ppermute x5, starting transfers between devices, send(): return lax.ppermute(rows, 'expert', across)  6.07 us
  transfers between devices with their start and end apart: 19, of which 12 were waited for; matrix products, arithmetic and copies ran while one was open for 0% of the time, Pallas kernels for 22%

profile of v4, /device:TPU:0, one launch (start us, length us, event | category | flops | bytes accessed | tf_op | source)
XLA Modules:
  0.0 123.2 jit_solution(17228466403744213736)
XLA Ops:
  0.6 3.0 %collective-permute-start.2 = (bf16[512,384]{1,0:T(8,128)(2,1)}, bf16[512,384]{1,0:T(8,128)(2,1)S(1)}, u32[]{:S(2)}, u32[]{:S(2)}) collective-permute-start(bf16[512,384]{1,0:T(8,128)(2,1)} %bitcast.28), channel_id=1, source_target_pairs={{0,16},{16,0},{1,17},{17,1},{2,18},{18,2},{3,19},{19,3},{4,20},{20... | collective-permute-start | bytes 1179656 | tf_op jit(solution)/shard_map/ppermute | solution.py:254
  3.7 3.0 %collective-permute-start = (bf16[128,1024]{1,0:T(8,128)(2,1)}, bf16[128,1024]{1,0:T(8,128)(2,1)S(1)}, u32[]{:S(2)}, u32[]{:S(2)}) collective-permute-start(bf16[128,1024]{1,0:T(8,128)(2,1)} %refs_2_.1), channel_id=1, source_target_pairs={{0,8},{1,9},{2,10},{3,11},{4,12},{5,13},{6,14},{7,15},{8,0},{9,1},... | collective-permute-start | bytes 786440 | tf_op jit(solution)/shard_map/ppermute | solution.py:226
  6.8 2.8 %shard_map.118 = (bf16[320,2048]{1,0:T(8,128)(2,1)}, f32[8,128]{1,0:T(8,128)S(1)}) custom-call(s32[1]{0:T(128)} %bitcast.starts_ref, s32[4,128]{1,0:T(4,128)} %bitcast.34, f32[4,128]{1,0:T(4,128)} %bitcast.35, bf16[128,1024]{1,0:T(8,128)(2,1)} %refs_2_.1, bf16[128,1024]{1,0:T(8,128)(2,1)} %cot_ref.1), custom_call_target="tpu_custom_call" | custom-call | flops 167772160 | bytes 528384 | tf_op jit(solution)/shard_map/pallas_call | solution.py:193
  9.6 4.2 %all-to-all-start = ((bf16[8,40,2048]{2,1,0:T(8,128)(2,1)}), bf16[8,40,2048]{2,1,0:T(8,128)(2,1)S(1)}, u32[]{:S(2)}, u32[]{:S(2)}) async-start(bf16[8,40,2048]{2,1,0:T(8,128)(2,1)} %bitcast.13), calls=%async_computation | async-start | bytes 2621440 | tf_op jit(solution)/shard_map/all_to_all | solution.py:236
  15.4 9.9 %collective-permute-done.refs_1_ = bf16[128,1024]{1,0:T(8,128)(2,1)S(1)} collective-permute-done((bf16[128,1024]{1,0:T(8,128)(2,1)}, bf16[128,1024]{1,0:T(8,128)(2,1)S(1)}, u32[]{:S(2)}, u32[]{:S(2)}) %collective-permute-start) | collective-permute-done | bytes 262176 | tf_op jit(solution)/shard_map/ppermute | solution.py:226
  25.4 4.4 %collective-permute-done.1.refs_2_.cot_ref = bf16[128,1024]{1,0:T(8,128)(2,1)S(1)} collective-permute-done((bf16[128,1024]{1,0:T(8,128)(2,1)}, bf16[128,1024]{1,0:T(8,128)(2,1)S(1)}, u32[]{:S(2)}, u32[]{:S(2)}) %collective-permute-start.1) | collective-permute-done | bytes 262176 | tf_op jit(solution)/shard_map/ppermute | solution.py:226
  29.7 2.1 %collective-permute-done.5.refs_0_ = f32[8,128]{1,0:T(8,128)S(1)} collective-permute-done((f32[8,128]{1,0:T(8,128)S(1)}, f32[8,128]{1,0:T(8,128)S(1)}, u32[]{:S(2)}, u32[]{:S(2)}) %collective-permute-start.5) | collective-permute-done | bytes 4128 | tf_op jit(solution)/shard_map/ppermute | solution.py:226
  31.9 2.2 %shard_map.120 = (bf16[40,2048]{1,0:T(8,128)(2,1)}, bf16[40,2048]{1,0:T(8,128)(2,1)S(1)}, bf16[40,2048]{1,0:T(8,128)(2,1)S(1)}, bf16[40,2048]{1,0:T(8,128)(2,1)}...) custom-call(s32[8]{0:T(128)S(1)} %stack.46.starts_ref, ...), custom_call_target="tpu_custom_call" | custom-call | flops 167772160 | bytes 528384 | tf_op jit(solution)/shard_map/pallas_call | solution.py:193
  35.9 2.3 %collective-permute-start.9 = (bf16[40,2048]{1,0:T(8,128)(2,1)}, bf16[40,2048]{1,0:T(8,128)(2,1)S(1)}, u32[]{:S(2)}, u32[]{:S(2)}) collective-permute-start(bf16[40,2048]{1,0:T(8,128)(2,1)} %get-tuple-element.57), channel_id=1, source_target_pairs={{0,4},{1,5},{2,6},{3,7},{4,0},{5,1},{6,2},{7,3},{8,12},{9,13},{10,... | collective-permute-start | bytes 491528 | tf_op jit(solution)/shard_map/ppermute | solution.py:231
  38.3 2.6 %collective-permute-start.11 = (bf16[40,2048]{1,0:T(8,128)(2,1)}, bf16[40,2048]{1,0:T(8,128)(2,1)}, u32[]{:S(2)}, u32[]{:S(2)}) collective-permute-start(bf16[40,2048]{1,0:T(8,128)(2,1)} %get-tuple-element.59), channel_id=1, source_target_pairs={{0,6},{1,7},{2,4},{3,5},{4,2},{5,3},{6,0},{7,1},{8,14},{9,15},{10,... | collective-permute-start | bytes 491528 | tf_op jit(solution)/shard_map/ppermute | solution.py:231
  46.0 2.0 %collective-permute-done.10.refs_5_.refs_9_ = bf16[40,2048]{1,0:T(8,128)(2,1)} collective-permute-done((bf16[40,2048]{1,0:T(8,128)(2,1)}, bf16[40,2048]{1,0:T(8,128)(2,1)}, u32[]{:S(2)}, u32[]{:S(2)}) %collective-permute-start.10) | collective-permute-done | bytes 163872 | tf_op jit(solution)/shard_map/ppermute | solution.py:231
  48.0 5.4 %collective-permute-done.11.refs_6_.refs_10_ = bf16[40,2048]{1,0:T(8,128)(2,1)} collective-permute-done((bf16[40,2048]{1,0:T(8,128)(2,1)}, bf16[40,2048]{1,0:T(8,128)(2,1)}, u32[]{:S(2)}, u32[]{:S(2)}) %collective-permute-start.11) | collective-permute-done | bytes 163872 | tf_op jit(solution)/shard_map/ppermute | solution.py:231
  53.4 2.6 %collective-permute-done.12.refs_7_.refs_11_ = bf16[40,2048]{1,0:T(8,128)(2,1)} collective-permute-done((bf16[40,2048]{1,0:T(8,128)(2,1)}, bf16[40,2048]{1,0:T(8,128)(2,1)}, u32[]{:S(2)}, u32[]{:S(2)}) %collective-permute-start.12) | collective-permute-done | bytes 163872 | tf_op jit(solution)/shard_map/ppermute | solution.py:231
  57.8 4.3 %shard_map.121 = (bf16[8,40,2048]{2,1,0:T(8,128)(2,1)S(1)}, bf16[320,384]{1,0:T(8,128)(2,1)}, bf16[320,384]{1,0:T(8,128)(2,1)}, bf16[320,384]{1,0:T(8,128)(2,1)}) custom-call(s32[10]{0:T(128)S(1)} %pad_add_fusion.at_ref, bf16[40,2048]{1,0:T(8,128)(2,1)S(1)} %copy-done.7, bf16[40,2048]{1,0:T(8,128)(2,1)S(1)} %collective-permute-done.6.refs_1_.refs_5_, ...), custom_call_target="tpu_custom_call" | custom-call | flops 18119393280 | bytes 3670016 | tf_op jit(solution)/shard_map/pallas_call | solution.py:193
  63.2 3.6 %all-to-all-start.1 = ((bf16[8,40,2048]{2,1,0:T(8,128)(2,1)}), bf16[8,40,2048]{2,1,0:T(8,128)(2,1)S(1)}, u32[]{:S(2)}, u32[]{:S(2)}) async-start(bf16[8,40,2048]{2,1,0:T(8,128)(2,1)} %copy-done.2), calls=%async_computation.1 | async-start | bytes 2621440 | tf_op jit(solution)/shard_map/all_to_all | solution.py:236
  66.8 4.1 %shard_map.119 = (bf16[320,2048]{1,0:T(8,128)(2,1)S(1)}, bf16[320,384]{1,0:T(8,128)(2,1)}, bf16[320,384]{1,0:T(8,128)(2,1)}, bf16[320,384]{1,0:T(8,128)(2,1)}) custom-call(s32[10]{0:T(128)S(1)} %pad_add_fusion.at_ref, bf16[320,2048]{1,0:T(8,128)(2,1)S(1)} %bitcast.23, bf16[512,384]{1,0:T(8,128)(2,1)} %bitcast.30, bf16[512,384]{1,0:T(8,128)(2,1)} %copy-done.3, ...), custom_call_target="tpu_custom_call" | custom-call | tf_op jit(solution)/shard_map/pallas_call | solution.py:193
  72.1 6.4 %shard_map.122 = (bf16[3,512,384]{2,1,0:T(8,128)(2,1)}, bf16[3,512,384]{2,1,0:T(8,128)(2,1)}) custom-call(s32[2]{0:T(128)S(1)} %pad_add_fusion.1.at_ref, bf16[320,2048]{1,0:T(8,128)(2,1)} %bitcast.24, bf16[320,384]{1,0:T(8,128)(2,1)} %get-tuple-element.62.refs_1_, bf16[320,384]{1,0:T(8,128)(2,1)} %get-tuple-element.63.refs_2_, ...), custom_call_target="tpu_custom_call" | custom-call | tf_op jit(solution)/shard_map/pallas_call | solution.py:193
  78.5 5.5 %all-to-all-done.1 = bf16[8,40,2048]{2,1,0:T(8,128)(2,1)S(1)} async-done(((bf16[8,40,2048]{2,1,0:T(8,128)(2,1)}), bf16[8,40,2048]{2,1,0:T(8,128)(2,1)S(1)}, u32[]{:S(2)}, u32[]{:S(2)}) %all-to-all-start.1) | async-done | bytes 1310752 | tf_op jit(solution)/shard_map/all_to_all | solution.py:236
  85.4 2.7 %shard_map.123 = (bf16[128,2048]{1,0:T(8,128)(2,1)}, f32[8,128]{1,0:T(8,128)S(1)}) custom-call(s32[1]{0:T(128)} %bitcast.starts_ref, f32[8,128]{1,0:T(8,128)S(1)} %get-tuple-element.52.plan_ref, bf16[128,1024]{1,0:T(8,128)(2,1)} %copy-done.6, bf16[320,2048]{1,0:T(8,128)(2,1)S(1)} %bitcast.25), custom_call_target="tpu_custom_call" | custom-call | flops 419430400 | bytes 1576960 | tf_op jit(solution)/shard_map/pallas_call | solution.py:193
  88.2 3.7 %all-to-all-start.2 = ((bf16[8,40,2048]{2,1,0:T(8,128)(2,1)}), bf16[8,40,2048]{2,1,0:T(8,128)(2,1)S(1)}, u32[]{:S(2)}, u32[]{:S(2)}) async-start(bf16[8,40,2048]{2,1,0:T(8,128)(2,1)} %bitcast.27), calls=%async_computation.2 | async-start | bytes 2621440 | tf_op jit(solution)/shard_map/all_to_all | solution.py:236
  91.9 2.3 %collective-permute-start.13 = (bf16[128,2048]{1,0:T(8,128)(2,1)S(1)}, bf16[128,2048]{1,0:T(8,128)(2,1)S(1)}, u32[]{:S(2)}, u32[]{:S(2)}) collective-permute-start(bf16[128,2048]{1,0:T(8,128)(2,1)S(1)} %copy-done.15), channel_id=1, source_target_pairs={{0,8},{1,9},{2,10},{3,11},{4,12},{5,13},{6,14},{7,15},{8,0},{9,1},... | collective-permute-start | bytes 1572872 | tf_op jit(solution)/shard_map/ppermute | solution.py:226
  94.9 16.9 %collective-permute-done.15.got_ref = bf16[3,512,384]{2,1,0:T(8,128)(2,1)} collective-permute-done((bf16[3,512,384]{2,1,0:T(8,128)(2,1)}, bf16[3,512,384]{2,1,0:T(8,128)(2,1)}, u32[]{:S(2)}, u32[]{:S(2)}) %collective-permute-start.15) | collective-permute-done | bytes 1179680 | tf_op jit(solution)/shard_map/ppermute | solution.py:338
  111.8 3.1 %shard_map.126 = (f32[1,512,384]{2,1,0:T(8,128)}, f32[1,512,384]{2,1,0:T(8,128)}, f32[1,512,384]{2,1,0:T(8,128)}) custom-call(bf16[3,512,384]{2,1,0:T(8,128)(2,1)} %get-tuple-element.79.kept_ref, bf16[3,512,384]{2,1,0:T(8,128)(2,1)} %collective-permute-done.15.got_ref), custom_call_target="tpu_custom_call" | custom-call | flops 18119393280 | bytes 2359296 | tf_op jit(solution)/shard_map/pallas_call | solution.py:193
  114.9 5.5 %all-to-all-done.2 = bf16[8,40,2048]{2,1,0:T(8,128)(2,1)S(1)} async-done(((bf16[8,40,2048]{2,1,0:T(8,128)(2,1)}), bf16[8,40,2048]{2,1,0:T(8,128)(2,1)S(1)}, u32[]{:S(2)}, u32[]{:S(2)}) %all-to-all-start.2) | async-done | bytes 1310752 | tf_op jit(solution)/shard_map/all_to_all | solution.py:236
  (61 shorter events, 17.7 us)
Async XLA Ops:
  0.6 29.1 %collective-permute-start.2 = (bf16[512,384]{1,0:T(8,128)(2,1)}, bf16[512,384]{1,0:T(8,128)(2,1)S(1)}, u32[]{:S(2)}, u32[]{:S(2)}) collective-permute-start(bf16[512,384]{1,0:T(8,128)(2,1)} %bitcast.28), channel_id=1, source_target_pairs={{0,16},{16,0},{1,17},{17,1},{2,18},{18,2},{3,19},{19,3},{4,20},{20... | collective-permute-start | bytes 1179656 | tf_op jit(solution)/shard_map/ppermute | solution.py:254
  3.6 26.1 %collective-permute-start.3 = (bf16[512,384]{1,0:T(8,128)(2,1)}, bf16[512,384]{1,0:T(8,128)(2,1)S(1)}, u32[]{:S(2)}, u32[]{:S(2)}) collective-permute-start(bf16[512,384]{1,0:T(8,128)(2,1)} %bitcast.31), channel_id=1, source_target_pairs={{0,16},{16,0},{1,17},{17,1},{2,18},{18,2},{3,19},{19,3},{4,20},{20... | collective-permute-start | bytes 1179656 | tf_op jit(solution)/shard_map/ppermute | solution.py:254
  3.7 21.5 %collective-permute-start = (bf16[128,1024]{1,0:T(8,128)(2,1)}, bf16[128,1024]{1,0:T(8,128)(2,1)S(1)}, u32[]{:S(2)}, u32[]{:S(2)}) collective-permute-start(bf16[128,1024]{1,0:T(8,128)(2,1)} %refs_2_.1), channel_id=1, source_target_pairs={{0,8},{1,9},{2,10},{3,11},{4,12},{5,13},{6,14},{7,15},{8,0},{9,1},... | collective-permute-start | bytes 786440 | tf_op jit(solution)/shard_map/ppermute | solution.py:226
  6.8 22.9 %collective-permute-start.1 = (bf16[128,1024]{1,0:T(8,128)(2,1)}, bf16[128,1024]{1,0:T(8,128)(2,1)S(1)}, u32[]{:S(2)}, u32[]{:S(2)}) collective-permute-start(bf16[128,1024]{1,0:T(8,128)(2,1)} %cot_ref.1), channel_id=1, source_target_pairs={{0,8},{1,9},{2,10},{3,11},{4,12},{5,13},{6,14},{7,15},{8,0},{9,1},... | collective-permute-start | bytes 786440 | tf_op jit(solution)/shard_map/ppermute | solution.py:226
  9.6 53.5 %all-to-all-start = ((bf16[8,40,2048]{2,1,0:T(8,128)(2,1)}), bf16[8,40,2048]{2,1,0:T(8,128)(2,1)S(1)}, u32[]{:S(2)}, u32[]{:S(2)}) async-start(bf16[8,40,2048]{2,1,0:T(8,128)(2,1)} %bitcast.13), calls=%async_computation | async-start | bytes 2621440 | tf_op jit(solution)/shard_map/all_to_all | solution.py:236
  13.9 24.4 %collective-permute-start.4 = (bf16[512,384]{1,0:T(8,128)(2,1)}, bf16[512,384]{1,0:T(8,128)(2,1)S(1)}, u32[]{:S(2)}, u32[]{:S(2)}) collective-permute-start(bf16[512,384]{1,0:T(8,128)(2,1)} %bitcast.17.refs_5_.refs_12_), channel_id=1, source_target_pairs={{0,16},{16,0},{1,17},{17,1},{2,18},{18,2},{3,19},{19,3},{4,20},{20... | collective-permute-start | bytes 1179656 | tf_op jit(solution)/shard_map/ppermute | solution.py:254
  25.3 6.6 %collective-permute-start.5 = (f32[8,128]{1,0:T(8,128)S(1)}, f32[8,128]{1,0:T(8,128)S(1)}, u32[]{:S(2)}, u32[]{:S(2)}) collective-permute-start(f32[8,128]{1,0:T(8,128)S(1)} %pad_maximum_fusion), channel_id=1, source_target_pairs={{0,8},{1,9},{2,10},{3,11},{4,12},{5,13},{6,14},{7,15},{8,0},{9,1},... | collective-permute-start | bytes 12296 | tf_op jit(solution)/shard_map/ppermute | solution.py:226
  29.7 32.3 %copy-start.6 = (bf16[128,1024]{1,0:T(8,128)(2,1)}, bf16[128,1024]{1,0:T(8,128)(2,1)S(1)}, u32[]{:S(2)}) copy-start(bf16[128,1024]{1,0:T(8,128)(2,1)S(1)} %collective-permute-done.1.refs_2_.cot_ref) | copy-start | bytes 786436
  29.7 32.3 %copy-start.3 = (bf16[512,384]{1,0:T(8,128)(2,1)}, bf16[512,384]{1,0:T(8,128)(2,1)S(1)}, u32[]{:S(2)}) copy-start(bf16[512,384]{1,0:T(8,128)(2,1)S(1)} %collective-permute-done.2.refs_2_.refs_9_) | copy-start | bytes 1179652
  29.7 32.3 %copy-start.4 = (bf16[512,384]{1,0:T(8,128)(2,1)}, bf16[512,384]{1,0:T(8,128)(2,1)S(1)}, u32[]{:S(2)}) copy-start(bf16[512,384]{1,0:T(8,128)(2,1)S(1)} %collective-permute-done.3.refs_4_.refs_11_) | copy-start | bytes 1179652
  34.1 4.2 %collective-permute-start.6 = (bf16[40,2048]{1,0:T(8,128)(2,1)S(1)}, bf16[40,2048]{1,0:T(8,128)(2,1)S(1)}, u32[]{:S(2)}, u32[]{:S(2)}) collective-permute-start(bf16[40,2048]{1,0:T(8,128)(2,1)S(1)} %get-tuple-element.54), channel_id=1, source_target_pairs={{0,1},{1,0},{2,3},{3,2},{4,5},{5,4},{6,7},{7,6},{8,9},{9,8},{10,11... | collective-permute-start | bytes 491528 | tf_op jit(solution)/shard_map/ppermute | solution.py:231
  34.1 7.4 %collective-permute-start.7 = (bf16[40,2048]{1,0:T(8,128)(2,1)S(1)}, bf16[40,2048]{1,0:T(8,128)(2,1)S(1)}, u32[]{:S(2)}, u32[]{:S(2)}) collective-permute-start(bf16[40,2048]{1,0:T(8,128)(2,1)S(1)} %get-tuple-element.55), channel_id=1, source_target_pairs={{0,2},{1,3},{2,0},{3,1},{4,6},{5,7},{6,4},{7,5},{8,10},{9,11},{10,... | collective-permute-start | bytes 491528 | tf_op jit(solution)/shard_map/ppermute | solution.py:231
  35.6 8.9 %collective-permute-start.8 = (bf16[40,2048]{1,0:T(8,128)(2,1)}, bf16[40,2048]{1,0:T(8,128)(2,1)S(1)}, u32[]{:S(2)}, u32[]{:S(2)}) collective-permute-start(bf16[40,2048]{1,0:T(8,128)(2,1)} %get-tuple-element.56), channel_id=1, source_target_pairs={{0,3},{1,2},{2,1},{3,0},{4,7},{5,6},{6,5},{7,4},{8,11},{9,10},{10,... | collective-permute-start | bytes 491528 | tf_op jit(solution)/shard_map/ppermute | solution.py:231
  35.9 9.4 %collective-permute-start.9 = (bf16[40,2048]{1,0:T(8,128)(2,1)}, bf16[40,2048]{1,0:T(8,128)(2,1)S(1)}, u32[]{:S(2)}, u32[]{:S(2)}) collective-permute-start(bf16[40,2048]{1,0:T(8,128)(2,1)} %get-tuple-element.57), channel_id=1, source_target_pairs={{0,4},{1,5},{2,6},{3,7},{4,0},{5,1},{6,2},{7,3},{8,12},{9,13},{10,... | collective-permute-start | bytes 491528 | tf_op jit(solution)/shard_map/ppermute | solution.py:231
  38.3 23.8 %copy-start.5 = (bf16[512,384]{1,0:T(8,128)(2,1)}, bf16[512,384]{1,0:T(8,128)(2,1)S(1)}, u32[]{:S(2)}) copy-start(bf16[512,384]{1,0:T(8,128)(2,1)S(1)} %collective-permute-done.4.refs_6_.refs_13_) | copy-start | bytes 1179652
  38.3 9.7 %collective-permute-start.10 = (bf16[40,2048]{1,0:T(8,128)(2,1)}, bf16[40,2048]{1,0:T(8,128)(2,1)}, u32[]{:S(2)}, u32[]{:S(2)}) collective-permute-start(bf16[40,2048]{1,0:T(8,128)(2,1)} %get-tuple-element.58), channel_id=1, source_target_pairs={{0,5},{1,4},{2,7},{3,6},{4,1},{5,0},{6,3},{7,2},{8,13},{9,12},{10,... | collective-permute-start | bytes 491528 | tf_op jit(solution)/shard_map/ppermute | solution.py:231
  38.3 23.8 %copy-start.8 = (bf16[40,2048]{1,0:T(8,128)(2,1)}, bf16[40,2048]{1,0:T(8,128)(2,1)S(1)}, u32[]{:S(2)}) copy-start(bf16[40,2048]{1,0:T(8,128)(2,1)S(1)} %collective-permute-done.6.refs_1_.refs_5_) | copy-start | bytes 491524
  38.3 15.1 %collective-permute-start.11 = (bf16[40,2048]{1,0:T(8,128)(2,1)}, bf16[40,2048]{1,0:T(8,128)(2,1)}, u32[]{:S(2)}, u32[]{:S(2)}) collective-permute-start(bf16[40,2048]{1,0:T(8,128)(2,1)} %get-tuple-element.59), channel_id=1, source_target_pairs={{0,6},{1,7},{2,4},{3,5},{4,2},{5,3},{6,0},{7,1},{8,14},{9,15},{10,... | collective-permute-start | bytes 491528 | tf_op jit(solution)/shard_map/ppermute | solution.py:231
  41.5 14.5 %collective-permute-start.12 = (bf16[40,2048]{1,0:T(8,128)(2,1)}, bf16[40,2048]{1,0:T(8,128)(2,1)}, u32[]{:S(2)}, u32[]{:S(2)}) collective-permute-start(bf16[40,2048]{1,0:T(8,128)(2,1)} %get-tuple-element.60), channel_id=1, source_target_pairs={{0,7},{1,6},{2,5},{3,4},{4,3},{5,2},{6,1},{7,0},{8,15},{9,14},{10,... | collective-permute-start | bytes 491528 | tf_op jit(solution)/shard_map/ppermute | solution.py:231
  63.2 20.8 %all-to-all-start.1 = ((bf16[8,40,2048]{2,1,0:T(8,128)(2,1)}), bf16[8,40,2048]{2,1,0:T(8,128)(2,1)S(1)}, u32[]{:S(2)}, u32[]{:S(2)}) async-start(bf16[8,40,2048]{2,1,0:T(8,128)(2,1)} %copy-done.2), calls=%async_computation.1 | async-start | bytes 2621440 | tf_op jit(solution)/shard_map/all_to_all | solution.py:236
  83.9 27.8 %collective-permute-start.15 = (bf16[3,512,384]{2,1,0:T(8,128)(2,1)}, bf16[3,512,384]{2,1,0:T(8,128)(2,1)}, u32[]{:S(2)}, u32[]{:S(2)}) collective-permute-start(bf16[3,512,384]{2,1,0:T(8,128)(2,1)} %get-tuple-element.80), channel_id=1, source_target_pairs={{0,16},{16,0},{1,17},{17,1},{2,18},{18,2},{3,19},{19,3},{4,20},{20... | collective-permute-start | bytes 3538952 | tf_op jit(solution)/shard_map/ppermute | solution.py:338
  88.2 32.2 %all-to-all-start.2 = ((bf16[8,40,2048]{2,1,0:T(8,128)(2,1)}), bf16[8,40,2048]{2,1,0:T(8,128)(2,1)S(1)}, u32[]{:S(2)}, u32[]{:S(2)}) async-start(bf16[8,40,2048]{2,1,0:T(8,128)(2,1)} %bitcast.27), calls=%async_computation.2 | async-start | bytes 2621440 | tf_op jit(solution)/shard_map/all_to_all | solution.py:236
  91.9 30.4 %collective-permute-start.13 = (bf16[128,2048]{1,0:T(8,128)(2,1)S(1)}, bf16[128,2048]{1,0:T(8,128)(2,1)S(1)}, u32[]{:S(2)}, u32[]{:S(2)}) collective-permute-start(bf16[128,2048]{1,0:T(8,128)(2,1)S(1)} %copy-done.15), channel_id=1, source_target_pairs={{0,8},{1,9},{2,10},{3,11},{4,12},{5,13},{6,14},{7,15},{8,0},{9,1},... | collective-permute-start | bytes 1572872 | tf_op jit(solution)/shard_map/ppermute | solution.py:226
  94.2 28.1 %collective-permute-start.14 = (f32[8,128]{1,0:T(8,128)S(1)}, f32[8,128]{1,0:T(8,128)S(1)}, u32[]{:S(2)}, u32[]{:S(2)}) collective-permute-start(f32[8,128]{1,0:T(8,128)S(1)} %get-tuple-element.75), channel_id=1, source_target_pairs={{0,8},{1,9},{2,10},{3,11},{4,12},{5,13},{6,14},{7,15},{8,0},{9,1},... | collective-permute-start | bytes 12296 | tf_op jit(solution)/shard_map/ppermute | solution.py:226
  (11 other events, 61.8 us)

commit v5 on v4

--- a/solution.py
+++ b/solution.py
@@ -11,6 +11,9 @@
 F32 = jnp.float32
 STRETCH = 12
 NEAR = 0
+PICK = 12
+EARLY = 0
+LATE = 12
 
 
 def dot(left, right):
@@ -279,13 +282,13 @@
     def starts_of(rows):
         return starts if len(rows) > 1 else one_start
 
-    def pick(facts, tokens_at, cot_at, rows):
+    def pick(facts, tokens_at, cot_at, rows, stretch):
         outs = call(
             functools.partial(pick_kernel, owners, capacity, len(facts) == 1),
             starts_of(rows),
             [*facts, tokens_at, cot_at],
             [*rows, plan_like],
-            4 * slot_count * tok_rows * feat,
+            6 * work * stretch,
         )
         return outs[:-1], outs[-1]
 
@@ -306,18 +309,19 @@
             starts_of(rows),
             [plan_at, cot_at, *[near(r) for r in rows]],
             [space((tok_rows, 2 * feat), dtype), pltpu.VMEM((8, tok_rows), F32)],
-            2 * (top + 1) * slot_count * tok_rows * feat,
+            6 * work * NEAR,
         )
 
     near_rows, plan = pick(
-        (far(routes.T), far(gates.T)), far(tokens), far(cotangent), whole_rows
+        (far(routes.T), far(gates.T)), far(tokens), far(cotangent), whole_rows, NEAR
     )
     near_in = exchange(near_rows)
-    far_rows, far_plan = pick((near(far_facts),), near(far_tokens), near(far_cot), split_rows)
+    far_rows, far_plan = pick((near(far_facts),), near(far_tokens), near(far_cot), split_rows, PICK)
     far_in = exchange(far_rows)
-    far_out, far_parts = expert(far_in, first_weights, STRETCH)
+    near_out, near_parts = expert(near_in, first_weights, EARLY)
+    far_in[0], near_parts = lax.optimization_barrier((far_in[0], near_parts))
+    far_out, far_parts = expert(far_in, weights, STRETCH)
     far_back = exchange(far_out)
-    near_out, near_parts = expert(near_in, weights, NEAR)
 
     partials = call(
         functools.partial(weights_kernel, (len(near_in), len(far_in)), pieces),
@@ -327,10 +331,9 @@
         6 * work * NEAR,
     )
     leaving = partials[-1]
-    far_back, leaving = lax.optimization_barrier((far_back, leaving))
+    far_back, leaving, near_out = lax.optimization_barrier((far_back, leaving, near_out))
+    near_back = exchange(near_out)
     far_sum, far_gg = combine(far_plan, far(far_cot), far_back, BF, pltpu.HBM)
-    near_out, far_sum = lax.optimization_barrier((near_out, far_sum))
-    near_back = exchange(near_out)
     got_sum = send(far_sum)
     got_gg = send(far_gg)
 
@@ -341,7 +344,7 @@
             None,
             [far(partials[0]), near(got)],
             [sds((1, share, hid), F32)] * 3,
-            6 * work * STRETCH,
+            6 * work * LATE,
         )
     else:
         got = lax.all_to_all(leaving, "dp", split_axis=1, concat_axis=0, tiled=True)

time: 124 us -> 120 us (0.968)
  waiting for transfers between devices: 56.8 us -> 52.5 us
  local copies, waits for them, and re-layouts: 4.8 us -> 1.23 us
  starting transfers between devices: 32.2 us -> 34.7 us
  Pallas kernels: 28.4 us -> 29.9 us
    ppermute x7, waiting for transfers between devices: 12.5 us -> 7.32 us  [exchange(): lax.ppermute(part, 'expert', [(i, i ^ k) for i in range(owners)])]
    unnamed x32 -> x28, local copies, waits for them, and re-layouts: 4.72 us -> 1.14 us
    ppermute x5, starting transfers between devices: 6.07 us -> 8.65 us  [send(): return lax.ppermute(rows, 'expert', across)]
    pallas_call x9, Pallas kernels: 28.4 us -> 29.9 us  [call(): pl.pallas_call(kernel, out_shape=outs, in_specs=([] if scalar is None els...]
  transfers between devices with their start and end apart: 19 -> 19, of which waited for: 12 -> 10; matrix products, arithmetic and copies ran while one was open for 0% -> 0% of each run, Pallas kernels for 22% -> 20%
where the time goes in v5:
time: 120 us; the launch traced here: 119 us
  waiting for transfers between devices  52.5 us (44%)
  starting transfers between devices  34.7 us (29%)
  Pallas kernels  29.9 us (25%)
  local copies, waits for them, and re-layouts  1.23 us (1%)
    pallas_call x9, Pallas kernels, call(): pl.pallas_call(kernel, out_shape=outs, in_specs=([] if scalar is None els...  29.9 us
    ppermute x1, waiting for transfers between devices, on_device(): got = lax.ppermute(leaving, 'dp', swap)  17.1 us
    ppermute x5, waiting for transfers between devices, send(): return lax.ppermute(rows, 'expert', across)  15.9 us
    all_to_all x3, waiting for transfers between devices, exchange(): lax.all_to_all(parts[0].reshape(half, capacity, 2 * feat), 'expert', spli...  12.2 us
    all_to_all x3, starting transfers between devices, exchange(): lax.all_to_all(parts[0].reshape(half, capacity, 2 * feat), 'expert', spli...  11.4 us
    ppermute x5, starting transfers between devices, send(): return lax.ppermute(rows, 'expert', across)  8.65 us
    ppermute x7, starting transfers between devices, exchange(): lax.ppermute(part, 'expert', [(i, i ^ k) for i in range(owners)])  8.56 us
    ppermute x7, waiting for transfers between devices, exchange(): lax.ppermute(part, 'expert', [(i, i ^ k) for i in range(owners)])  7.32 us
  transfers between devices with their start and end apart: 19, of which 10 were waited for; matrix products, arithmetic and copies ran while one was open for 0% of the time, Pallas kernels for 20%

profile of v5, /device:TPU:0, one launch (start us, length us, event | category | flops | bytes accessed | tf_op | source)
XLA Modules:
  0.0 119.4 jit_solution(7046205875776263411)
XLA Ops:
  0.6 3.0 %collective-permute-start.3 = (bf16[512,384]{1,0:T(8,128)(2,1)}, bf16[512,384]{1,0:T(8,128)(2,1)S(1)}, u32[]{:S(2)}, u32[]{:S(2)}) collective-permute-start(bf16[512,384]{1,0:T(8,128)(2,1)} %bitcast.28), channel_id=1, source_target_pairs={{0,16},{16,0},{1,17},{17,1},{2,18},{18,2},{3,19},{19,3},{4,20},{20... | collective-permute-start | bytes 1179656 | tf_op jit(solution)/shard_map/ppermute | solution.py:257
  3.7 3.0 %collective-permute-start.1 = (bf16[128,1024]{1,0:T(8,128)(2,1)}, bf16[128,1024]{1,0:T(8,128)(2,1)S(1)}, u32[]{:S(2)}, u32[]{:S(2)}) collective-permute-start(bf16[128,1024]{1,0:T(8,128)(2,1)} %refs_2_.1), channel_id=1, source_target_pairs={{0,8},{1,9},{2,10},{3,11},{4,12},{5,13},{6,14},{7,15},{8,0},{9,1},... | collective-permute-start | bytes 786440 | tf_op jit(solution)/shard_map/ppermute | solution.py:229
  6.8 2.8 %shard_map.118 = (bf16[320,2048]{1,0:T(8,128)(2,1)}, f32[8,128]{1,0:T(8,128)S(1)}) custom-call(s32[1]{0:T(128)} %bitcast.starts_ref, s32[4,128]{1,0:T(4,128)} %bitcast.37, f32[4,128]{1,0:T(4,128)} %bitcast.38, bf16[128,1024]{1,0:T(8,128)(2,1)} %refs_2_.1, bf16[128,1024]{1,0:T(8,128)(2,1)} %cot_ref.1), custom_call_target="tpu_custom_call" | custom-call | tf_op jit(solution)/shard_map/pallas_call | solution.py:196
  9.6 4.2 %all-to-all-start = ((bf16[8,40,2048]{2,1,0:T(8,128)(2,1)}), bf16[8,40,2048]{2,1,0:T(8,128)(2,1)S(1)}, u32[]{:S(2)}, u32[]{:S(2)}) async-start(bf16[8,40,2048]{2,1,0:T(8,128)(2,1)} %bitcast.15), calls=%async_computation | async-start | bytes 2621440 | tf_op jit(solution)/shard_map/all_to_all | solution.py:239
  13.9 2.7 %collective-permute-start = (f32[8,128]{1,0:T(8,128)S(1)}, f32[8,128]{1,0:T(8,128)S(1)}, u32[]{:S(2)}, u32[]{:S(2)}) collective-permute-start(f32[8,128]{1,0:T(8,128)S(1)} %pad_maximum_fusion), channel_id=1, source_target_pairs={{0,8},{1,9},{2,10},{3,11},{4,12},{5,13},{6,14},{7,15},{8,0},{9,1},... | collective-permute-start | bytes 12296 | tf_op jit(solution)/shard_map/ppermute | solution.py:229
  16.6 8.6 %collective-permute-done.1.refs_1_ = bf16[128,1024]{1,0:T(8,128)(2,1)S(1)} collective-permute-done((bf16[128,1024]{1,0:T(8,128)(2,1)}, bf16[128,1024]{1,0:T(8,128)(2,1)S(1)}, u32[]{:S(2)}, u32[]{:S(2)}) %collective-permute-start.1) | collective-permute-done | bytes 262176 | tf_op jit(solution)/shard_map/ppermute | solution.py:229
  26.8 2.9 %collective-permute-done.2.refs_2_.cot_ref = bf16[128,1024]{1,0:T(8,128)(2,1)S(1)} collective-permute-done((bf16[128,1024]{1,0:T(8,128)(2,1)}, bf16[128,1024]{1,0:T(8,128)(2,1)S(1)}, u32[]{:S(2)}, u32[]{:S(2)}) %collective-permute-start.2) | collective-permute-done | bytes 262176 | tf_op jit(solution)/shard_map/ppermute | solution.py:229
  29.7 2.1 %collective-permute-done.refs_0_ = f32[8,128]{1,0:T(8,128)S(1)} collective-permute-done((f32[8,128]{1,0:T(8,128)S(1)}, f32[8,128]{1,0:T(8,128)S(1)}, u32[]{:S(2)}, u32[]{:S(2)}) %collective-permute-start) | collective-permute-done | bytes 4128 | tf_op jit(solution)/shard_map/ppermute | solution.py:229
  31.9 2.2 %shard_map.119 = (bf16[40,2048]{1,0:T(8,128)(2,1)}, bf16[40,2048]{1,0:T(8,128)(2,1)S(1)}, bf16[40,2048]{1,0:T(8,128)(2,1)S(1)}, bf16[40,2048]{1,0:T(8,128)(2,1)}...) custom-call(s32[8]{0:T(128)S(1)} %stack.46.starts_ref, ...), custom_call_target="tpu_custom_call" | custom-call | flops 18119393280 | bytes 528384 | tf_op jit(solution)/shard_map/pallas_call | solution.py:196
  36.0 2.3 %collective-permute-start.9 = (bf16[40,2048]{1,0:T(8,128)(2,1)}, bf16[40,2048]{1,0:T(8,128)(2,1)S(1)}, u32[]{:S(2)}, u32[]{:S(2)}) collective-permute-start(bf16[40,2048]{1,0:T(8,128)(2,1)} %get-tuple-element.62), channel_id=1, source_target_pairs={{0,4},{1,5},{2,6},{3,7},{4,0},{5,1},{6,2},{7,3},{8,12},{9,13},{10,... | collective-permute-start | bytes 491528 | tf_op jit(solution)/shard_map/ppermute | solution.py:234
  38.3 2.6 %collective-permute-start.11 = (bf16[40,2048]{1,0:T(8,128)(2,1)}, bf16[40,2048]{1,0:T(8,128)(2,1)}, u32[]{:S(2)}, u32[]{:S(2)}) collective-permute-start(bf16[40,2048]{1,0:T(8,128)(2,1)} %get-tuple-element.64), channel_id=1, source_target_pairs={{0,6},{1,7},{2,4},{3,5},{4,2},{5,3},{6,0},{7,1},{8,14},{9,15},{10,... | collective-permute-start | bytes 491528 | tf_op jit(solution)/shard_map/ppermute | solution.py:234
  43.4 4.7 %shard_map.120 = (bf16[320,2048]{1,0:T(8,128)(2,1)S(1)}, bf16[320,384]{1,0:T(8,128)(2,1)}, bf16[320,384]{1,0:T(8,128)(2,1)}, bf16[320,384]{1,0:T(8,128)(2,1)}) custom-call(s32[10]{0:T(128)S(1)} %pad_add_fusion.at_ref, bf16[320,2048]{1,0:T(8,128)(2,1)S(1)} %bitcast.23, bf16[512,384]{1,0:T(8,128)(2,1)} %bitcast.29, ...), custom_call_target="tpu_custom_call" | custom-call | tf_op jit(solution)/shard_map/pallas_call | solution.py:196
  49.2 4.2 %collective-permute-done.11.refs_6_.refs_10_ = bf16[40,2048]{1,0:T(8,128)(2,1)} collective-permute-done((bf16[40,2048]{1,0:T(8,128)(2,1)}, bf16[40,2048]{1,0:T(8,128)(2,1)}, u32[]{:S(2)}, u32[]{:S(2)}) %collective-permute-start.11) | collective-permute-done | bytes 163872 | tf_op jit(solution)/shard_map/ppermute | solution.py:234
  53.3 2.6 %collective-permute-done.12.refs_7_.refs_11_ = bf16[40,2048]{1,0:T(8,128)(2,1)} collective-permute-done((bf16[40,2048]{1,0:T(8,128)(2,1)}, bf16[40,2048]{1,0:T(8,128)(2,1)}, u32[]{:S(2)}, u32[]{:S(2)}) %collective-permute-start.12) | collective-permute-done | bytes 163872 | tf_op jit(solution)/shard_map/ppermute | solution.py:234
  55.9 5.2 %shard_map.121 = (bf16[8,40,2048]{2,1,0:T(8,128)(2,1)}, bf16[320,384]{1,0:T(8,128)(2,1)}, bf16[320,384]{1,0:T(8,128)(2,1)}, bf16[320,384]{1,0:T(8,128)(2,1)}) custom-call(s32[10]{0:T(128)S(1)} %pad_add_fusion.at_ref, bf16[40,2048]{1,0:T(8,128)(2,1)S(1)} %copy-done.6, bf16[40,2048]{1,0:T(8,128)(2,1)S(1)} %collective-permute-done.6.refs_1_.refs_5_, ...), custom_call_target="tpu_custom_call" | custom-call | flops 18119393280 | bytes 3670016 | tf_op jit(solution)/shard_map/pallas_call | solution.py:196
  61.2 3.6 %all-to-all-start.1 = ((bf16[8,40,2048]{2,1,0:T(8,128)(2,1)}), bf16[8,40,2048]{2,1,0:T(8,128)(2,1)S(1)}, u32[]{:S(2)}, u32[]{:S(2)}) async-start(bf16[8,40,2048]{2,1,0:T(8,128)(2,1)} %get-tuple-element.66), calls=%async_computation.1 | async-start | bytes 2621440 | tf_op jit(solution)/shard_map/all_to_all | solution.py:239
  64.8 6.4 %shard_map.122 = (bf16[3,512,384]{2,1,0:T(8,128)(2,1)}, bf16[3,512,384]{2,1,0:T(8,128)(2,1)}) custom-call(s32[2]{0:T(128)S(1)} %pad_add_fusion.1.at_ref, bf16[320,2048]{1,0:T(8,128)(2,1)} %bitcast.24, bf16[320,384]{1,0:T(8,128)(2,1)} %get-tuple-element.67.refs_1_, bf16[320,384]{1,0:T(8,128)(2,1)} %get-tuple-element.68.refs_2_, ...), custom_call_target="tpu_custom_call" | custom-call | tf_op jit(solution)/shard_map/pallas_call | solution.py:196
  71.2 10.7 %all-to-all-done.1 = bf16[8,40,2048]{2,1,0:T(8,128)(2,1)S(1)} async-done(((bf16[8,40,2048]{2,1,0:T(8,128)(2,1)}), bf16[8,40,2048]{2,1,0:T(8,128)(2,1)S(1)}, u32[]{:S(2)}, u32[]{:S(2)}) %all-to-all-start.1) | async-done | bytes 1310752 | tf_op jit(solution)/shard_map/all_to_all | solution.py:239
  83.4 3.6 %all-to-all-start.2 = ((bf16[8,40,2048]{2,1,0:T(8,128)(2,1)}), bf16[8,40,2048]{2,1,0:T(8,128)(2,1)S(1)}, u32[]{:S(2)}, u32[]{:S(2)}) async-start(bf16[8,40,2048]{2,1,0:T(8,128)(2,1)} %bitcast.27), calls=%async_computation.2 | async-start | bytes 2621440 | tf_op jit(solution)/shard_map/all_to_all | solution.py:239
  87.0 2.7 %shard_map.124 = (bf16[128,2048]{1,0:T(8,128)(2,1)}, f32[8,128]{1,0:T(8,128)S(1)}) custom-call(s32[1]{0:T(128)} %bitcast.starts_ref, f32[8,128]{1,0:T(8,128)S(1)} %get-tuple-element.77.plan_ref, bf16[128,1024]{1,0:T(8,128)(2,1)} %copy-done.5, bf16[320,2048]{1,0:T(8,128)(2,1)S(1)} %bitcast.25), custom_call_target="tpu_custom_call" | custom-call | tf_op jit(solution)/shard_map/pallas_call | solution.py:196
  89.7 2.3 %collective-permute-start.14 = (f32[8,128]{1,0:T(8,128)S(1)}, f32[8,128]{1,0:T(8,128)S(1)}, u32[]{:S(2)}, u32[]{:S(2)}) collective-permute-start(f32[8,128]{1,0:T(8,128)S(1)} %get-tuple-element.81), channel_id=1, source_target_pairs={{0,8},{1,9},{2,10},{3,11},{4,12},{5,13},{6,14},{7,15},{8,0},{9,1},... | collective-permute-start | bytes 12296 | tf_op jit(solution)/shard_map/ppermute | solution.py:229
  92.7 17.1 %collective-permute-done.15.got_ref = bf16[3,512,384]{2,1,0:T(8,128)(2,1)} collective-permute-done((bf16[3,512,384]{2,1,0:T(8,128)(2,1)}, bf16[3,512,384]{2,1,0:T(8,128)(2,1)}, u32[]{:S(2)}, u32[]{:S(2)}) %collective-permute-start.15) | collective-permute-done | bytes 1179680 | tf_op jit(solution)/shard_map/ppermute | solution.py:341
  109.8 3.1 %shard_map.126 = (f32[1,512,384]{2,1,0:T(8,128)}, f32[1,512,384]{2,1,0:T(8,128)}, f32[1,512,384]{2,1,0:T(8,128)}) custom-call(bf16[3,512,384]{2,1,0:T(8,128)(2,1)} %get-tuple-element.85.kept_ref, bf16[3,512,384]{2,1,0:T(8,128)(2,1)} %collective-permute-done.15.got_ref), custom_call_target="tpu_custom_call" | custom-call | flops 18119393280 | bytes 2359296 | tf_op jit(solution)/shard_map/pallas_call | solution.py:196
  116.3 2.2 %collective-permute-done.13.far_ref = bf16[128,2048]{1,0:T(8,128)(2,1)S(1)} collective-permute-done((bf16[128,2048]{1,0:T(8,128)(2,1)}, bf16[128,2048]{1,0:T(8,128)(2,1)S(1)}, u32[]{:S(2)}, u32[]{:S(2)}) %collective-permute-start.13) | collective-permute-done | bytes 524320 | tf_op jit(solution)/shard_map/ppermute | solution.py:229
  (57 shorter events, 13.7 us)
Async XLA Ops:
  0.6 29.1 %collective-permute-start.3 = (bf16[512,384]{1,0:T(8,128)(2,1)}, bf16[512,384]{1,0:T(8,128)(2,1)S(1)}, u32[]{:S(2)}, u32[]{:S(2)}) collective-permute-start(bf16[512,384]{1,0:T(8,128)(2,1)} %bitcast.28), channel_id=1, source_target_pairs={{0,16},{16,0},{1,17},{17,1},{2,18},{18,2},{3,19},{19,3},{4,20},{20... | collective-permute-start | bytes 1179656 | tf_op jit(solution)/shard_map/ppermute | solution.py:257
  3.6 26.1 %collective-permute-start.4 = (bf16[512,384]{1,0:T(8,128)(2,1)}, bf16[512,384]{1,0:T(8,128)(2,1)S(1)}, u32[]{:S(2)}, u32[]{:S(2)}) collective-permute-start(bf16[512,384]{1,0:T(8,128)(2,1)} %bitcast.31), channel_id=1, source_target_pairs={{0,16},{16,0},{1,17},{17,1},{2,18},{18,2},{3,19},{19,3},{4,20},{20... | collective-permute-start | bytes 1179656 | tf_op jit(solution)/shard_map/ppermute | solution.py:257
  3.7 21.5 %collective-permute-start.1 = (bf16[128,1024]{1,0:T(8,128)(2,1)}, bf16[128,1024]{1,0:T(8,128)(2,1)S(1)}, u32[]{:S(2)}, u32[]{:S(2)}) collective-permute-start(bf16[128,1024]{1,0:T(8,128)(2,1)} %refs_2_.1), channel_id=1, source_target_pairs={{0,8},{1,9},{2,10},{3,11},{4,12},{5,13},{6,14},{7,15},{8,0},{9,1},... | collective-permute-start | bytes 786440 | tf_op jit(solution)/shard_map/ppermute | solution.py:229
  6.8 22.9 %collective-permute-start.2 = (bf16[128,1024]{1,0:T(8,128)(2,1)}, bf16[128,1024]{1,0:T(8,128)(2,1)S(1)}, u32[]{:S(2)}, u32[]{:S(2)}) collective-permute-start(bf16[128,1024]{1,0:T(8,128)(2,1)} %cot_ref.1), channel_id=1, source_target_pairs={{0,8},{1,9},{2,10},{3,11},{4,12},{5,13},{6,14},{7,15},{8,0},{9,1},... | collective-permute-start | bytes 786440 | tf_op jit(solution)/shard_map/ppermute | solution.py:229
  9.6 33.7 %all-to-all-start = ((bf16[8,40,2048]{2,1,0:T(8,128)(2,1)}), bf16[8,40,2048]{2,1,0:T(8,128)(2,1)S(1)}, u32[]{:S(2)}, u32[]{:S(2)}) async-start(bf16[8,40,2048]{2,1,0:T(8,128)(2,1)} %bitcast.15), calls=%async_computation | async-start | bytes 2621440 | tf_op jit(solution)/shard_map/all_to_all | solution.py:239
  13.9 18.0 %collective-permute-start = (f32[8,128]{1,0:T(8,128)S(1)}, f32[8,128]{1,0:T(8,128)S(1)}, u32[]{:S(2)}, u32[]{:S(2)}) collective-permute-start(f32[8,128]{1,0:T(8,128)S(1)} %pad_maximum_fusion), channel_id=1, source_target_pairs={{0,8},{1,9},{2,10},{3,11},{4,12},{5,13},{6,14},{7,15},{8,0},{9,1},... | collective-permute-start | bytes 12296 | tf_op jit(solution)/shard_map/ppermute | solution.py:229
  25.3 13.0 %collective-permute-start.5 = (bf16[512,384]{1,0:T(8,128)(2,1)}, bf16[512,384]{1,0:T(8,128)(2,1)S(1)}, u32[]{:S(2)}, u32[]{:S(2)}) collective-permute-start(bf16[512,384]{1,0:T(8,128)(2,1)} %bitcast.34), channel_id=1, source_target_pairs={{0,16},{16,0},{1,17},{17,1},{2,18},{18,2},{3,19},{19,3},{4,20},{20... | collective-permute-start | bytes 1179656 | tf_op jit(solution)/shard_map/ppermute | solution.py:257
  29.7 13.6 %copy-start.2 = (bf16[512,384]{1,0:T(8,128)(2,1)}, bf16[512,384]{1,0:T(8,128)(2,1)S(1)}, u32[]{:S(2)}) copy-start(bf16[512,384]{1,0:T(8,128)(2,1)S(1)} %collective-permute-done.3.refs_2_.refs_9_) | copy-start | bytes 1179652
  29.7 13.6 %copy-start.3 = (bf16[512,384]{1,0:T(8,128)(2,1)}, bf16[512,384]{1,0:T(8,128)(2,1)S(1)}, u32[]{:S(2)}) copy-start(bf16[512,384]{1,0:T(8,128)(2,1)S(1)} %collective-permute-done.4.refs_4_.refs_11_) | copy-start | bytes 1179652
  34.1 4.2 %collective-permute-start.6 = (bf16[40,2048]{1,0:T(8,128)(2,1)S(1)}, bf16[40,2048]{1,0:T(8,128)(2,1)S(1)}, u32[]{:S(2)}, u32[]{:S(2)}) collective-permute-start(bf16[40,2048]{1,0:T(8,128)(2,1)S(1)} %get-tuple-element.59), channel_id=1, source_target_pairs={{0,1},{1,0},{2,3},{3,2},{4,5},{5,4},{6,7},{7,6},{8,9},{9,8},{10,11... | collective-permute-start | bytes 491528 | tf_op jit(solution)/shard_map/ppermute | solution.py:234
  34.1 7.4 %collective-permute-start.7 = (bf16[40,2048]{1,0:T(8,128)(2,1)S(1)}, bf16[40,2048]{1,0:T(8,128)(2,1)S(1)}, u32[]{:S(2)}, u32[]{:S(2)}) collective-permute-start(bf16[40,2048]{1,0:T(8,128)(2,1)S(1)} %get-tuple-element.60), channel_id=1, source_target_pairs={{0,2},{1,3},{2,0},{3,1},{4,6},{5,7},{6,4},{7,5},{8,10},{9,11},{10,... | collective-permute-start | bytes 491528 | tf_op jit(solution)/shard_map/ppermute | solution.py:234
  35.7 13.5 %collective-permute-start.8 = (bf16[40,2048]{1,0:T(8,128)(2,1)}, bf16[40,2048]{1,0:T(8,128)(2,1)S(1)}, u32[]{:S(2)}, u32[]{:S(2)}) collective-permute-start(bf16[40,2048]{1,0:T(8,128)(2,1)} %get-tuple-element.61), channel_id=1, source_target_pairs={{0,3},{1,2},{2,1},{3,0},{4,7},{5,6},{6,5},{7,4},{8,11},{9,10},{10,... | collective-permute-start | bytes 491528 | tf_op jit(solution)/shard_map/ppermute | solution.py:234
  36.0 13.2 %collective-permute-start.9 = (bf16[40,2048]{1,0:T(8,128)(2,1)}, bf16[40,2048]{1,0:T(8,128)(2,1)S(1)}, u32[]{:S(2)}, u32[]{:S(2)}) collective-permute-start(bf16[40,2048]{1,0:T(8,128)(2,1)} %get-tuple-element.62), channel_id=1, source_target_pairs={{0,4},{1,5},{2,6},{3,7},{4,0},{5,1},{6,2},{7,3},{8,12},{9,13},{10,... | collective-permute-start | bytes 491528 | tf_op jit(solution)/shard_map/ppermute | solution.py:234
  38.3 10.9 %collective-permute-start.10 = (bf16[40,2048]{1,0:T(8,128)(2,1)}, bf16[40,2048]{1,0:T(8,128)(2,1)S(1)}, u32[]{:S(2)}, u32[]{:S(2)}) collective-permute-start(bf16[40,2048]{1,0:T(8,128)(2,1)} %get-tuple-element.63), channel_id=1, source_target_pairs={{0,5},{1,4},{2,7},{3,6},{4,1},{5,0},{6,3},{7,2},{8,13},{9,12},{10,... | collective-permute-start | bytes 491528 | tf_op jit(solution)/shard_map/ppermute | solution.py:234
  38.3 17.6 %copy-start.7 = (bf16[40,2048]{1,0:T(8,128)(2,1)}, bf16[40,2048]{1,0:T(8,128)(2,1)S(1)}, u32[]{:S(2)}) copy-start(bf16[40,2048]{1,0:T(8,128)(2,1)S(1)} %collective-permute-done.6.refs_1_.refs_5_) | copy-start | bytes 491524
  38.3 15.0 %collective-permute-start.11 = (bf16[40,2048]{1,0:T(8,128)(2,1)}, bf16[40,2048]{1,0:T(8,128)(2,1)}, u32[]{:S(2)}, u32[]{:S(2)}) collective-permute-start(bf16[40,2048]{1,0:T(8,128)(2,1)} %get-tuple-element.64), channel_id=1, source_target_pairs={{0,6},{1,7},{2,4},{3,5},{4,2},{5,3},{6,0},{7,1},{8,14},{9,15},{10,... | collective-permute-start | bytes 491528 | tf_op jit(solution)/shard_map/ppermute | solution.py:234
  41.5 14.4 %copy-start.8 = (bf16[40,2048]{1,0:T(8,128)(2,1)}, bf16[40,2048]{1,0:T(8,128)(2,1)S(1)}, u32[]{:S(2)}) copy-start(bf16[40,2048]{1,0:T(8,128)(2,1)S(1)} %collective-permute-done.7.refs_2_.refs_6_) | copy-start | bytes 491524
  41.5 14.4 %collective-permute-start.12 = (bf16[40,2048]{1,0:T(8,128)(2,1)}, bf16[40,2048]{1,0:T(8,128)(2,1)}, u32[]{:S(2)}, u32[]{:S(2)}) collective-permute-start(bf16[40,2048]{1,0:T(8,128)(2,1)} %get-tuple-element.65), channel_id=1, source_target_pairs={{0,7},{1,6},{2,5},{3,4},{4,3},{5,2},{6,1},{7,0},{8,15},{9,14},{10,... | collective-permute-start | bytes 491528 | tf_op jit(solution)/shard_map/ppermute | solution.py:234
  43.4 12.6 %copy-start.6 = (bf16[40,2048]{1,0:T(8,128)(2,1)S(1)}, bf16[40,2048]{1,0:T(8,128)(2,1)}, u32[]{:S(2)}) copy-start(bf16[40,2048]{1,0:T(8,128)(2,1)} %get-tuple-element.58.refs_0_.refs_4_) | copy-start | bytes 491524
  61.2 20.8 %all-to-all-start.1 = ((bf16[8,40,2048]{2,1,0:T(8,128)(2,1)}), bf16[8,40,2048]{2,1,0:T(8,128)(2,1)S(1)}, u32[]{:S(2)}, u32[]{:S(2)}) async-start(bf16[8,40,2048]{2,1,0:T(8,128)(2,1)} %get-tuple-element.66), calls=%async_computation.1 | async-start | bytes 2621440 | tf_op jit(solution)/shard_map/all_to_all | solution.py:239
  81.9 27.8 %collective-permute-start.15 = (bf16[3,512,384]{2,1,0:T(8,128)(2,1)}, bf16[3,512,384]{2,1,0:T(8,128)(2,1)}, u32[]{:S(2)}, u32[]{:S(2)}) collective-permute-start(bf16[3,512,384]{2,1,0:T(8,128)(2,1)} %get-tuple-element.86), channel_id=1, source_target_pairs={{0,16},{16,0},{1,17},{17,1},{2,18},{18,2},{3,19},{19,3},{4,20},{20... | collective-permute-start | bytes 3538952 | tf_op jit(solution)/shard_map/ppermute | solution.py:341
  83.4 30.9 %all-to-all-start.2 = ((bf16[8,40,2048]{2,1,0:T(8,128)(2,1)}), bf16[8,40,2048]{2,1,0:T(8,128)(2,1)S(1)}, u32[]{:S(2)}, u32[]{:S(2)}) async-start(bf16[8,40,2048]{2,1,0:T(8,128)(2,1)} %bitcast.27), calls=%async_computation.2 | async-start | bytes 2621440 | tf_op jit(solution)/shard_map/all_to_all | solution.py:239
  89.7 26.6 %collective-permute-start.14 = (f32[8,128]{1,0:T(8,128)S(1)}, f32[8,128]{1,0:T(8,128)S(1)}, u32[]{:S(2)}, u32[]{:S(2)}) collective-permute-start(f32[8,128]{1,0:T(8,128)S(1)} %get-tuple-element.81), channel_id=1, source_target_pairs={{0,8},{1,9},{2,10},{3,11},{4,12},{5,13},{6,14},{7,15},{8,0},{9,1},... | collective-permute-start | bytes 12296 | tf_op jit(solution)/shard_map/ppermute | solution.py:229
  92.0 26.5 %collective-permute-start.13 = (bf16[128,2048]{1,0:T(8,128)(2,1)}, bf16[128,2048]{1,0:T(8,128)(2,1)S(1)}, u32[]{:S(2)}, u32[]{:S(2)}) collective-permute-start(bf16[128,2048]{1,0:T(8,128)(2,1)} %get-tuple-element.79), channel_id=1, source_target_pairs={{0,8},{1,9},{2,10},{3,11},{4,12},{5,13},{6,14},{7,15},{8,0},{9,1},... | collective-permute-start | bytes 1572872 | tf_op jit(solution)/shard_map/ppermute | solution.py:229
  (9 other events, 64.4 us)

commit v6 on v5

--- a/solution.py
+++ b/solution.py
@@ -50,20 +50,32 @@
 
 def pick_kernel(owners, capacity, packed, starts_ref, *refs):
     if packed:
-        facts_ref, tokens_ref, cot_ref, *outs = refs
-        top = facts_ref.shape[0] // 2
-        routes = facts_ref[0:top, :].astype(jnp.int32)
-        gates = facts_ref[top : 2 * top, :]
+        parcel_ref, rest_ref, cot_ref, *outs, plan_ref = refs
+        top = plan_ref.shape[0] // 2
+        rows, first = cot_ref.shape[0], cot_ref.shape[0] // 2
+        facts = parcel_ref[first : first + 4 * top, 0:rows].astype(F32)
+        routes = facts[0:top, :].astype(jnp.int32)
+        gates = facts[top : 2 * top] + facts[2 * top : 3 * top] + facts[3 * top : 4 * top]
+        tokens = jnp.concatenate([parcel_ref[0:first, :], rest_ref[...]], axis=0)
     else:
-        routes_ref, gates_ref, tokens_ref, cot_ref, *outs = refs
-        top = routes_ref.shape[0]
-        routes, gates = routes_ref[...], gates_ref[...]
-    *outs, plan_ref = outs
+        routes_ref, gates_ref, tokens_ref, cot_ref, *outs, plan_ref, parcel_ref, rest_ref = refs
+        top = plan_ref.shape[0] // 2
+        rows, first = cot_ref.shape[0], cot_ref.shape[0] // 2
+        routes, gates, tokens = routes_ref[...], gates_ref[...], tokens_ref[...]
+        high = gates.astype(BF)
+        after = gates - high.astype(F32)
+        middle = after.astype(BF)
+        low = after - middle.astype(F32)
+        facts = [routes.astype(F32), high.astype(F32), middle.astype(F32), low]
+        parcel_ref[0:first, :] = tokens[:first]
+        rest_ref[...] = tokens[first:]
+        parcel_ref[first : first + 4 * top, :] = jnp.zeros((4 * top, tokens.shape[1]), BF)
+        parcel_ref[first : first + 4 * top, 0:rows] = jnp.concatenate(facts, axis=0).astype(BF)
     slots = slots_in(owners, capacity, routes)
     for k in range(top):
         plan_ref[k : k + 1, :] = slots[k].astype(F32)
     plan_ref[top : 2 * top, :] = gates
-    feat = tokens_ref.shape[1]
+    feat = tokens.shape[1]
     for b, out_ref in enumerate(outs):
         rows = out_ref.shape[0]
         at = lax.broadcasted_iota(jnp.int32, (rows, slots[0].shape[1]), 0) + starts_ref[b]
@@ -73,7 +85,7 @@
         )
         gate = jnp.sum(weight, axis=1, keepdims=True)
         picked = sum(hit.astype(F32) for hit in hits).astype(BF)
-        out_ref[:, :feat] = dot(picked, tokens_ref[...]).astype(BF)
+        out_ref[:, :feat] = dot(picked, tokens).astype(BF)
         out_ref[:, feat:] = (gate * dot(picked, cot_ref[...])).astype(BF)
 
 
@@ -93,8 +105,11 @@
 
 
 def expert_kernel(pieces, blocks, at_ref, *refs):
-    ins, weights = refs[:blocks], refs[blocks : blocks + 3 * pieces]
-    out_ref, d_gate_ref, d_up_ref, hidden_ref = refs[blocks + 3 * pieces :]
+    ins, held = refs[:blocks], refs[blocks : blocks + 2 + pieces]
+    weights = held
+    if pieces == 2:
+        weights = [ref for i in range(3) for ref in (held[i], held[3].at[i])]
+    out_ref, d_gate_ref, d_up_ref, hidden_ref = refs[blocks + 2 + pieces :]
     feat = ins[0].shape[1] // 2
     width = feat // pieces
 
@@ -246,19 +261,13 @@
         )
         return [moved.reshape(slot_count, 2 * feat)]
 
-    far_facts = send(jnp.concatenate([routes.T.astype(F32), gates.T], axis=0))
-    far_tokens = send(tokens)
     far_cot = send(cotangent)
     own = [gate_weight[0], up_weight[0], down_weight[0]]
     share = own[0].shape[0]
     if replicas == 2:
         me = lax.axis_index("dp")
         swap = [(0, 1), (1, 0)]
-        peer = [lax.ppermute(w, "dp", swap) for w in own]
-        far_tokens, far_cot, peer[0], peer[1] = lax.optimization_barrier(
-            (far_tokens, far_cot, peer[0], peer[1])
-        )
-        weights = [own[0], peer[0], own[1], peer[1], own[2], peer[2]]
+        weights = [*own, lax.ppermute(jnp.stack(own), "dp", swap)]
         pieces = 2
         at = jnp.stack([me * share, (1 - me) * share]).astype(jnp.int32)
     else:
@@ -274,7 +283,7 @@
         split_rows = [pltpu.HBM((capacity, 2 * feat), BF)]
         split_rows = split_rows + [pltpu.VMEM((capacity, 2 * feat), BF)] * (half - 1)
     narrow = pltpu.HBM((slot_count, hid), BF)
-    first_weights = [far(w) if i % pieces == 0 else near(w) for i, w in enumerate(weights)]
+    first_weights = [far(w) for w in weights[:3]] + [near(w) for w in weights[3:]]
     weights = [far(w) for w in weights]
     plan_like = sds((2 * top, tok_rows), F32)
     work = 2 * slot_count * feat * hid
@@ -282,15 +291,14 @@
     def starts_of(rows):
         return starts if len(rows) > 1 else one_start
 
-    def pick(facts, tokens_at, cot_at, rows, stretch):
-        outs = call(
-            functools.partial(pick_kernel, owners, capacity, len(facts) == 1),
+    def pick(arrays, rows, more, stretch):
+        return call(
+            functools.partial(pick_kernel, owners, capacity, not more),
             starts_of(rows),
-            [*facts, tokens_at, cot_at],
-            [*rows, plan_like],
+            arrays,
+            [*rows, plan_like, *more],
             6 * work * stretch,
         )
-        return outs[:-1], outs[-1]
 
     def expert(rows, weights_at, stretch):
         shape = (half, *rows[0].shape) if len(rows) > 1 else rows[0].shape
@@ -312,15 +320,20 @@
             6 * work * NEAR,
         )
 
-    near_rows, plan = pick(
-        (far(routes.T), far(gates.T)), far(tokens), far(cotangent), whole_rows, NEAR
-    )
+    first = tok_rows // 2
+    *near_rows, plan, parcel, rest = pick(
+        [far(routes.T), far(gates.T), far(tokens), far(cotangent)],
+        whole_rows,
+        [pltpu.VMEM((first + 4 * top, feat), BF), pltpu.VMEM((tok_rows - first, feat), BF)],
+        NEAR,
+    )
+    far_parcel = [near(send(parcel)), far(send(rest))]
     near_in = exchange(near_rows)
-    far_rows, far_plan = pick((near(far_facts),), near(far_tokens), near(far_cot), split_rows, PICK)
+    *far_rows, far_plan = pick([*far_parcel, near(far_cot)], split_rows, [], PICK)
     far_in = exchange(far_rows)
     near_out, near_parts = expert(near_in, first_weights, EARLY)
     far_in[0], near_parts = lax.optimization_barrier((far_in[0], near_parts))
-    far_out, far_parts = expert(far_in, weights, STRETCH)
+    far_out, far_parts = expert(far_in, first_weights, STRETCH)
     far_back = exchange(far_out)
 
     partials = call(
@@ -333,7 +346,7 @@
     leaving = partials[-1]
     far_back, leaving, near_out = lax.optimization_barrier((far_back, leaving, near_out))
     near_back = exchange(near_out)
-    far_sum, far_gg = combine(far_plan, far(far_cot), far_back, BF, pltpu.HBM)
+    far_sum, far_gg = combine(far_plan, far(far_cot), far_back, BF, pltpu.VMEM)
     got_sum = send(far_sum)
     got_gg = send(far_gg)
 

time: 120 us -> 118 us (0.983)
  waiting for transfers between devices: 52.5 us -> 50.6 us
    ppermute x3 -> x1, starting transfers between devices: 4.59 us -> 1.49 us  [on_device(): weights = [*own, lax.ppermute(jnp.stack(own), 'dp', swap)]]
    ppermute x5, waiting for transfers between devices: 15.9 us -> 13.8 us  [send(): return lax.ppermute(rows, 'expert', across)]
    ppermute x7, waiting for transfers between devices: 7.32 us -> 5.76 us  [exchange(): lax.ppermute(part, 'expert', [(i, i ^ k) for i in range(owners)])]
    ppermute x7, starting transfers between devices: 8.56 us -> 9.87 us  [exchange(): lax.ppermute(part, 'expert', [(i, i ^ k) for i in range(owners)])]
  transfers between devices with their start and end apart: 19 -> 17, of which waited for: 10 -> 7; matrix products, arithmetic and copies ran while one was open for 0% -> 1% of each run, Pallas kernels for 20% -> 20%
where the time goes in v6:
time: 118 us
  waiting for transfers between devices  50.6 us (43%)
  starting transfers between devices  34 us (29%)
  Pallas kernels  29.1 us (25%)
  local copies, waits for them, and re-layouts  1.87 us (2%)
  other arithmetic  1.36 us (1%)
    pallas_call x9, Pallas kernels, call(): pl.pallas_call(kernel, out_shape=outs, in_specs=([] if scalar is None els...  29.1 us
    ppermute x1, waiting for transfers between devices, on_device(): got = lax.ppermute(leaving, 'dp', swap)  17.8 us
    ppermute x5, waiting for transfers between devices, send(): return lax.ppermute(rows, 'expert', across)  13.8 us
    all_to_all x3, waiting for transfers between devices, exchange(): lax.all_to_all(parts[0].reshape(half, capacity, 2 * feat), 'expert', spli...  13.2 us
    all_to_all x3, starting transfers between devices, exchange(): lax.all_to_all(parts[0].reshape(half, capacity, 2 * feat), 'expert', spli...  11.4 us
    ppermute x7, starting transfers between devices, exchange(): lax.ppermute(part, 'expert', [(i, i ^ k) for i in range(owners)])  9.87 us
    ppermute x5, starting transfers between devices, send(): return lax.ppermute(rows, 'expert', across)  9.72 us
    ppermute x7, waiting for transfers between devices, exchange(): lax.ppermute(part, 'expert', [(i, i ^ k) for i in range(owners)])  5.76 us
  transfers between devices with their start and end apart: 17, of which 7 were waited for; matrix products, arithmetic and copies ran while one was open for 1% of the time, Pallas kernels for 20%

profile of v6, /device:TPU:0, one launch (start us, length us, event | category | flops | bytes accessed | tf_op | source)
XLA Modules:
  0.0 117.7 jit_solution(6301688699735985296)
XLA Ops:
  0.6 4.1 %collective-permute-start.2 = (bf16[128,1024]{1,0:T(8,128)(2,1)}, bf16[128,1024]{1,0:T(8,128)(2,1)S(1)}, u32[]{:S(2)}, u32[]{:S(2)}) collective-permute-start(bf16[128,1024]{1,0:T(8,128)(2,1)} %cot_ref.1), channel_id=1, source_target_pairs={{0,8},{1,9},{2,10},{3,11},{4,12},{5,13},{6,14},{7,15},{8,0},{9,1},... | collective-permute-start | bytes 786440 | tf_op jit(solution)/shard_map/ppermute | solution.py:244
  4.7 2.8 %shard_map.118 = (bf16[320,2048]{1,0:T(8,128)(2,1)}, f32[8,128]{1,0:T(8,128)S(1)}, bf16[80,1024]{1,0:T(8,128)(2,1)S(1)}, bf16[64,1024]{1,0:T(8,128)(2,1)S(1)}) custom-call(s32[1]{0:T(128)} %bitcast.starts_ref, s32[4,128]{1,0:T(4,128)} %bitcast.33, f32[4,128]{1,0:T(4,128)} %bitcast.34, bf16[128,1024]{1,0:T(8,128)(2,1)} %refs_2_.1, bf16[128,1024]{1,0:T(8,128)(2,1)} %cot_ref.1), custom_call_target="tpu_custom_call" | custom-call | tf_op jit(solution)/shard_map/pallas_call | solution.py:211
  7.6 4.2 %all-to-all-start = ((bf16[8,40,2048]{2,1,0:T(8,128)(2,1)}), bf16[8,40,2048]{2,1,0:T(8,128)(2,1)S(1)}, u32[]{:S(2)}, u32[]{:S(2)}) async-start(bf16[8,40,2048]{2,1,0:T(8,128)(2,1)} %bitcast.13), calls=%async_computation | async-start | bytes 2621440 | tf_op jit(solution)/shard_map/all_to_all | solution.py:254
  11.8 2.6 %collective-permute-start.1 = (bf16[64,1024]{1,0:T(8,128)(2,1)S(1)}, bf16[64,1024]{1,0:T(8,128)(2,1)S(1)}, u32[]{:S(2)}, u32[]{:S(2)}) collective-permute-start(bf16[64,1024]{1,0:T(8,128)(2,1)S(1)} %get-tuple-element.48), channel_id=1, source_target_pairs={{0,8},{1,9},{2,10},{3,11},{4,12},{5,13},{6,14},{7,15},{8,0},{9,1},... | collective-permute-start | bytes 393224 | tf_op jit(solution)/shard_map/ppermute | solution.py:244
  15.6 1.5 %collective-permute-start.3 = (bf16[3,512,384]{2,1,0:T(8,128)(2,1)}, bf16[3,512,384]{2,1,0:T(8,128)(2,1)S(1)}, u32[]{:S(2)}, u32[]{:S(2)}) collective-permute-start(bf16[3,512,384]{2,1,0:T(8,128)(2,1)} %pad_maximum_fusion), channel_id=1, source_target_pairs={{0,16},{16,0},{1,17},{17,1},{2,18},{18,2},{3,19},{19,3},{4,20},{20... | collective-permute-start | bytes 3538952 | tf_op jit(solution)/shard_map/ppermute | solution.py:270
  17.2 13.8 %collective-permute-done.1.refs_1_ = bf16[64,1024]{1,0:T(8,128)(2,1)S(1)} collective-permute-done((bf16[64,1024]{1,0:T(8,128)(2,1)S(1)}, bf16[64,1024]{1,0:T(8,128)(2,1)S(1)}, u32[]{:S(2)}, u32[]{:S(2)}) %collective-permute-start.1) | collective-permute-done | bytes 131104 | tf_op jit(solution)/shard_map/ppermute | solution.py:244
  31.6 2.7 %shard_map.119 = (bf16[40,2048]{1,0:T(8,128)(2,1)}, bf16[40,2048]{1,0:T(8,128)(2,1)S(1)}, bf16[40,2048]{1,0:T(8,128)(2,1)S(1)}, bf16[40,2048]{1,0:T(8,128)(2,1)}...) custom-call(s32[8]{0:T(128)S(1)} %stack.49.starts_ref, ...), custom_call_target="tpu_custom_call" | custom-call | flops 18119393280 | bytes 557056 | tf_op jit(solution)/shard_map/pallas_call | solution.py:211
  34.3 1.6 %collective-permute-start.5 = (bf16[40,2048]{1,0:T(8,128)(2,1)S(1)}, bf16[40,2048]{1,0:T(8,128)(2,1)S(1)}, u32[]{:S(2)}, u32[]{:S(2)}) collective-permute-start(bf16[40,2048]{1,0:T(8,128)(2,1)S(1)} %get-tuple-element.56), channel_id=1, source_target_pairs={{0,2},{1,3},{2,0},{3,1},{4,6},{5,7},{6,4},{7,5},{8,10},{9,11},{10,... | collective-permute-start | bytes 491528 | tf_op jit(solution)/shard_map/ppermute | solution.py:249
  36.1 3.5 %collective-permute-start.7 = (bf16[40,2048]{1,0:T(8,128)(2,1)}, bf16[40,2048]{1,0:T(8,128)(2,1)S(1)}, u32[]{:S(2)}, u32[]{:S(2)}) collective-permute-start(bf16[40,2048]{1,0:T(8,128)(2,1)} %get-tuple-element.58), channel_id=1, source_target_pairs={{0,4},{1,5},{2,6},{3,7},{4,0},{5,1},{6,2},{7,3},{8,12},{9,13},{10,... | collective-permute-start | bytes 491528 | tf_op jit(solution)/shard_map/ppermute | solution.py:249
  39.7 1.6 %collective-permute-done.5.refs_2_.refs_6_ = bf16[40,2048]{1,0:T(8,128)(2,1)S(1)} collective-permute-done((bf16[40,2048]{1,0:T(8,128)(2,1)S(1)}, bf16[40,2048]{1,0:T(8,128)(2,1)S(1)}, u32[]{:S(2)}, u32[]{:S(2)}) %collective-permute-start.5) | collective-permute-done | bytes 163872 | tf_op jit(solution)/shard_map/ppermute | solution.py:249
  41.4 4.4 %collective-permute-start.9 = (bf16[40,2048]{1,0:T(8,128)(2,1)}, bf16[40,2048]{1,0:T(8,128)(2,1)}, u32[]{:S(2)}, u32[]{:S(2)}) collective-permute-start(bf16[40,2048]{1,0:T(8,128)(2,1)} %get-tuple-element.60), channel_id=1, source_target_pairs={{0,6},{1,7},{2,4},{3,5},{4,2},{5,3},{6,0},{7,1},{8,14},{9,15},{10,... | collective-permute-start | bytes 491528 | tf_op jit(solution)/shard_map/ppermute | solution.py:249
  45.9 4.6 %shard_map.120 = (bf16[320,2048]{1,0:T(8,128)(2,1)S(1)}, bf16[320,384]{1,0:T(8,128)(2,1)}, bf16[320,384]{1,0:T(8,128)(2,1)}, bf16[320,384]{1,0:T(8,128)(2,1)}) custom-call(s32[10]{0:T(128)S(1)} %pad_add_fusion.at_ref, bf16[320,2048]{1,0:T(8,128)(2,1)S(1)} %bitcast.22, bf16[512,384]{1,0:T(8,128)(2,1)} %bitcast.27, bf16[512,384]{1,0:T(8,128)(2,1)} %bitcast.29, ...), custom_call_target="tpu_custom_call" | custom-call | tf_op jit(solution)/shard_map/pallas_call | solution.py:211
  53.0 2.8 %collective-permute-done.10.refs_7_.refs_11_ = bf16[40,2048]{1,0:T(8,128)(2,1)} collective-permute-done((bf16[40,2048]{1,0:T(8,128)(2,1)}, bf16[40,2048]{1,0:T(8,128)(2,1)}, u32[]{:S(2)}, u32[]{:S(2)}) %collective-permute-start.10) | collective-permute-done | bytes 163872 | tf_op jit(solution)/shard_map/ppermute | solution.py:249
  55.8 4.8 %shard_map.121 = (bf16[8,40,2048]{2,1,0:T(8,128)(2,1)}, bf16[320,384]{1,0:T(8,128)(2,1)}, bf16[320,384]{1,0:T(8,128)(2,1)}, bf16[320,384]{1,0:T(8,128)(2,1)}) custom-call(s32[10]{0:T(128)S(1)} %pad_add_fusion.at_ref, bf16[40,2048]{1,0:T(8,128)(2,1)S(1)} %copy-done.3, bf16[40,2048]{1,0:T(8,128)(2,1)S(1)} %collective-permute-done.4.refs_1_.refs_5_, ...), custom_call_target="tpu_custom_call" | custom-call | flops 18119393280 | bytes 3670016 | tf_op jit(solution)/shard_map/pallas_call | solution.py:211
  60.7 3.6 %all-to-all-start.1 = ((bf16[8,40,2048]{2,1,0:T(8,128)(2,1)}), bf16[8,40,2048]{2,1,0:T(8,128)(2,1)S(1)}, u32[]{:S(2)}, u32[]{:S(2)}) async-start(bf16[8,40,2048]{2,1,0:T(8,128)(2,1)} %get-tuple-element.62), calls=%async_computation.1 | async-start | bytes 2621440 | tf_op jit(solution)/shard_map/all_to_all | solution.py:254
  64.3 6.4 %shard_map.122 = (bf16[3,512,384]{2,1,0:T(8,128)(2,1)}, bf16[3,512,384]{2,1,0:T(8,128)(2,1)}) custom-call(s32[2]{0:T(128)S(1)} %pad_add_fusion.1.at_ref, bf16[320,2048]{1,0:T(8,128)(2,1)} %bitcast.23, bf16[320,384]{1,0:T(8,128)(2,1)} %get-tuple-element.63.refs_1_, bf16[320,384]{1,0:T(8,128)(2,1)} %get-tuple-element.64.refs_2_, ...), custom_call_target="tpu_custom_call" | custom-call | tf_op jit(solution)/shard_map/pallas_call | solution.py:211
  70.7 10.7 %all-to-all-done.1 = bf16[8,40,2048]{2,1,0:T(8,128)(2,1)S(1)} async-done(((bf16[8,40,2048]{2,1,0:T(8,128)(2,1)}), bf16[8,40,2048]{2,1,0:T(8,128)(2,1)S(1)}, u32[]{:S(2)}, u32[]{:S(2)}) %all-to-all-start.1) | async-done | bytes 1310752 | tf_op jit(solution)/shard_map/all_to_all | solution.py:254
  82.9 3.6 %all-to-all-start.2 = ((bf16[8,40,2048]{2,1,0:T(8,128)(2,1)}), bf16[8,40,2048]{2,1,0:T(8,128)(2,1)S(1)}, u32[]{:S(2)}, u32[]{:S(2)}) async-start(bf16[8,40,2048]{2,1,0:T(8,128)(2,1)} %bitcast.26), calls=%async_computation.2 | async-start | bytes 2621440 | tf_op jit(solution)/shard_map/all_to_all | solution.py:254
  86.5 1.9 %shard_map.124 = (bf16[128,2048]{1,0:T(8,128)(2,1)S(1)}, f32[8,128]{1,0:T(8,128)S(1)}) custom-call(s32[1]{0:T(128)} %bitcast.starts_ref, f32[8,128]{1,0:T(8,128)S(1)} %get-tuple-element.73.plan_ref, bf16[128,1024]{1,0:T(8,128)(2,1)} %copy-done.2, bf16[320,2048]{1,0:T(8,128)(2,1)S(1)} %bitcast.24), custom_call_target="tpu_custom_call" | custom-call | tf_op jit(solution)/shard_map/pallas_call | solution.py:211
  89.9 1.5 %collective-permute-start.11 = (bf16[128,2048]{1,0:T(8,128)(2,1)S(1)}, bf16[128,2048]{1,0:T(8,128)(2,1)S(1)}, u32[]{:S(2)}, u32[]{:S(2)}) collective-permute-start(bf16[128,2048]{1,0:T(8,128)(2,1)S(1)} %get-tuple-element.75), channel_id=1, source_target_pairs={{0,8},{1,9},{2,10},{3,11},{4,12},{5,13},{6,14},{7,15},{8,0},{9,1},... | collective-permute-start | bytes 1572872 | tf_op jit(solution)/shard_map/ppermute | solution.py:244
  91.5 17.8 %collective-permute-done.13.got_ref = bf16[3,512,384]{2,1,0:T(8,128)(2,1)} collective-permute-done((bf16[3,512,384]{2,1,0:T(8,128)(2,1)}, bf16[3,512,384]{2,1,0:T(8,128)(2,1)}, u32[]{:S(2)}, u32[]{:S(2)}) %collective-permute-start.13) | collective-permute-done | bytes 1179680 | tf_op jit(solution)/shard_map/ppermute | solution.py:354
  109.3 3.1 %shard_map.126 = (f32[1,512,384]{2,1,0:T(8,128)}, f32[1,512,384]{2,1,0:T(8,128)}, f32[1,512,384]{2,1,0:T(8,128)}) custom-call(bf16[3,512,384]{2,1,0:T(8,128)(2,1)} %get-tuple-element.81.kept_ref, bf16[3,512,384]{2,1,0:T(8,128)(2,1)} %collective-permute-done.13.got_ref), custom_call_target="tpu_custom_call" | custom-call | flops 18119393280 | bytes 2359296 | tf_op jit(solution)/shard_map/pallas_call | solution.py:211
  112.4 2.5 %all-to-all-done.2 = bf16[8,40,2048]{2,1,0:T(8,128)(2,1)S(1)} async-done(((bf16[8,40,2048]{2,1,0:T(8,128)(2,1)}), bf16[8,40,2048]{2,1,0:T(8,128)(2,1)S(1)}, u32[]{:S(2)}, u32[]{:S(2)}) %all-to-all-start.2) | async-done | bytes 1310752 | tf_op jit(solution)/shard_map/all_to_all | solution.py:254
  114.8 1.9 %shard_map.123 = (f32[128,2048]{1,0:T(8,128)S(1)}, f32[8,128]{1,0:T(8,128)S(1)}) custom-call(s32[1]{0:T(128)} %bitcast.starts_ref, f32[8,128]{1,0:T(8,128)S(1)} %get-tuple-element.46.plan_ref, bf16[128,1024]{1,0:T(8,128)(2,1)} %cot_ref.1, bf16[320,2048]{1,0:T(8,128)(2,1)S(1)} %bitcast.25), custom_call_target="tpu_custom_call" | custom-call | tf_op jit(solution)/shard_map/pallas_call | solution.py:211
  (50 shorter events, 8.7 us)
Async XLA Ops:
  0.6 31.0 %collective-permute-start.2 = (bf16[128,1024]{1,0:T(8,128)(2,1)}, bf16[128,1024]{1,0:T(8,128)(2,1)S(1)}, u32[]{:S(2)}, u32[]{:S(2)}) collective-permute-start(bf16[128,1024]{1,0:T(8,128)(2,1)} %cot_ref.1), channel_id=1, source_target_pairs={{0,8},{1,9},{2,10},{3,11},{4,12},{5,13},{6,14},{7,15},{8,0},{9,1},... | collective-permute-start | bytes 786440 | tf_op jit(solution)/shard_map/ppermute | solution.py:244
  7.5 23.4 %collective-permute-start = (bf16[80,1024]{1,0:T(8,128)(2,1)S(1)}, bf16[80,1024]{1,0:T(8,128)(2,1)S(1)}, u32[]{:S(2)}, u32[]{:S(2)}) collective-permute-start(bf16[80,1024]{1,0:T(8,128)(2,1)S(1)} %get-tuple-element.47), channel_id=1, source_target_pairs={{0,8},{1,9},{2,10},{3,11},{4,12},{5,13},{6,14},{7,15},{8,0},{9,1},... | collective-permute-start | bytes 491528 | tf_op jit(solution)/shard_map/ppermute | solution.py:244
  7.6 6.8 %copy-start.11 = (bf16[1,512,384]{2,1,0:T(8,128)(2,1)S(1)}, bf16[1,512,384]{2,1,0:T(8,128)(2,1)}, u32[]{:S(2)}) copy-start(bf16[1,512,384]{2,1,0:T(8,128)(2,1)} %param.12) | copy-start | bytes 1179652
  7.6 38.3 %all-to-all-start = ((bf16[8,40,2048]{2,1,0:T(8,128)(2,1)}), bf16[8,40,2048]{2,1,0:T(8,128)(2,1)S(1)}, u32[]{:S(2)}, u32[]{:S(2)}) async-start(bf16[8,40,2048]{2,1,0:T(8,128)(2,1)} %bitcast.13), calls=%async_computation | async-start | bytes 2621440 | tf_op jit(solution)/shard_map/all_to_all | solution.py:254
  11.8 19.1 %collective-permute-start.1 = (bf16[64,1024]{1,0:T(8,128)(2,1)S(1)}, bf16[64,1024]{1,0:T(8,128)(2,1)S(1)}, u32[]{:S(2)}, u32[]{:S(2)}) collective-permute-start(bf16[64,1024]{1,0:T(8,128)(2,1)S(1)} %get-tuple-element.48), channel_id=1, source_target_pairs={{0,8},{1,9},{2,10},{3,11},{4,12},{5,13},{6,14},{7,15},{8,0},{9,1},... | collective-permute-start | bytes 393224 | tf_op jit(solution)/shard_map/ppermute | solution.py:244
  15.6 30.2 %collective-permute-start.3 = (bf16[3,512,384]{2,1,0:T(8,128)(2,1)}, bf16[3,512,384]{2,1,0:T(8,128)(2,1)S(1)}, u32[]{:S(2)}, u32[]{:S(2)}) collective-permute-start(bf16[3,512,384]{2,1,0:T(8,128)(2,1)} %pad_maximum_fusion), channel_id=1, source_target_pairs={{0,16},{16,0},{1,17},{17,1},{2,18},{18,2},{3,19},{19,3},{4,20},{20... | collective-permute-start | bytes 3538952 | tf_op jit(solution)/shard_map/ppermute | solution.py:270
  34.3 5.4 %collective-permute-start.4 = (bf16[40,2048]{1,0:T(8,128)(2,1)S(1)}, bf16[40,2048]{1,0:T(8,128)(2,1)S(1)}, u32[]{:S(2)}, u32[]{:S(2)}) collective-permute-start(bf16[40,2048]{1,0:T(8,128)(2,1)S(1)} %get-tuple-element.55), channel_id=1, source_target_pairs={{0,1},{1,0},{2,3},{3,2},{4,5},{5,4},{6,7},{7,6},{8,9},{9,8},{10,11... | collective-permute-start | bytes 491528 | tf_op jit(solution)/shard_map/ppermute | solution.py:249
  34.3 7.1 %collective-permute-start.5 = (bf16[40,2048]{1,0:T(8,128)(2,1)S(1)}, bf16[40,2048]{1,0:T(8,128)(2,1)S(1)}, u32[]{:S(2)}, u32[]{:S(2)}) collective-permute-start(bf16[40,2048]{1,0:T(8,128)(2,1)S(1)} %get-tuple-element.56), channel_id=1, source_target_pairs={{0,2},{1,3},{2,0},{3,1},{4,6},{5,7},{6,4},{7,5},{8,10},{9,11},{10,... | collective-permute-start | bytes 491528 | tf_op jit(solution)/shard_map/ppermute | solution.py:249
  35.9 15.8 %collective-permute-start.6 = (bf16[40,2048]{1,0:T(8,128)(2,1)}, bf16[40,2048]{1,0:T(8,128)(2,1)S(1)}, u32[]{:S(2)}, u32[]{:S(2)}) collective-permute-start(bf16[40,2048]{1,0:T(8,128)(2,1)} %get-tuple-element.57), channel_id=1, source_target_pairs={{0,3},{1,2},{2,1},{3,0},{4,7},{5,6},{6,5},{7,4},{8,11},{9,10},{10,... | collective-permute-start | bytes 491528 | tf_op jit(solution)/shard_map/ppermute | solution.py:249
  36.1 15.5 %collective-permute-start.7 = (bf16[40,2048]{1,0:T(8,128)(2,1)}, bf16[40,2048]{1,0:T(8,128)(2,1)S(1)}, u32[]{:S(2)}, u32[]{:S(2)}) collective-permute-start(bf16[40,2048]{1,0:T(8,128)(2,1)} %get-tuple-element.58), channel_id=1, source_target_pairs={{0,4},{1,5},{2,6},{3,7},{4,0},{5,1},{6,2},{7,3},{8,12},{9,13},{10,... | collective-permute-start | bytes 491528 | tf_op jit(solution)/shard_map/ppermute | solution.py:249
  39.7 16.1 %copy-start.4 = (bf16[40,2048]{1,0:T(8,128)(2,1)}, bf16[40,2048]{1,0:T(8,128)(2,1)S(1)}, u32[]{:S(2)}) copy-start(bf16[40,2048]{1,0:T(8,128)(2,1)S(1)} %collective-permute-done.4.refs_1_.refs_5_) | copy-start | bytes 491524
  39.7 12.0 %collective-permute-start.8 = (bf16[40,2048]{1,0:T(8,128)(2,1)}, bf16[40,2048]{1,0:T(8,128)(2,1)S(1)}, u32[]{:S(2)}, u32[]{:S(2)}) collective-permute-start(bf16[40,2048]{1,0:T(8,128)(2,1)} %get-tuple-element.59), channel_id=1, source_target_pairs={{0,5},{1,4},{2,7},{3,6},{4,1},{5,0},{6,3},{7,2},{8,13},{9,12},{10,... | collective-permute-start | bytes 491528 | tf_op jit(solution)/shard_map/ppermute | solution.py:249
  41.4 14.5 %copy-start.5 = (bf16[40,2048]{1,0:T(8,128)(2,1)}, bf16[40,2048]{1,0:T(8,128)(2,1)S(1)}, u32[]{:S(2)}) copy-start(bf16[40,2048]{1,0:T(8,128)(2,1)S(1)} %collective-permute-done.5.refs_2_.refs_6_) | copy-start | bytes 491524
  41.4 11.6 %collective-permute-start.9 = (bf16[40,2048]{1,0:T(8,128)(2,1)}, bf16[40,2048]{1,0:T(8,128)(2,1)}, u32[]{:S(2)}, u32[]{:S(2)}) collective-permute-start(bf16[40,2048]{1,0:T(8,128)(2,1)} %get-tuple-element.60), channel_id=1, source_target_pairs={{0,6},{1,7},{2,4},{3,5},{4,2},{5,3},{6,0},{7,1},{8,14},{9,15},{10,... | collective-permute-start | bytes 491528 | tf_op jit(solution)/shard_map/ppermute | solution.py:249
  45.8 10.0 %collective-permute-start.10 = (bf16[40,2048]{1,0:T(8,128)(2,1)}, bf16[40,2048]{1,0:T(8,128)(2,1)}, u32[]{:S(2)}, u32[]{:S(2)}) collective-permute-start(bf16[40,2048]{1,0:T(8,128)(2,1)} %get-tuple-element.61), channel_id=1, source_target_pairs={{0,7},{1,6},{2,5},{3,4},{4,3},{5,2},{6,1},{7,0},{8,15},{9,14},{10,... | collective-permute-start | bytes 491528 | tf_op jit(solution)/shard_map/ppermute | solution.py:249
  45.9 9.9 %copy-start.3 = (bf16[40,2048]{1,0:T(8,128)(2,1)S(1)}, bf16[40,2048]{1,0:T(8,128)(2,1)}, u32[]{:S(2)}) copy-start(bf16[40,2048]{1,0:T(8,128)(2,1)} %get-tuple-element.54.refs_0_.refs_4_) | copy-start | bytes 491524
  51.6 9.0 %copy-start.6 = (bf16[40,2048]{1,0:T(8,128)(2,1)}, bf16[40,2048]{1,0:T(8,128)(2,1)S(1)}, u32[]{:S(2)}) copy-start(bf16[40,2048]{1,0:T(8,128)(2,1)S(1)} %collective-permute-done.6.refs_3_.refs_7_) | copy-start | bytes 491524
  51.7 9.0 %copy-start.7 = (bf16[40,2048]{1,0:T(8,128)(2,1)}, bf16[40,2048]{1,0:T(8,128)(2,1)S(1)}, u32[]{:S(2)}) copy-start(bf16[40,2048]{1,0:T(8,128)(2,1)S(1)} %collective-permute-done.7.refs_4_.refs_8_) | copy-start | bytes 491524
  51.7 9.0 %copy-start.8 = (bf16[40,2048]{1,0:T(8,128)(2,1)}, bf16[40,2048]{1,0:T(8,128)(2,1)S(1)}, u32[]{:S(2)}) copy-start(bf16[40,2048]{1,0:T(8,128)(2,1)S(1)} %collective-permute-done.8.refs_5_.refs_9_) | copy-start | bytes 491524
  60.7 20.8 %all-to-all-start.1 = ((bf16[8,40,2048]{2,1,0:T(8,128)(2,1)}), bf16[8,40,2048]{2,1,0:T(8,128)(2,1)S(1)}, u32[]{:S(2)}, u32[]{:S(2)}) async-start(bf16[8,40,2048]{2,1,0:T(8,128)(2,1)} %get-tuple-element.62), calls=%async_computation.1 | async-start | bytes 2621440 | tf_op jit(solution)/shard_map/all_to_all | solution.py:254
  81.5 27.8 %collective-permute-start.13 = (bf16[3,512,384]{2,1,0:T(8,128)(2,1)}, bf16[3,512,384]{2,1,0:T(8,128)(2,1)}, u32[]{:S(2)}, u32[]{:S(2)}) collective-permute-start(bf16[3,512,384]{2,1,0:T(8,128)(2,1)} %get-tuple-element.82), channel_id=1, source_target_pairs={{0,16},{16,0},{1,17},{17,1},{2,18},{18,2},{3,19},{19,3},{4,20},{20... | collective-permute-start | bytes 3538952 | tf_op jit(solution)/shard_map/ppermute | solution.py:354
  82.9 31.9 %all-to-all-start.2 = ((bf16[8,40,2048]{2,1,0:T(8,128)(2,1)}), bf16[8,40,2048]{2,1,0:T(8,128)(2,1)S(1)}, u32[]{:S(2)}, u32[]{:S(2)}) async-start(bf16[8,40,2048]{2,1,0:T(8,128)(2,1)} %bitcast.26), calls=%async_computation.2 | async-start | bytes 2621440 | tf_op jit(solution)/shard_map/all_to_all | solution.py:254
  88.5 28.3 %collective-permute-start.12 = (f32[8,128]{1,0:T(8,128)S(1)}, f32[8,128]{1,0:T(8,128)S(1)}, u32[]{:S(2)}, u32[]{:S(2)}) collective-permute-start(f32[8,128]{1,0:T(8,128)S(1)} %get-tuple-element.77), channel_id=1, source_target_pairs={{0,8},{1,9},{2,10},{3,11},{4,12},{5,13},{6,14},{7,15},{8,0},{9,1},... | collective-permute-start | bytes 12296 | tf_op jit(solution)/shard_map/ppermute | solution.py:244
  89.9 26.8 %collective-permute-start.11 = (bf16[128,2048]{1,0:T(8,128)(2,1)S(1)}, bf16[128,2048]{1,0:T(8,128)(2,1)S(1)}, u32[]{:S(2)}, u32[]{:S(2)}) collective-permute-start(bf16[128,2048]{1,0:T(8,128)(2,1)S(1)} %get-tuple-element.75), channel_id=1, source_target_pairs={{0,8},{1,9},{2,10},{3,11},{4,12},{5,13},{6,14},{7,15},{8,0},{9,1},... | collective-permute-start | bytes 1572872 | tf_op jit(solution)/shard_map/ppermute | solution.py:244
  (6 other events, 22.7 us)

commit v7 on v6

--- a/solution.py
+++ b/solution.py
@@ -235,9 +235,10 @@
     base = group * slot_count
     across = [(i, (i + half) % owners) for i in range(owners)]
     split = half <= 8 and half & (half - 1) == 0
+    order = [0, 4, 2, 6, 5, 3, 7, 1] if half == 8 else list(range(half))
     one_start = base.astype(jnp.int32).reshape(1)
     if split:
-        starts = jnp.stack([base + (member ^ k) * capacity for k in range(half)])
+        starts = jnp.stack([base + (member ^ k) * capacity for k in order])
         starts = starts.astype(jnp.int32)
 
     def send(rows):
@@ -247,10 +248,10 @@
         if len(parts) > 1:
             moved = [
                 lax.ppermute(part, "expert", [(i, i ^ k) for i in range(owners)])
-                for k, part in reversed(list(enumerate(parts)))
+                for k, part in zip(order, parts)
                 if k
             ]
-            return [parts[0], *reversed(moved)]
+            return [parts[0], *moved]
         moved = lax.all_to_all(
             parts[0].reshape(half, capacity, 2 * feat),
             "expert",

time: 118 us -> 117 us (level)
  starting transfers between devices: 34 us -> 31.8 us
    ppermute x7, starting transfers between devices: 9.87 us -> 7.69 us  [exchange(): lax.ppermute(part, 'expert', [(i, i ^ k) for i in range(owners)])]
where the time goes in v7:
time: 117 us
  waiting for transfers between devices  51.7 us (44%)
  starting transfers between devices  31.8 us (27%)
  Pallas kernels  29.1 us (25%)
  local copies, waits for them, and re-layouts  1.87 us (2%)
  other arithmetic  1.36 us (1%)
    pallas_call x9, Pallas kernels, call(): pl.pallas_call(kernel, out_shape=outs, in_specs=([] if scalar is None els...  29.1 us
    ppermute x1, waiting for transfers between devices, on_device(): got = lax.ppermute(leaving, 'dp', swap)  17.8 us
    ppermute x5, waiting for transfers between devices, send(): return lax.ppermute(rows, 'expert', across)  14 us
    all_to_all x3, waiting for transfers between devices, exchange(): lax.all_to_all(parts[0].reshape(half, capacity, 2 * feat), 'expert', spli...  13.2 us
    all_to_all x3, starting transfers between devices, exchange(): lax.all_to_all(parts[0].reshape(half, capacity, 2 * feat), 'expert', spli...  11.4 us
    ppermute x5, starting transfers between devices, send(): return lax.ppermute(rows, 'expert', across)  9.75 us
    ppermute x7, starting transfers between devices, exchange(): lax.ppermute(part, 'expert', [(i, i ^ k) for i in range(owners)])  7.69 us
    ppermute x7, waiting for transfers between devices, exchange(): lax.ppermute(part, 'expert', [(i, i ^ k) for i in range(owners)])  6.64 us
  transfers between devices with their start and end apart: 17, of which 7 were waited for; matrix products, arithmetic and copies ran while one was open for 1% of the time, Pallas kernels for 20%

profile of v7, /device:TPU:0, one launch (start us, length us, event | category | flops | bytes accessed | tf_op | source)
XLA Modules:
  0.0 116.6 jit_solution(16280808421163271170)
XLA Ops:
  0.6 4.1 %collective-permute-start.2 = (bf16[128,1024]{1,0:T(8,128)(2,1)}, bf16[128,1024]{1,0:T(8,128)(2,1)S(1)}, u32[]{:S(2)}, u32[]{:S(2)}) collective-permute-start(bf16[128,1024]{1,0:T(8,128)(2,1)} %cot_ref.1), channel_id=1, source_target_pairs={{0,8},{1,9},{2,10},{3,11},{4,12},{5,13},{6,14},{7,15},{8,0},{9,1},... | collective-permute-start | bytes 786440 | tf_op jit(solution)/shard_map/ppermute | solution.py:245
  4.7 2.8 %shard_map.118 = (bf16[320,2048]{1,0:T(8,128)(2,1)}, f32[8,128]{1,0:T(8,128)S(1)}, bf16[80,1024]{1,0:T(8,128)(2,1)S(1)}, bf16[64,1024]{1,0:T(8,128)(2,1)S(1)}) custom-call(s32[1]{0:T(128)} %bitcast.starts_ref, s32[4,128]{1,0:T(4,128)} %bitcast.33, f32[4,128]{1,0:T(4,128)} %bitcast.34, bf16[128,1024]{1,0:T(8,128)(2,1)} %refs_2_.1, bf16[128,1024]{1,0:T(8,128)(2,1)} %cot_ref.1), custom_call_target="tpu_custom_call" | custom-call | tf_op jit(solution)/shard_map/pallas_call | solution.py:211
  7.6 4.2 %all-to-all-start = ((bf16[8,40,2048]{2,1,0:T(8,128)(2,1)}), bf16[8,40,2048]{2,1,0:T(8,128)(2,1)S(1)}, u32[]{:S(2)}, u32[]{:S(2)}) async-start(bf16[8,40,2048]{2,1,0:T(8,128)(2,1)} %bitcast.13), calls=%async_computation | async-start | bytes 2621440 | tf_op jit(solution)/shard_map/all_to_all | solution.py:255
  11.8 2.6 %collective-permute-start.1 = (bf16[64,1024]{1,0:T(8,128)(2,1)S(1)}, bf16[64,1024]{1,0:T(8,128)(2,1)S(1)}, u32[]{:S(2)}, u32[]{:S(2)}) collective-permute-start(bf16[64,1024]{1,0:T(8,128)(2,1)S(1)} %get-tuple-element.48), channel_id=1, source_target_pairs={{0,8},{1,9},{2,10},{3,11},{4,12},{5,13},{6,14},{7,15},{8,0},{9,1},... | collective-permute-start | bytes 393224 | tf_op jit(solution)/shard_map/ppermute | solution.py:245
  15.6 1.5 %collective-permute-start.3 = (bf16[3,512,384]{2,1,0:T(8,128)(2,1)}, bf16[3,512,384]{2,1,0:T(8,128)(2,1)S(1)}, u32[]{:S(2)}, u32[]{:S(2)}) collective-permute-start(bf16[3,512,384]{2,1,0:T(8,128)(2,1)} %pad_maximum_fusion), channel_id=1, source_target_pairs={{0,16},{16,0},{1,17},{17,1},{2,18},{18,2},{3,19},{19,3},{4,20},{20... | collective-permute-start | bytes 3538952 | tf_op jit(solution)/shard_map/ppermute | solution.py:271
  17.2 13.8 %collective-permute-done.1.refs_1_ = bf16[64,1024]{1,0:T(8,128)(2,1)S(1)} collective-permute-done((bf16[64,1024]{1,0:T(8,128)(2,1)S(1)}, bf16[64,1024]{1,0:T(8,128)(2,1)S(1)}, u32[]{:S(2)}, u32[]{:S(2)}) %collective-permute-start.1) | collective-permute-done | bytes 131104 | tf_op jit(solution)/shard_map/ppermute | solution.py:245
  31.6 2.7 %shard_map.119 = (bf16[40,2048]{1,0:T(8,128)(2,1)}, bf16[40,2048]{1,0:T(8,128)(2,1)S(1)}, bf16[40,2048]{1,0:T(8,128)(2,1)S(1)}, bf16[40,2048]{1,0:T(8,128)(2,1)}...) custom-call(s32[8]{0:T(128)S(1)} %stack.49.starts_ref, ...), custom_call_target="tpu_custom_call" | custom-call | flops 18119393280 | bytes 557056 | tf_op jit(solution)/shard_map/pallas_call | solution.py:211
  34.3 3.5 %collective-permute-start.4 = (bf16[40,2048]{1,0:T(8,128)(2,1)S(1)}, bf16[40,2048]{1,0:T(8,128)(2,1)S(1)}, u32[]{:S(2)}, u32[]{:S(2)}) collective-permute-start(bf16[40,2048]{1,0:T(8,128)(2,1)S(1)} %get-tuple-element.55), channel_id=1, source_target_pairs={{0,4},{1,5},{2,6},{3,7},{4,0},{5,1},{6,2},{7,3},{8,12},{9,13},{10,... | collective-permute-start | bytes 491528 | tf_op jit(solution)/shard_map/ppermute | solution.py:250
  39.7 4.1 %collective-permute-done.4.refs_1_.refs_5_ = bf16[40,2048]{1,0:T(8,128)(2,1)S(1)} collective-permute-done((bf16[40,2048]{1,0:T(8,128)(2,1)S(1)}, bf16[40,2048]{1,0:T(8,128)(2,1)S(1)}, u32[]{:S(2)}, u32[]{:S(2)}) %collective-permute-start.4) | collective-permute-done | bytes 163872 | tf_op jit(solution)/shard_map/ppermute | solution.py:250
  44.1 2.0 %collective-permute-start.9 = (bf16[40,2048]{1,0:T(8,128)(2,1)}, bf16[40,2048]{1,0:T(8,128)(2,1)}, u32[]{:S(2)}, u32[]{:S(2)}) collective-permute-start(bf16[40,2048]{1,0:T(8,128)(2,1)} %get-tuple-element.60), channel_id=1, source_target_pairs={{0,7},{1,6},{2,5},{3,4},{4,3},{5,2},{6,1},{7,0},{8,15},{9,14},{10,... | collective-permute-start | bytes 491528 | tf_op jit(solution)/shard_map/ppermute | solution.py:250
  46.2 4.6 %shard_map.120 = (bf16[320,2048]{1,0:T(8,128)(2,1)S(1)}, bf16[320,384]{1,0:T(8,128)(2,1)}, bf16[320,384]{1,0:T(8,128)(2,1)}, bf16[320,384]{1,0:T(8,128)(2,1)}) custom-call(s32[10]{0:T(128)S(1)} %pad_add_fusion.at_ref, bf16[320,2048]{1,0:T(8,128)(2,1)S(1)} %bitcast.22, bf16[512,384]{1,0:T(8,128)(2,1)} %bitcast.27, bf16[512,384]{1,0:T(8,128)(2,1)} %bitcast.29, ...), custom_call_target="tpu_custom_call" | custom-call | tf_op jit(solution)/shard_map/pallas_call | solution.py:211
  52.0 2.5 %collective-permute-done.9.refs_6_.refs_10_ = bf16[40,2048]{1,0:T(8,128)(2,1)} collective-permute-done((bf16[40,2048]{1,0:T(8,128)(2,1)}, bf16[40,2048]{1,0:T(8,128)(2,1)}, u32[]{:S(2)}, u32[]{:S(2)}) %collective-permute-start.9) | collective-permute-done | bytes 163872 | tf_op jit(solution)/shard_map/ppermute | solution.py:250
  54.5 4.8 %shard_map.121 = (bf16[8,40,2048]{2,1,0:T(8,128)(2,1)}, bf16[320,384]{1,0:T(8,128)(2,1)}, bf16[320,384]{1,0:T(8,128)(2,1)}, bf16[320,384]{1,0:T(8,128)(2,1)}) custom-call(s32[10]{0:T(128)S(1)} %pad_add_fusion.at_ref, bf16[40,2048]{1,0:T(8,128)(2,1)S(1)} %copy-done.3, bf16[40,2048]{1,0:T(8,128)(2,1)S(1)} %collective-permute-done.4.refs_1_.refs_5_, ...), custom_call_target="tpu_custom_call" | custom-call | flops 18119393280 | bytes 3670016 | tf_op jit(solution)/shard_map/pallas_call | solution.py:211
  59.4 3.6 %all-to-all-start.1 = ((bf16[8,40,2048]{2,1,0:T(8,128)(2,1)}), bf16[8,40,2048]{2,1,0:T(8,128)(2,1)S(1)}, u32[]{:S(2)}, u32[]{:S(2)}) async-start(bf16[8,40,2048]{2,1,0:T(8,128)(2,1)} %get-tuple-element.62), calls=%async_computation.1 | async-start | bytes 2621440 | tf_op jit(solution)/shard_map/all_to_all | solution.py:255
  63.1 6.4 %shard_map.122 = (bf16[3,512,384]{2,1,0:T(8,128)(2,1)}, bf16[3,512,384]{2,1,0:T(8,128)(2,1)}) custom-call(s32[2]{0:T(128)S(1)} %pad_add_fusion.1.at_ref, bf16[320,2048]{1,0:T(8,128)(2,1)} %bitcast.23, bf16[320,384]{1,0:T(8,128)(2,1)} %get-tuple-element.63.refs_1_, bf16[320,384]{1,0:T(8,128)(2,1)} %get-tuple-element.64.refs_2_, ...), custom_call_target="tpu_custom_call" | custom-call | tf_op jit(solution)/shard_map/pallas_call | solution.py:211
  69.4 10.7 %all-to-all-done.1 = bf16[8,40,2048]{2,1,0:T(8,128)(2,1)S(1)} async-done(((bf16[8,40,2048]{2,1,0:T(8,128)(2,1)}), bf16[8,40,2048]{2,1,0:T(8,128)(2,1)S(1)}, u32[]{:S(2)}, u32[]{:S(2)}) %all-to-all-start.1) | async-done | bytes 1310752 | tf_op jit(solution)/shard_map/all_to_all | solution.py:255
  80.2 1.5 %collective-permute-start.13 = (bf16[3,512,384]{2,1,0:T(8,128)(2,1)}, bf16[3,512,384]{2,1,0:T(8,128)(2,1)}, u32[]{:S(2)}, u32[]{:S(2)}) collective-permute-start(bf16[3,512,384]{2,1,0:T(8,128)(2,1)} %get-tuple-element.82), channel_id=1, source_target_pairs={{0,16},{16,0},{1,17},{17,1},{2,18},{18,2},{3,19},{19,3},{4,20},{20... | collective-permute-start | bytes 3538952 | tf_op jit(solution)/shard_map/ppermute | solution.py:355
  81.6 3.6 %all-to-all-start.2 = ((bf16[8,40,2048]{2,1,0:T(8,128)(2,1)}), bf16[8,40,2048]{2,1,0:T(8,128)(2,1)S(1)}, u32[]{:S(2)}, u32[]{:S(2)}) async-start(bf16[8,40,2048]{2,1,0:T(8,128)(2,1)} %bitcast.26), calls=%async_computation.2 | async-start | bytes 2621440 | tf_op jit(solution)/shard_map/all_to_all | solution.py:255
  85.2 1.9 %shard_map.124 = (bf16[128,2048]{1,0:T(8,128)(2,1)S(1)}, f32[8,128]{1,0:T(8,128)S(1)}) custom-call(s32[1]{0:T(128)} %bitcast.starts_ref, f32[8,128]{1,0:T(8,128)S(1)} %get-tuple-element.73.plan_ref, bf16[128,1024]{1,0:T(8,128)(2,1)} %copy-done.2, bf16[320,2048]{1,0:T(8,128)(2,1)S(1)} %bitcast.24), custom_call_target="tpu_custom_call" | custom-call | tf_op jit(solution)/shard_map/pallas_call | solution.py:211
  87.2 2.3 %collective-permute-start.12 = (f32[8,128]{1,0:T(8,128)S(1)}, f32[8,128]{1,0:T(8,128)S(1)}, u32[]{:S(2)}, u32[]{:S(2)}) collective-permute-start(f32[8,128]{1,0:T(8,128)S(1)} %get-tuple-element.77), channel_id=1, source_target_pairs={{0,8},{1,9},{2,10},{3,11},{4,12},{5,13},{6,14},{7,15},{8,0},{9,1},... | collective-permute-start | bytes 12296 | tf_op jit(solution)/shard_map/ppermute | solution.py:245
  90.2 17.8 %collective-permute-done.13.got_ref = bf16[3,512,384]{2,1,0:T(8,128)(2,1)} collective-permute-done((bf16[3,512,384]{2,1,0:T(8,128)(2,1)}, bf16[3,512,384]{2,1,0:T(8,128)(2,1)}, u32[]{:S(2)}, u32[]{:S(2)}) %collective-permute-start.13) | collective-permute-done | bytes 1179680 | tf_op jit(solution)/shard_map/ppermute | solution.py:355
  108.0 3.1 %shard_map.126 = (f32[1,512,384]{2,1,0:T(8,128)}, f32[1,512,384]{2,1,0:T(8,128)}, f32[1,512,384]{2,1,0:T(8,128)}) custom-call(bf16[3,512,384]{2,1,0:T(8,128)(2,1)} %get-tuple-element.81.kept_ref, bf16[3,512,384]{2,1,0:T(8,128)(2,1)} %collective-permute-done.13.got_ref), custom_call_target="tpu_custom_call" | custom-call | flops 18119393280 | bytes 2359296 | tf_op jit(solution)/shard_map/pallas_call | solution.py:211
  111.1 2.5 %all-to-all-done.2 = bf16[8,40,2048]{2,1,0:T(8,128)(2,1)S(1)} async-done(((bf16[8,40,2048]{2,1,0:T(8,128)(2,1)}), bf16[8,40,2048]{2,1,0:T(8,128)(2,1)S(1)}, u32[]{:S(2)}, u32[]{:S(2)}) %all-to-all-start.2) | async-done | bytes 1310752 | tf_op jit(solution)/shard_map/all_to_all | solution.py:255
  113.5 1.9 %shard_map.123 = (f32[128,2048]{1,0:T(8,128)S(1)}, f32[8,128]{1,0:T(8,128)S(1)}) custom-call(s32[1]{0:T(128)} %bitcast.starts_ref, f32[8,128]{1,0:T(8,128)S(1)} %get-tuple-element.46.plan_ref, bf16[128,1024]{1,0:T(8,128)(2,1)} %cot_ref.1, bf16[320,2048]{1,0:T(8,128)(2,1)S(1)} %bitcast.25), custom_call_target="tpu_custom_call" | custom-call | tf_op jit(solution)/shard_map/pallas_call | solution.py:211
  (50 shorter events, 7.3 us)
Async XLA Ops:
  0.6 31.0 %collective-permute-start.2 = (bf16[128,1024]{1,0:T(8,128)(2,1)}, bf16[128,1024]{1,0:T(8,128)(2,1)S(1)}, u32[]{:S(2)}, u32[]{:S(2)}) collective-permute-start(bf16[128,1024]{1,0:T(8,128)(2,1)} %cot_ref.1), channel_id=1, source_target_pairs={{0,8},{1,9},{2,10},{3,11},{4,12},{5,13},{6,14},{7,15},{8,0},{9,1},... | collective-permute-start | bytes 786440 | tf_op jit(solution)/shard_map/ppermute | solution.py:245
  7.5 23.4 %collective-permute-start = (bf16[80,1024]{1,0:T(8,128)(2,1)S(1)}, bf16[80,1024]{1,0:T(8,128)(2,1)S(1)}, u32[]{:S(2)}, u32[]{:S(2)}) collective-permute-start(bf16[80,1024]{1,0:T(8,128)(2,1)S(1)} %get-tuple-element.47), channel_id=1, source_target_pairs={{0,8},{1,9},{2,10},{3,11},{4,12},{5,13},{6,14},{7,15},{8,0},{9,1},... | collective-permute-start | bytes 491528 | tf_op jit(solution)/shard_map/ppermute | solution.py:245
  7.6 6.8 %copy-start.11 = (bf16[1,512,384]{2,1,0:T(8,128)(2,1)S(1)}, bf16[1,512,384]{2,1,0:T(8,128)(2,1)}, u32[]{:S(2)}) copy-start(bf16[1,512,384]{2,1,0:T(8,128)(2,1)} %param.12) | copy-start | bytes 1179652
  7.6 38.6 %all-to-all-start = ((bf16[8,40,2048]{2,1,0:T(8,128)(2,1)}), bf16[8,40,2048]{2,1,0:T(8,128)(2,1)S(1)}, u32[]{:S(2)}, u32[]{:S(2)}) async-start(bf16[8,40,2048]{2,1,0:T(8,128)(2,1)} %bitcast.13), calls=%async_computation | async-start | bytes 2621440 | tf_op jit(solution)/shard_map/all_to_all | solution.py:255
  11.8 19.1 %collective-permute-start.1 = (bf16[64,1024]{1,0:T(8,128)(2,1)S(1)}, bf16[64,1024]{1,0:T(8,128)(2,1)S(1)}, u32[]{:S(2)}, u32[]{:S(2)}) collective-permute-start(bf16[64,1024]{1,0:T(8,128)(2,1)S(1)} %get-tuple-element.48), channel_id=1, source_target_pairs={{0,8},{1,9},{2,10},{3,11},{4,12},{5,13},{6,14},{7,15},{8,0},{9,1},... | collective-permute-start | bytes 393224 | tf_op jit(solution)/shard_map/ppermute | solution.py:245
  15.6 30.5 %collective-permute-start.3 = (bf16[3,512,384]{2,1,0:T(8,128)(2,1)}, bf16[3,512,384]{2,1,0:T(8,128)(2,1)S(1)}, u32[]{:S(2)}, u32[]{:S(2)}) collective-permute-start(bf16[3,512,384]{2,1,0:T(8,128)(2,1)} %pad_maximum_fusion), channel_id=1, source_target_pairs={{0,16},{16,0},{1,17},{17,1},{2,18},{18,2},{3,19},{19,3},{4,20},{20... | collective-permute-start | bytes 3538952 | tf_op jit(solution)/shard_map/ppermute | solution.py:271
  34.3 9.6 %collective-permute-start.4 = (bf16[40,2048]{1,0:T(8,128)(2,1)S(1)}, bf16[40,2048]{1,0:T(8,128)(2,1)S(1)}, u32[]{:S(2)}, u32[]{:S(2)}) collective-permute-start(bf16[40,2048]{1,0:T(8,128)(2,1)S(1)} %get-tuple-element.55), channel_id=1, source_target_pairs={{0,4},{1,5},{2,6},{3,7},{4,0},{5,1},{6,2},{7,3},{8,12},{9,13},{10,... | collective-permute-start | bytes 491528 | tf_op jit(solution)/shard_map/ppermute | solution.py:250
  37.8 6.3 %collective-permute-start.5 = (bf16[40,2048]{1,0:T(8,128)(2,1)S(1)}, bf16[40,2048]{1,0:T(8,128)(2,1)S(1)}, u32[]{:S(2)}, u32[]{:S(2)}) collective-permute-start(bf16[40,2048]{1,0:T(8,128)(2,1)S(1)} %get-tuple-element.56), channel_id=1, source_target_pairs={{0,2},{1,3},{2,0},{3,1},{4,6},{5,7},{6,4},{7,5},{8,10},{9,11},{10,... | collective-permute-start | bytes 491528 | tf_op jit(solution)/shard_map/ppermute | solution.py:250
  39.3 12.7 %collective-permute-start.6 = (bf16[40,2048]{1,0:T(8,128)(2,1)}, bf16[40,2048]{1,0:T(8,128)(2,1)S(1)}, u32[]{:S(2)}, u32[]{:S(2)}) collective-permute-start(bf16[40,2048]{1,0:T(8,128)(2,1)} %get-tuple-element.57), channel_id=1, source_target_pairs={{0,6},{1,7},{2,4},{3,5},{4,2},{5,3},{6,0},{7,1},{8,14},{9,15},{10,... | collective-permute-start | bytes 491528 | tf_op jit(solution)/shard_map/ppermute | solution.py:250
  39.3 12.6 %collective-permute-start.7 = (bf16[40,2048]{1,0:T(8,128)(2,1)}, bf16[40,2048]{1,0:T(8,128)(2,1)S(1)}, u32[]{:S(2)}, u32[]{:S(2)}) collective-permute-start(bf16[40,2048]{1,0:T(8,128)(2,1)} %get-tuple-element.58), channel_id=1, source_target_pairs={{0,5},{1,4},{2,7},{3,6},{4,1},{5,0},{6,3},{7,2},{8,13},{9,12},{10,... | collective-permute-start | bytes 491528 | tf_op jit(solution)/shard_map/ppermute | solution.py:250
  43.9 10.6 %copy-start.4 = (bf16[40,2048]{1,0:T(8,128)(2,1)}, bf16[40,2048]{1,0:T(8,128)(2,1)S(1)}, u32[]{:S(2)}) copy-start(bf16[40,2048]{1,0:T(8,128)(2,1)S(1)} %collective-permute-done.4.refs_1_.refs_5_) | copy-start | bytes 491524
  43.9 8.1 %collective-permute-start.8 = (bf16[40,2048]{1,0:T(8,128)(2,1)}, bf16[40,2048]{1,0:T(8,128)(2,1)S(1)}, u32[]{:S(2)}, u32[]{:S(2)}) collective-permute-start(bf16[40,2048]{1,0:T(8,128)(2,1)} %get-tuple-element.59), channel_id=1, source_target_pairs={{0,3},{1,2},{2,1},{3,0},{4,7},{5,6},{6,5},{7,4},{8,11},{9,10},{10,... | collective-permute-start | bytes 491528 | tf_op jit(solution)/shard_map/ppermute | solution.py:250
  44.1 10.4 %copy-start.5 = (bf16[40,2048]{1,0:T(8,128)(2,1)}, bf16[40,2048]{1,0:T(8,128)(2,1)S(1)}, u32[]{:S(2)}) copy-start(bf16[40,2048]{1,0:T(8,128)(2,1)S(1)} %collective-permute-done.5.refs_2_.refs_6_) | copy-start | bytes 491524
  44.1 10.3 %collective-permute-start.9 = (bf16[40,2048]{1,0:T(8,128)(2,1)}, bf16[40,2048]{1,0:T(8,128)(2,1)}, u32[]{:S(2)}, u32[]{:S(2)}) collective-permute-start(bf16[40,2048]{1,0:T(8,128)(2,1)} %get-tuple-element.60), channel_id=1, source_target_pairs={{0,7},{1,6},{2,5},{3,4},{4,3},{5,2},{6,1},{7,0},{8,15},{9,14},{10,... | collective-permute-start | bytes 491528 | tf_op jit(solution)/shard_map/ppermute | solution.py:250
  46.1 8.4 %collective-permute-start.10 = (bf16[40,2048]{1,0:T(8,128)(2,1)}, bf16[40,2048]{1,0:T(8,128)(2,1)}, u32[]{:S(2)}, u32[]{:S(2)}) collective-permute-start(bf16[40,2048]{1,0:T(8,128)(2,1)} %get-tuple-element.61), channel_id=1, source_target_pairs={{0,1},{1,0},{2,3},{3,2},{4,5},{5,4},{6,7},{7,6},{8,9},{9,8},{10,11... | collective-permute-start | bytes 491528 | tf_op jit(solution)/shard_map/ppermute | solution.py:250
  46.2 8.3 %copy-start.3 = (bf16[40,2048]{1,0:T(8,128)(2,1)S(1)}, bf16[40,2048]{1,0:T(8,128)(2,1)}, u32[]{:S(2)}) copy-start(bf16[40,2048]{1,0:T(8,128)(2,1)} %get-tuple-element.54.refs_0_.refs_4_) | copy-start | bytes 491524
  52.0 7.4 %copy-start.6 = (bf16[40,2048]{1,0:T(8,128)(2,1)}, bf16[40,2048]{1,0:T(8,128)(2,1)S(1)}, u32[]{:S(2)}) copy-start(bf16[40,2048]{1,0:T(8,128)(2,1)S(1)} %collective-permute-done.6.refs_3_.refs_7_) | copy-start | bytes 491524
  52.0 7.4 %copy-start.7 = (bf16[40,2048]{1,0:T(8,128)(2,1)}, bf16[40,2048]{1,0:T(8,128)(2,1)S(1)}, u32[]{:S(2)}) copy-start(bf16[40,2048]{1,0:T(8,128)(2,1)S(1)} %collective-permute-done.7.refs_4_.refs_8_) | copy-start | bytes 491524
  52.0 7.4 %copy-start.8 = (bf16[40,2048]{1,0:T(8,128)(2,1)}, bf16[40,2048]{1,0:T(8,128)(2,1)S(1)}, u32[]{:S(2)}) copy-start(bf16[40,2048]{1,0:T(8,128)(2,1)S(1)} %collective-permute-done.8.refs_5_.refs_9_) | copy-start | bytes 491524
  59.4 20.8 %all-to-all-start.1 = ((bf16[8,40,2048]{2,1,0:T(8,128)(2,1)}), bf16[8,40,2048]{2,1,0:T(8,128)(2,1)S(1)}, u32[]{:S(2)}, u32[]{:S(2)}) async-start(bf16[8,40,2048]{2,1,0:T(8,128)(2,1)} %get-tuple-element.62), calls=%async_computation.1 | async-start | bytes 2621440 | tf_op jit(solution)/shard_map/all_to_all | solution.py:255
  80.2 27.8 %collective-permute-start.13 = (bf16[3,512,384]{2,1,0:T(8,128)(2,1)}, bf16[3,512,384]{2,1,0:T(8,128)(2,1)}, u32[]{:S(2)}, u32[]{:S(2)}) collective-permute-start(bf16[3,512,384]{2,1,0:T(8,128)(2,1)} %get-tuple-element.82), channel_id=1, source_target_pairs={{0,16},{16,0},{1,17},{17,1},{2,18},{18,2},{3,19},{19,3},{4,20},{20... | collective-permute-start | bytes 3538952 | tf_op jit(solution)/shard_map/ppermute | solution.py:355
  81.6 31.9 %all-to-all-start.2 = ((bf16[8,40,2048]{2,1,0:T(8,128)(2,1)}), bf16[8,40,2048]{2,1,0:T(8,128)(2,1)S(1)}, u32[]{:S(2)}, u32[]{:S(2)}) async-start(bf16[8,40,2048]{2,1,0:T(8,128)(2,1)} %bitcast.26), calls=%async_computation.2 | async-start | bytes 2621440 | tf_op jit(solution)/shard_map/all_to_all | solution.py:255
  87.2 28.3 %collective-permute-start.12 = (f32[8,128]{1,0:T(8,128)S(1)}, f32[8,128]{1,0:T(8,128)S(1)}, u32[]{:S(2)}, u32[]{:S(2)}) collective-permute-start(f32[8,128]{1,0:T(8,128)S(1)} %get-tuple-element.77), channel_id=1, source_target_pairs={{0,8},{1,9},{2,10},{3,11},{4,12},{5,13},{6,14},{7,15},{8,0},{9,1},... | collective-permute-start | bytes 12296 | tf_op jit(solution)/shard_map/ppermute | solution.py:245
  89.5 26.2 %collective-permute-start.11 = (bf16[128,2048]{1,0:T(8,128)(2,1)S(1)}, bf16[128,2048]{1,0:T(8,128)(2,1)S(1)}, u32[]{:S(2)}, u32[]{:S(2)}) collective-permute-start(bf16[128,2048]{1,0:T(8,128)(2,1)S(1)} %get-tuple-element.75), channel_id=1, source_target_pairs={{0,8},{1,9},{2,10},{3,11},{4,12},{5,13},{6,14},{7,15},{8,0},{9,1},... | collective-permute-start | bytes 1572872 | tf_op jit(solution)/shard_map/ppermute | solution.py:245
  (6 other events, 22.7 us)
